TPU v7x, 128 devices: a whole 4x4x4 slice. The times are simulated.
128 devices in a mesh: lat: 8 (over x, core), lev: 16 (over y, z).
Axes of the slice: x: 4, y: 4, z: 4, core: 2. Of those that a mesh axis runs over, the one named last changes fastest.
Arguments:
- spectral: float32 [2, 128, 256, 256], P(None, 'lev', 'lat'), may hold values from -6 to 6
- background: bfloat16 [384, 768, 128], P('lat', 'lev'), may hold values from -6 to 6
- columns: int32 [128, 2048], P(('lat', 'lev')), may hold values from 0 to 2303
- counts: int32 [128], P(('lat', 'lev')), may hold values from 1 to 2048, 131072 in all
- radiances: bfloat16 [128, 2048, 512], P(('lat', 'lev')), may hold values from -6 to 6
- used_pairs: int32 [128, 2048], P(('lat', 'lev')), may hold values from 1 to 256
- channel_weight: float32 [512], replicated, may hold values from 0.25 to 4
- weight_in: bfloat16 [128, 1024], replicated, may hold values from -0.5 to 0.5
- weight_mid: bfloat16 [1024, 1024], replicated, may hold values from -0.1875 to 0.1875
- weight_out: bfloat16 [1024, 512], replicated, may hold values from -0.1875 to 0.1875
Outputs:
- spectral_grad: float32 [2, 128, 256, 256], P(None, 'lev', 'lat')
- grid_grad: float32 [384, 768, 128], P('lat', 'lev')
Inputs may be any that keep to these rules, and one draw needn't show every extreme that they name: Entry [o, s] is the column of owner o's slot s inside o's region of 48 x 48 columns, numbered latitude-major; slots at or past counts[o] are unused. The counts sum to 131072, and the largest is exactly 2048. Block [o, s] uses channels 0 to 2 x used_pairs[o, s] - 1.
All inputs are finite; a program needn't handle non-finite values. No bound on the sum of `counts` on one device may be relied on, other than what follows from the above.
Results may differ from a plain program's by a relative error of at most 0.008.
Values may be sent and summed in bfloat16 or wider, within the bound.
No kernel may reach another device: no remote copies, remote signals or barrier semaphores. Data moves between devices by JAX's collectives and lax.ppermute only.
A program may use at most 128 MiB of HBM per device.

v0:
```python
import math

import jax
import jax.numpy as jnp
from jax import lax
from jax.sharding import PartitionSpec as P

M = 256
N = 256
NLAT = 384
NLON = 768
BLK_DEV = 1024


RESCALE_TOP = 2.0**60
RESCALE_BY = 2.0 ** (-60)
RESCALE_LOG = 60.0 * math.log(2.0)
HALF_LOG = 0.5 * math.log(0.5)


def shortened(shard):
    return jax.tree.map(lambda a: a.astype(jnp.bfloat16) if a.dtype == jnp.float32 else a, shard)


def legendre_table(orders, lat_total, degree_total):
    m_float = orders.astype(jnp.float32)
    lat_ids = jnp.arange(lat_total, dtype=jnp.float32)
    latitude = (0.5 - (lat_ids + 0.5) / lat_total) * jnp.pi
    sin_lat = jnp.sin(latitude)
    cos_lat = jnp.cos(latitude)
    order_ids = jnp.arange(1, degree_total, dtype=jnp.float32)
    log_steps = 0.5 * jnp.log((2.0 * order_ids + 1.0) / (2.0 * order_ids))
    log_norm = jnp.sum(
        jnp.where(order_ids[None, :] <= m_float[:, None], log_steps[None, :], 0.0), axis=1
    )
    log_start = HALF_LOG + log_norm[:, None] + m_float[:, None] * jnp.log(cos_lat)[None, :]

    def advance(recur_state, degree):
        previous, earlier, shifts = recur_state
        n_float = degree.astype(jnp.float32)
        on_diagonal = (n_float == m_float)[:, None]
        next_diag = (n_float == m_float + 1.0)[:, None]
        beyond = (n_float > m_float + 1.0)[:, None]
        factor_a = jnp.sqrt(
            jnp.maximum(4.0 * n_float * n_float - 1.0, 1.0)
            / jnp.maximum(n_float * n_float - m_float * m_float, 1.0)
        )
        lower = n_float - 1.0
        factor_b = jnp.sqrt(
            jnp.maximum(lower * lower - m_float * m_float, 0.0)
            / jnp.maximum(4.0 * lower * lower - 1.0, 1.0)
        )
        current = jnp.where(
            beyond,
            factor_a[:, None] * (sin_lat[None, :] * previous - factor_b[:, None] * earlier),
            0.0,
        )
        current = jnp.where(
            next_diag, jnp.sqrt(2.0 * m_float + 3.0)[:, None] * sin_lat[None, :] * previous, current
        )
        current = jnp.where(on_diagonal, 1.0, current)
        oversized = jnp.abs(current) > RESCALE_TOP
        current = jnp.where(oversized, current * RESCALE_BY, current)
        previous = jnp.where(oversized, previous * RESCALE_BY, previous)
        shifts = shifts + oversized.astype(jnp.float32)
        values = current * jnp.exp(log_start + shifts * RESCALE_LOG)
        return ((current, previous, shifts), values)

    zeros = jnp.zeros((orders.shape[0], lat_total), jnp.float32)
    _, legendre = lax.scan(
        advance, (zeros, zeros, zeros), jnp.arange(degree_total, dtype=jnp.int32), unroll=8
    )
    return legendre


def wave_table(wave_total, lon_total):
    wave_ids = jnp.arange(wave_total, dtype=jnp.int32)
    lon_ids = jnp.arange(lon_total, dtype=jnp.int32)
    phase = (wave_ids[:, None] * lon_ids[None, :] % lon_total).astype(jnp.float32) * (
        2.0 * math.pi / lon_total
    )
    weights = jnp.where(wave_ids == 0, 1.0, 2.0).astype(jnp.float32) / wave_total
    return jnp.stack([weights[:, None] * jnp.cos(phase), -weights[:, None] * jnp.sin(phase)])


def silu_slope(inputs):
    sigmoid_v = jax.nn.sigmoid(inputs)
    return sigmoid_v * (1.0 + inputs * (1.0 - sigmoid_v))


def radiance_pass(
    profiles, observed, pair_counts, usable, channel_weight, weight_in, weight_mid, weight_out
):
    pre_first = jnp.dot(profiles, weight_in, preferred_element_type=jnp.float32)
    act_first = jax.nn.silu(pre_first).astype(jnp.bfloat16)
    pre_second = jnp.dot(act_first, weight_mid, preferred_element_type=jnp.float32)
    act_second = jax.nn.silu(pre_second).astype(jnp.bfloat16)
    evolved = jnp.dot(act_second, weight_out, preferred_element_type=jnp.float32)
    channel_ids = jnp.arange(weight_out.shape[1], dtype=jnp.float32)
    active = (channel_ids[None, :] < 2.0 * pair_counts[:, None]) & usable[:, None]
    misfit = jnp.where(
        active, channel_weight[None, :] * (evolved - observed.astype(jnp.float32)), 0.0
    ).astype(jnp.bfloat16)
    back_second = (
        jnp.dot(misfit, weight_out.T, preferred_element_type=jnp.float32) * silu_slope(pre_second)
    ).astype(jnp.bfloat16)
    back_first = (
        jnp.dot(back_second, weight_mid.T, preferred_element_type=jnp.float32)
        * silu_slope(pre_first)
    ).astype(jnp.bfloat16)
    return jnp.dot(back_first, weight_in.T, preferred_element_type=jnp.float32).astype(jnp.bfloat16)


def route_out(profile_slots, observed_slots, pair_slots):
    arrived = (
        lax.all_to_all(profile_slots, ("lat", "lev"), split_axis=1, concat_axis=1, tiled=True),
        lax.all_to_all(observed_slots, ("lat", "lev"), split_axis=1, concat_axis=1, tiled=True),
        lax.all_to_all(pair_slots, ("lat", "lev"), split_axis=1, concat_axis=1, tiled=True),
    )
    return arrived


def route_back(reply):
    returned = lax.all_to_all(reply, ("lat", "lev"), split_axis=1, concat_axis=1, tiled=True)
    return returned


def dealt(
    profiles,
    observed,
    pair_counts,
    usable,
    counts,
    own_index,
    lat_count,
    lev_count,
    channel_weight,
    weight_in,
    weight_mid,
    weight_out,
):
    devices = lat_count * lev_count
    all_counts = lax.all_gather(counts, ("lat", "lev"), axis=0, tiled=True)
    start_ranks = jnp.cumsum(all_counts) - all_counts
    owner_ids = jnp.arange(devices, dtype=jnp.int32)
    own_start = jnp.sum(jnp.where(owner_ids == own_index, start_ranks, 0))
    lead_pos = own_start % devices
    capacity = profiles.shape[0]
    slot_count = (capacity + 2 * devices - 2) // devices

    def place(rows):
        keep = usable.reshape((capacity,) + (1,) * (rows.ndim - 1))
        masked = jnp.where(keep, rows, jnp.zeros((), rows.dtype))
        frame = jnp.zeros((slot_count * devices,) + rows.shape[1:], rows.dtype)
        frame = lax.dynamic_update_slice_in_dim(frame, masked, lead_pos, 0)
        return frame.reshape((slot_count, devices) + rows.shape[1:])

    arrived = route_out(place(profiles), place(observed), place(pair_counts.astype(jnp.bfloat16)))
    flat_profiles = arrived[0].reshape(slot_count * devices, -1)
    flat_observed = arrived[1].reshape(slot_count * devices, -1)
    flat_pairs = arrived[2].reshape(slot_count * devices)
    row_ids = jnp.arange(BLK_DEV, dtype=jnp.int32)
    my_ranks = own_index + devices * row_ids
    covers = start_ranks[None, :] <= my_ranks[:, None]
    source = jnp.sum(covers.astype(jnp.int32), axis=1) - 1
    source_start = jnp.max(jnp.where(covers, start_ranks[None, :], 0), axis=1)
    flat_pos = (row_ids - source_start // devices) * devices + source
    worker_grad = radiance_pass(
        jnp.take(flat_profiles, flat_pos, axis=0),
        jnp.take(flat_observed, flat_pos, axis=0),
        jnp.take(flat_pairs, flat_pos, axis=0).astype(jnp.float32),
        jnp.ones((BLK_DEV,), jnp.bool_),
        channel_weight,
        weight_in,
        weight_mid,
        weight_out,
    )
    slot_ids = jnp.arange(slot_count, dtype=jnp.int32)
    position = slot_ids[:, None] * devices + own_index - (start_ranks % devices)[None, :]
    returned = (position >= 0) & (position < all_counts[None, :])
    target = jnp.clip(start_ranks[None, :] // devices + slot_ids[:, None], 0, BLK_DEV - 1)
    reply = jnp.take(worker_grad, target.reshape(-1), axis=0).reshape(
        slot_count, devices, worker_grad.shape[1]
    )
    reply = jnp.where(returned[:, :, None], reply, jnp.zeros((), jnp.bfloat16))
    back_rows = route_back(reply).reshape(slot_count * devices, -1)
    mine = lax.dynamic_slice_in_dim(back_rows, lead_pos, capacity, 0)
    return jnp.where(usable[:, None], mine, jnp.zeros((), jnp.bfloat16))


def per_device(
    spectral,
    background,
    columns,
    counts,
    radiances,
    used_pairs,
    channel_weight,
    weight_in,
    weight_mid,
    weight_out,
):
    highest = lax.Precision.HIGHEST
    lat_count = lax.axis_size("lat")
    lev_count = lax.axis_size("lev")
    lat_index = lax.axis_index("lat")
    lev_index = lax.axis_index("lev")
    own_index = lat_index * lev_count + lev_index
    waves_local = spectral.shape[2]
    orders = lat_index * waves_local + jnp.arange(waves_local, dtype=jnp.int32)
    legendre = legendre_table(orders, NLAT, N)
    fourier = jnp.einsum("nmj,clmn->clmj", legendre, spectral, precision=highest)
    fourier = lax.all_to_all(fourier, "lat", split_axis=3, concat_axis=2, tiled=True)
    dft_table = wave_table(M, NLON)
    increment = jnp.einsum("clmj,cmx->jlx", fourier, dft_table, precision=highest)
    increment = lax.all_to_all(increment, "lev", split_axis=2, concat_axis=1, tiled=True)
    increment = jnp.transpose(increment, (0, 2, 1))
    grid_state = (background.astype(jnp.float32) + increment).astype(jnp.bfloat16)
    band_rows = grid_state.shape[0]
    tile_cols = grid_state.shape[1]
    cell_rows = grid_state.reshape(band_rows * tile_cols, grid_state.shape[2])
    local_cols = columns[0]
    profiles = jnp.take(cell_rows, local_cols, axis=0)
    capacity = local_cols.shape[0]
    usable = jnp.arange(capacity, dtype=jnp.int32) < counts[0]
    observed = radiances[0]
    pair_counts = used_pairs[0].astype(jnp.float32)
    block_grad = dealt(
        profiles,
        observed,
        pair_counts,
        usable,
        counts,
        own_index,
        lat_count,
        lev_count,
        channel_weight,
        weight_in,
        weight_mid,
        weight_out,
    )
    grid_grad = (
        jnp.zeros(cell_rows.shape, jnp.float32).at[local_cols].add(block_grad.astype(jnp.float32))
    )
    grid_grad = grid_grad.reshape(band_rows, tile_cols, cell_rows.shape[1])
    grad_rows = lax.all_to_all(
        jnp.transpose(grid_grad, (0, 2, 1)).astype(jnp.bfloat16),
        "lev",
        split_axis=1,
        concat_axis=2,
        tiled=True,
    ).astype(jnp.float32)
    coeff_grad = jnp.einsum("jlx,cmx->clmj", grad_rows, dft_table, precision=highest)
    coeff_grad = lax.all_to_all(
        shortened(coeff_grad), "lat", split_axis=2, concat_axis=3, tiled=True
    ).astype(coeff_grad.dtype)
    spectral_grad = jnp.einsum("nmj,clmj->clmn", legendre, coeff_grad, precision=highest)
    return (spectral_grad, grid_grad)


def solution(mesh):
    in_specs = (
        P(None, "lev", "lat", None),
        P("lat", "lev", None),
        P(("lat", "lev"), None),
        P(("lat", "lev")),
        P(("lat", "lev"), None, None),
        P(("lat", "lev"), None),
        P(),
        P(),
        P(),
        P(),
    )
    out_specs = (P(None, "lev", "lat", None), P("lat", "lev", None))
    return jax.shard_map(
        per_device, mesh=mesh, in_specs=in_specs, out_specs=out_specs, check_vma=False
    )
```

profile of v0, /device:TPU:1, one launch (start us, length us, event | category | flops | bytes accessed | tf_op | source)
XLA Modules:
  0.0 645.3 jit_solution(7367198378319178831)
XLA Ops:
  1.0 258.0 %while.23 = (s32[]{:T(128)}, f32[32,384]{1,0:T(8,128)S(1)}, f32[32,384]{1,0:T(8,128)S(1)}, f32[32,384]{1,0:T(8,128)S(1)}, f32[32,8,32,384]{3,2,1,0:T(8,128)}, /*...) while((s32[]{:T(128)}, f32[32,384]{1,0:T(8,128)S(1)}, ...), condition=%wide.region_6.7_spmd.clone.clone.clone.clone, body=%wide.region_5.6_spmd.clone.clone.clone.clone.sunk | while | flops 3778274 | bytes 3127550 | solution.py:70
  259.0 14.5 %fusion.88 = f32[2,8,32,384]{3,1,0,2:T(8,128)S(1)} fusion(f32[256,32,384]{2,1,0:T(8,128)} %bitcast.226, f32[2,8,32,256]{3,2,1,0:T(8,128)S(1)} %copy-done.6), kind=kOutput, calls=%fused_computation.199 | convolution fusion | flops 603979776 | bytes 13893632
  275.8 3.6 reshape.978
  279.3 5.8 all-to-all-start.1
  285.9 69.5 %all-reduce = s32[128]{0:T(128)S(1)} all-reduce(s32[128]{0:T(128)S(1)} %dynamic-update-slice), channel_id=1, replica_groups=mesh['lat'=8,'lev'=16] {'lat','lev'}, use_global_device_ids=true, to_apply=%add | all-reduce | flops 128 | bytes 1024
  359.9 4.1 sine_multiply_fusion
  364.0 5.0 all-to-all-start
  369.5 3.6 reduce.5
  373.2 3.8 reshape.979
  377.0 5.4 copy.208
  382.3 3.1 all_to_all.72
  385.5 3.7 convolution_bitcast_fusion
  389.2 2.3 copy.165
  391.5 5.1 reshape.980
  396.6 7.6 %all-to-all-start.2 = ((f32[16,1,18432]{2,1,0:T(1,128)}), f32[16,1,18432]{2,1,0:T(1,128)S(1)}, u32[]{:S(2)}, u32[]{:S(2)}) async-start(f32[16,1,18432]{2,1,0:T(1,128)} %reshape.980), calls=%async_computation.2 | async-start | bytes 2359296 | tf_op jit(solution)/shard_map/all_to_all | solution.py:216
  404.2 2.8 bitcast_select_fusion
  408.5 11.1 %dynamic_update_slice.19 = bf16[2176,512]{1,0:T(8,128)(2,1)} dynamic-update-slice(bf16[2176,512]{1,0:T(8,128)(2,1)} %broadcast_in_dim.596, bf16[2048,512]{1,0:T(8,128)(2,1)} %bitcast_select_fusion, s32[]{:T(128)S(6)} %select_n.488, s32[]{:T(128)} %constant.254.clone.1) | dynamic-update-slice | bytes 4194308 | tf_op jit(solution)/shard_map/dynamic_update_slice | solution.py:155
  419.5 4.6 copy.170
  424.7 10.3 %all-to-all-start.4 = ((bf16[17,128,512]{2,0,1:T(8,128)(2,1)}), bf16[17,128,512]{2,0,1:T(8,128)(2,1)}, u32[]{:S(2)}, u32[]{:S(2)}) async-start(bf16[17,128,512]{2,0,1:T(8,128)(2,1)} %copy.170), calls=%async_computation.4 | async-start | bytes 6291456 | tf_op jit(solution)/shard_map/all_to_all | solution.py:117
  435.7 4.8 reduce.6
  440.5 3.6 reshape.981
  444.1 5.1 copy.166
  449.2 3.2 copy.167
  453.8 6.2 gather_fusion.1
  460.0 2.3 select_select_fusion
  462.4 3.1 dynamic_update_slice.18
  466.7 8.7 %all-to-all-done.4 = bf16[17,128,512]{2,0,1:T(8,128)(2,1)} async-done(((bf16[17,128,512]{2,0,1:T(8,128)(2,1)}), bf16[17,128,512]{2,0,1:T(8,128)(2,1)}, u32[]{:S(2)}, u32[]{:S(2)}) %all-to-all-start.4) | async-done | bytes 2228256 | tf_op jit(solution)/shard_map/all_to_all | solution.py:117
  475.4 5.3 all-to-all-start.3
  482.1 6.8 %gather_fusion = bf16[1024]{0:T(1024)(128)(2,1)S(1)} fusion(bf16[2176]{0:T(1024)(128)(2,1)S(1)} %bitcast.224, s32[1024]{0:T(1024)S(1)} %broadcast_clamp_fusion.1), kind=kCustom, calls=%fused_computation | custom fusion | bytes 8192 | tf_op jit(solution)/shard_map/jit(_take)/gather | solution.py:171
  489.6 4.0 copy.171
  493.6 7.0 %gather_fusion.3 = bf16[1024,512]{1,0:T(8,128)(2,1)} fusion(bf16[2176,512]{1,0:T(8,128)(2,1)} %bitcast.225, s32[1024]{0:T(1024)S(1)} %broadcast_clamp_fusion.1), kind=kCustom, calls=%fused_computation.3 | custom fusion | bytes 2101248 | tf_op jit(solution)/shard_map/jit(_take)/gather | solution.py:170
  500.8 3.2 gather_fusion.2
  505.7 4.3 fusion.85
  510.1 8.9 %multiply_convert_fusion.1 = bf16[1024,1024]{1,0:T(8,128)(2,1)} fusion(f32[1024,1024]{1,0:T(8,128)} %fusion.85, bf16[1024,512]{1,0:T(8,128)(2,1)} %param.21, bf16[1024,512]{1,0:T(8,128)(2,1)S(1)} %copy-done.3, f32[512]{0:T(512)S(1)} %copy-done.16, f32[1024]{0:T(1024)S(1)} %get-tuple-element.400, pred[1024]{0:T(1024)(128)(4,1)S(1)} %get-tuple-element.401), kind=kOutput, calls=%fused_computation.185 | convolution fusion | flops 2165833728 | bytes 8395776 | tf_op jit(solution)/shard_map/dot_general | solution.py:105
  518.9 6.0 fusion.97
  524.9 4.8 gather_fusion.4
  531.6 26.2 %all_to_all.96 = bf16[17,128,128]{2,0,1:T(8,128)(2,1)S(1)} all-to-all(bf16[17,128,128]{2,0,1:T(8,128)(2,1)S(1)} %fusion.108), channel_id=1, replica_groups=mesh['lat'=8,'lev'=16] {'lat','lev'}, dimensions={1} | all-to-all | bytes 1114112 | tf_op jit(solution)/shard_map/all_to_all | solution.py:124
  558.8 12.2 %scatter_custom_fusion = f32[2304,128]{1,0:T(8,128)S(1)} fusion(s32[2048]{0:T(1024)} %bitcast.249, f32[]{:T(128)} %constant.260.clone.1, bf16[2176,128]{1,0:T(8,128)(2,1)} %bitcast.245, s32[]{:T(128)S(6)} %select_n.488, s32[]{:T(128)} %constant.254.clone.1, pred[2048]{0:T(1024)(128)(4,1)S(1)} %copy-done.12, bf16[]{:T(256)} %constant.276.clone.1), kind=kCustom, calls=%fused_computation.208 | custom fusion | flops 786432 | bytes 1707524 | tf_op jit(solution)/shard_map/scatter-add | solution.py:243
  572.0 2.7 copy.174
  574.7 4.2 reshape.982
  578.8 15.5 %all_to_all.97 = bf16[16,2,9216]{2,1,0:T(2,128)(2,1)} all-to-all(bf16[16,2,9216]{2,1,0:T(2,128)(2,1)} %reshape.982), channel_id=1, replica_groups=mesh['lat'=8,'lev'=16] {'lev'}, dimensions={0} | all-to-all | bytes 1179648 | tf_op jit(solution)/shard_map/all_to_all | solution.py:246
  594.3 3.3 reshape.983
  597.6 3.7 copy.176
  601.3 2.7 reshape.967
  604.1 3.0 fusion.96
  610.6 13.3 %all_to_all.98 = bf16[8,2,12288]{2,1,0:T(2,128)(2,1)} all-to-all(bf16[8,2,12288]{2,1,0:T(2,128)(2,1)S(1)} %reshape.984), channel_id=1, replica_groups=mesh['lat'=8,'lev'=16] {'lat'}, dimensions={0} | all-to-all | bytes 786432 | tf_op jit(solution)/shard_map/all_to_all | solution.py:254
  626.2 2.3 copy.179
  630.5 13.3 %fusion.93 = f32[2,8,32,256]{3,1,0,2:T(8,128)S(1)} fusion(bf16[2,8,32,384]{3,1,0,2:T(8,128)(2,1)S(1)} %all_to_all.87, f32[256,32,384,1]{2,1,0,3:T(8,128)} %bitcast.227), kind=kOutput, calls=%fused_computation.202 | convolution fusion | flops 603979776 | bytes 13500416 | tf_op jit(solution)/shard_map/nmj,clmj->clmn/dot_general | solution.py:257
  (1185 shorter events, 122.2 us)
Async XLA Ops:
  0.6 505.1 %copy-start = (bf16[1024,1024]{1,0:T(8,128)(2,1)S(1)}, bf16[1024,1024]{1,0:T(8,128)(2,1)}, u32[]{:S(2)}) copy-start(bf16[1024,1024]{1,0:T(8,128)(2,1)} %param.20) | copy-start | bytes 6291460
  1.0 258.1 %copy-start.6 = (f32[2,8,32,256]{3,2,1,0:T(8,128)S(1)}, f32[2,8,32,256]{3,2,1,0:T(8,128)}, u32[]{:S(2)}) copy-start(f32[2,8,32,256]{3,2,1,0:T(8,128)} %param.12) | copy-start | bytes 1572868
  275.8 82.7 %copy-start.15 = (s32[1,2048]{1,0:T(1,128)S(1)}, s32[1,2048]{1,0:T(1,128)}, u32[]{:S(2)}) copy-start(s32[1,2048]{1,0:T(1,128)} %param.17) | copy-start | bytes 24580
  279.3 84.7 %all-to-all-start.1 = ((f32[8,1,24576]{2,1,0:T(1,128)}), f32[8,1,24576]{2,1,0:T(1,128)S(1)}, u32[]{:S(2)}, u32[]{:S(2)}) async-start(f32[8,1,24576]{2,1,0:T(1,128)} %reshape.978), calls=%async_computation.1 | async-start | bytes 1572864 | tf_op jit(solution)/shard_map/all_to_all | solution.py:213
  364.0 32.6 %all-to-all-start = ((bf16[17,128,1]{0,2,1:T(2,128)(2,1)}), bf16[17,128,1]{0,2,1:T(2,128)(2,1)S(1)}, u32[]{:S(2)}, u32[]{:S(2)}) async-start(bf16[17,128,1]{0,2,1:T(2,128)(2,1)} %copy.158), calls=%async_computation | async-start | bytes 131072 | tf_op jit(solution)/shard_map/all_to_all | solution.py:118
  396.6 28.1 %all-to-all-start.2 = ((f32[16,1,18432]{2,1,0:T(1,128)}), f32[16,1,18432]{2,1,0:T(1,128)S(1)}, u32[]{:S(2)}, u32[]{:S(2)}) async-start(f32[16,1,18432]{2,1,0:T(1,128)} %reshape.980), calls=%async_computation.2 | async-start | bytes 2359296 | tf_op jit(solution)/shard_map/all_to_all | solution.py:216
  404.2 55.8 %copy-start.11 = (pred[2048]{0:T(1024)(128)(4,1)}, pred[2048]{0:T(1024)(128)(4,1)S(1)}, u32[]{:S(2)}) copy-start(pred[2048]{0:T(1024)(128)(4,1)S(1)} %iota_compare_fusion.1) | copy-start | bytes 6148
  424.6 10.4 %copy-start.10 = (s32[1024]{0:T(1024)}, s32[1024]{0:T(1024)S(1)}, u32[]{:S(2)}) copy-start(s32[1024]{0:T(1024)S(1)} %get-tuple-element.361) | copy-start | bytes 12292
  424.6 10.4 %copy-start.9 = (s32[1024]{0:T(1024)}, s32[1024]{0:T(1024)S(1)}, u32[]{:S(2)}) copy-start(s32[1024]{0:T(1024)S(1)} %get-tuple-element.360) | copy-start | bytes 12292
  424.7 10.4 %copy-start.13 = (s32[1,2048]{1,0:T(1,128)S(1)}, s32[1,2048]{1,0:T(1,128)}, u32[]{:S(2)}) copy-start(s32[1,2048]{1,0:T(1,128)} %param.14) | copy-start | bytes 24580
  424.7 50.7 %all-to-all-start.4 = ((bf16[17,128,512]{2,0,1:T(8,128)(2,1)}), bf16[17,128,512]{2,0,1:T(8,128)(2,1)}, u32[]{:S(2)}, u32[]{:S(2)}) async-start(bf16[17,128,512]{2,0,1:T(8,128)(2,1)} %copy.170), calls=%async_computation.4 | async-start | bytes 6291456 | tf_op jit(solution)/shard_map/all_to_all | solution.py:117
  435.7 8.4 %copy-start.14 = (s32[2048,1]{0,1:T(1,128)}, s32[2048,1]{0,1:T(1,128)S(1)}, u32[]{:S(2)}) copy-start(s32[2048,1]{0,1:T(1,128)S(1)} %compare_select_fusion.2) | copy-start | bytes 24580
  449.2 3.2 copy-start.5
  475.4 25.3 %all-to-all-start.3 = ((bf16[17,128,128]{2,0,1:T(8,128)(2,1)}), bf16[17,128,128]{2,0,1:T(8,128)(2,1)S(1)}, u32[]{:S(2)}, u32[]{:S(2)}) async-start(bf16[17,128,128]{2,0,1:T(8,128)(2,1)} %copy.168), calls=%async_computation.3 | async-start | bytes 1572864 | tf_op jit(solution)/shard_map/all_to_all | solution.py:116
  505.7 4.4 copy-start.2
  505.7 4.4 copy-start.3
  505.7 4.3 copy-start.16
  510.1 8.9 %copy-start.7 = (bf16[128,1024]{1,0:T(8,128)(2,1)S(1)}, bf16[128,1024]{1,0:T(8,128)(2,1)}, u32[]{:S(2)}) copy-start(bf16[128,1024]{1,0:T(8,128)(2,1)} %param.19) | copy-start | bytes 786436
  518.9 6.0 copy-start.8
  529.7 29.0 %copy-start.12 = (pred[2048]{0:T(1024)(128)(4,1)S(1)}, pred[2048]{0:T(1024)(128)(4,1)}, u32[]{:S(2)}) copy-start(pred[2048]{0:T(1024)(128)(4,1)} %copy-done.11) | copy-start | bytes 6148
  571.0 23.3 %copy-start.1 = (f32[2304,128]{1,0:T(8,128)}, f32[2304,128]{1,0:T(8,128)S(1)}, u32[]{:S(2)}) copy-start(f32[2304,128]{1,0:T(8,128)S(1)} %scatter_custom_fusion) | copy-start | bytes 3538948
  597.6 6.4 copy-start.4
where the time goes:
time: 658 us; the launch traced here: 645 us
  local copies, waits for them, and re-layouts  169 us (26%)
  loops' own time  163 us (25%)
  blocking collectives  125 us (19%)
  other arithmetic  85.6 us (13%)
  matrix products  55.4 us (8%)
  starting transfers between devices  33.9 us (5%)
  waiting for transfers between devices  8.66 us (1%)
    another operation x1, loops' own time, legendre_table(): lax.scan(advance, (zeros, zeros, zeros), jnp.arange(degree_total, dtype=j...  163 us
    unnamed x1, blocking collectives  69.5 us
    while x224, other arithmetic  31.7 us
    unnamed x45, local copies, waits for them, and re-layouts  28.7 us
    all_to_all x1, blocking collectives, route_back(): lax.all_to_all(reply, ('lat', 'lev'), split_axis=1, concat_axis=1, tiled=...  26.2 us
    dynamic_update_slice x32, local copies, waits for them, and re-layouts, legendre_table(): lax.scan(advance, (zeros, zeros, zeros), jnp.arange(degree_total, dtype=j...  25.3 us
    slice x32, local copies, waits for them, and re-layouts, legendre_table(): lax.scan(advance, (zeros, zeros, zeros), jnp.arange(degree_total, dtype=j...  19.7 us
    all_to_all x1, blocking collectives, per_device(): lax.all_to_all(jnp.transpose(grid_grad, (0, 2, 1)).astype(jnp.bfloat16),...  15.5 us
  transfers between devices with their start and end apart: 5, of which 1 were waited for; matrix products, arithmetic and copies ran while one was open for 16% of the time, Pallas kernels for 0%

commit v1 on v0

v1 whole, which is shorter than its diff:
```python
import math

import jax
import jax.numpy as jnp
import numpy as np
from jax import lax
from jax.experimental import pallas as pl
from jax.experimental.pallas import tpu as pltpu
from jax.sharding import PartitionSpec as P

LEV = 128
M = 256
N = 256
NLAT = 384
NLON = 768
HALF = NLAT // 2
LANES = 128
N_LAT = 8
N_LEV = 16
ML = M // N_LAT
LL = LEV // N_LEV
CLAT = NLAT // N_LAT
CLON = NLON // N_LEV
CELLS = CLAT * CLON
CAP = 2048
CHAN = 512
JL = CLAT * LL
KM = 2 * M
ROWS = 2 * LL * ML

RESCALE_TOP = 2.0**30
RESCALE_BY = 2.0 ** (-60)
RESCALE_LOG = 60.0 * math.log(2.0)
HALF_LOG = 0.5 * math.log(0.5)

bf16 = jnp.bfloat16
f32 = jnp.float32


def params(**kwargs):
    return pltpu.CompilerParams(vmem_limit_bytes=56 << 20, **kwargs)


def dot_nt(a, b):
    return lax.dot_general(a, b, (((1,), (1,)), ((), ())), preferred_element_type=f32)


def dot_tn(a, b):
    return lax.dot_general(a, b, (((0,), (0,)), ((), ())), preferred_element_type=f32)


def dot_nn(a, b):
    return jnp.dot(a, b, preferred_element_type=f32)


def geometry():
    lat = (0.5 - (np.arange(256, dtype=np.float64) + 0.5) / NLAT) * np.pi
    valid = np.arange(256) < HALF
    sin_lat = np.where(valid, np.sin(lat), 0.0)
    log_cos = np.where(valid, np.log(np.cos(np.where(valid, lat, 0.0))), 0.0)
    rows = np.zeros((8, 256), np.float32)
    rows[0], rows[1], rows[2] = sin_lat, log_cos, valid
    k = np.arange(1, M, dtype=np.float64)
    steps = 0.5 * np.log((2.0 * k + 1.0) / (2.0 * k))
    log_norm = np.concatenate([[0.0], np.cumsum(steps)]) + HALF_LOG
    return rows, np.repeat(log_norm[:, None], LANES, axis=1).astype(np.float32)


def wave_table():
    m = np.arange(M)
    phase = (np.arange(NLON)[:, None] * m[None, :] % NLON) * (2.0 * np.pi / NLON)
    weight = np.where(m == 0, 1.0, 2.0) / M
    pair = np.stack([weight * np.cos(phase), -weight * np.sin(phase)])
    table = pair.reshape(2, NLON, N_LAT, ML).transpose(1, 2, 0, 3).reshape(NLON, KM)
    return jnp.asarray(table, f32).astype(bf16)


M_STEP = 4


def legendre_kernel(lat_ref, geo_ref, norm_ref, spec_ref, p_ref, four_ref, table, waves):
    step = pl.program_id(0)
    groups = range(ML // 8)

    @pl.when(step == 0)
    def _():
        m0 = lat_ref[0] * ML
        sub = lax.broadcasted_iota(jnp.int32, (8, LANES), 0)
        mf = [(sub + (m0 + 8 * g)).astype(f32) for g in groups]
        m2 = [v * v for v in mf]
        zero = jnp.zeros((8, LANES), f32)
        x = [jnp.broadcast_to(geo_ref[0:1, h * LANES : (h + 1) * LANES], (8, LANES)) for h in (0, 1)]
        log_cos = [
            jnp.broadcast_to(geo_ref[1:2, h * LANES : (h + 1) * LANES], (8, LANES)) for h in (0, 1)
        ]
        valid = [
            jnp.broadcast_to(geo_ref[2:3, h * LANES : (h + 1) * LANES], (8, LANES)) for h in (0, 1)
        ]
        logs = [
            [norm_ref[pl.ds(m0 + 8 * g, 8), :] + mf[g] * log_cos[h] for h in (0, 1)] for g in groups
        ]

        def block(i, carry):
            prev, earlier, logs, eps_prev, nf = carry
            big = [
                [jnp.maximum(jnp.abs(prev[g][h]), jnp.abs(earlier[g][h])) > RESCALE_TOP for h in (0, 1)]
                for g in groups
            ]
            shrink = [[jnp.where(big[g][h], RESCALE_BY, 1.0) for h in (0, 1)] for g in groups]
            prev = [[prev[g][h] * shrink[g][h] for h in (0, 1)] for g in groups]
            earlier = [[earlier[g][h] * shrink[g][h] for h in (0, 1)] for g in groups]
            logs = [
                [jnp.where(big[g][h], logs[g][h] + RESCALE_LOG, logs[g][h]) for h in (0, 1)]
                for g in groups
            ]
            scale = [[jnp.exp(logs[g][h]) * valid[h] for h in (0, 1)] for g in groups]
            for k in range(8):
                n2 = nf * nf
                inv = 1.0 / jnp.maximum(4.0 * n2 - 1.0, 1.0)
                at = pl.multiple_of((i * 8 + k) * ML, ML)
                new = []
                eps = []
                for g in groups:
                    t = n2 - m2[g]
                    q = jnp.maximum(t, 1.0) * inv
                    a = lax.rsqrt(q)
                    eps.append(jnp.where(t > 0.0, q * a, 0.0))
                    diag = nf == mf[g]
                    row = []
                    for h in (0, 1):
                        cur = (x[h] * prev[g][h] - eps_prev[g] * earlier[g][h]) * a
                        cur = jnp.where(diag, 1.0, cur)
                        table[h, pl.ds(at + 8 * g, 8), :] = cur * scale[g][h]
                        row.append(cur)
                    new.append(row)
                prev, earlier, eps_prev = new, prev, eps
                nf = nf + 1.0
            return prev, earlier, logs, eps_prev, nf

        empty = [[zero, zero] for _ in groups]
        lax.fori_loop(0, N // 8, block, (empty, empty, logs, [zero for _ in groups], zero))

    lane = lax.broadcasted_iota(jnp.int32, (1, N), 1)
    alternate = jnp.where(lane % 2 == 0, 1.0, -1.0)
    for k in range(M_STEP):
        m = step * M_STEP + k
        p_m = jnp.concatenate(
            [table[h, pl.ds(m, N, stride=ML), :].astype(bf16) for h in (0, 1)], axis=1
        )
        p_ref[k] = p_m
        s = jnp.concatenate([spec_ref[h, pl.ds(m, 2 * LL, stride=ML), :] for h in (0, 1)], axis=1)
        signed = s * (alternate if k % 2 == 0 else -alternate)
        out = dot_nn(jnp.concatenate([s, signed], axis=0).astype(bf16), p_m)
        for hemi in (0, 1):
            for c in (0, 1):
                first = (hemi * 2 + c) * LL
                for h in (0, 1):
                    waves[hemi, h, pl.ds(c * ML + m, LL, stride=2 * ML), :] = out[
                        first : first + LL, h * LANES : (h + 1) * LANES
                    ]

    @pl.when(step == pl.num_programs(0) - 1)
    def _():
        row = lax.broadcasted_iota(jnp.int32, (HALF, 256), 0)
        col = lax.broadcasted_iota(jnp.int32, (HALF, 256), 1)
        for hemi in (0, 1):
            pick = jnp.where(col == (row if hemi == 0 else HALF - 1 - row), 1.0, 0.0).astype(bf16)
            values = jnp.concatenate([waves[hemi, h].astype(bf16) for h in (0, 1)], axis=1)
            four_ref[hemi * HALF : (hemi + 1) * HALF, :] = dot_nt(pick, values).astype(bf16)


def legendre_transform(lat_index, spectral):
    geo, norm = geometry()
    spec = spectral.reshape(ROWS, 2, LANES).transpose(1, 0, 2)
    whole = lambda shape: pl.BlockSpec(shape, lambda i, *_: (0,) * len(shape))
    return pl.pallas_call(
        legendre_kernel,
        grid_spec=pltpu.PrefetchScalarGridSpec(
            num_scalar_prefetch=1,
            grid=(ML // M_STEP,),
            in_specs=[whole((8, 256)), whole((M, LANES)), whole((2, ROWS, LANES))],
            out_specs=[
                pl.BlockSpec((M_STEP, N, 256), lambda i, *_: (i, 0, 0)),
                whole((NLAT, ROWS)),
            ],
            scratch_shapes=[
                pltpu.VMEM((2, N * ML, LANES), f32),
                pltpu.VMEM((2, 2, ROWS, LANES), f32),
            ],
        ),
        out_shape=[
            jax.ShapeDtypeStruct((ML, N, 256), bf16),
            jax.ShapeDtypeStruct((NLAT, ROWS), bf16),
        ],
        compiler_params=params(),
        name="legendre",
    )(lat_index, jnp.asarray(geo), jnp.asarray(norm), spec)


def adjoint_kernel(p_ref, rows_ref, out_ref, folded):
    step = pl.program_id(0)

    @pl.when(step == 0)
    def _():
        j = lax.broadcasted_iota(jnp.int32, (NLAT, 256), 0)
        col = lax.broadcasted_iota(jnp.int32, (NLAT, 256), 1)
        north = jnp.where(col == j, 1.0, 0.0)
        south = jnp.where((j >= HALF) & (col == NLAT - 1 - j), 1.0, 0.0)
        north = jnp.where(col < HALF, north, 0.0)
        for part, pick in ((0, north + south), (1, north - south)):
            value = dot_tn(rows_ref[...], pick.astype(bf16))
            for h in (0, 1):
                folded[part, h] = value[:, h * LANES : (h + 1) * LANES]

    lane = lax.broadcasted_iota(jnp.int32, (2 * LL, N), 1)
    for k in range(M_STEP):
        m = step * M_STEP + k
        pieces = []
        for part in (0, 1):
            for c in (0, 1):
                pieces.append(
                    jnp.concatenate(
                        [
                            folded[part, h, pl.ds(c * ML + m, LL, stride=2 * ML), :]
                            for h in (0, 1)
                        ],
                        axis=1,
                    )
                )
        value = dot_nt(jnp.concatenate(pieces, axis=0).astype(bf16), p_ref[k])
        picked = jnp.where(lane % 2 == k % 2, value[: 2 * LL], value[2 * LL :])
        for h in (0, 1):
            out_ref[h, pl.ds(m, 2 * LL, stride=ML), :] = picked[:, h * LANES : (h + 1) * LANES]


def legendre_adjoint(table, rows):
    whole = lambda shape: pl.BlockSpec(shape, lambda i: (0,) * len(shape))
    out = pl.pallas_call(
        adjoint_kernel,
        grid=(ML // M_STEP,),
        in_specs=[pl.BlockSpec((M_STEP, N, 256), lambda i: (i, 0, 0)), whole((NLAT, ROWS))],
        out_specs=whole((2, ROWS, LANES)),
        scratch_shapes=[pltpu.VMEM((2, 2, ROWS, LANES), f32)],
        out_shape=jax.ShapeDtypeStruct((2, ROWS, LANES), f32),
        compiler_params=params(),
        name="legendre_adjoint",
    )(table, rows)
    return out.transpose(1, 0, 2).reshape(2, LL, ML, N)


def waves_kernel(rows_ref, table_ref, out_ref, held):
    for pair in range(N_LAT // 2):
        for l in range(LL):
            pieces = [
                rows_ref[(2 * pair + k) * CLAT : (2 * pair + k + 1) * CLAT, l * 64 : (l + 1) * 64]
                for k in (0, 1)
            ]
            held[pair, pl.ds(l, CLAT, stride=LL), :] = jnp.concatenate(pieces, axis=1).astype(f32)
    waves = jnp.concatenate([held[k].astype(bf16) for k in range(N_LAT // 2)], axis=1)
    out_ref[...] = dot_nt(table_ref[...], waves).astype(bf16)


def waves_to_grid(rows, table):
    return pl.pallas_call(
        waves_kernel,
        out_shape=jax.ShapeDtypeStruct((NLON, JL), bf16),
        scratch_shapes=[pltpu.VMEM((N_LAT // 2, JL, LANES), f32)],
        compiler_params=params(),
        name="waves",
    )(rows, table)


def waves_adjoint_kernel(grid_ref, table_ref, out_ref, held):
    value = dot_tn(grid_ref[...], table_ref[...])
    for k in range(N_LAT // 2):
        held[k] = value[:, k * LANES : (k + 1) * LANES]
    for pair in range(N_LAT // 2):
        for lp in range(LL // 2):
            two = [held[pair, pl.ds(2 * lp + k, CLAT, stride=LL), :] for k in (0, 1)]
            for k in (0, 1):
                piece = jnp.concatenate([v[:, k * 64 : (k + 1) * 64] for v in two], axis=1)
                first = (2 * pair + k) * CLAT
                out_ref[first : first + CLAT, lp * LANES : (lp + 1) * LANES] = piece.astype(bf16)


def grid_to_waves(grid, table):
    return pl.pallas_call(
        waves_adjoint_kernel,
        out_shape=jax.ShapeDtypeStruct((NLAT, ROWS), bf16),
        scratch_shapes=[pltpu.VMEM((N_LAT // 2, JL, LANES), f32)],
        compiler_params=params(),
        name="waves_adjoint",
    )(grid, table)


SUM_TILE = 256


def sums_kernel(count_ref, columns_ref, pairs_ref, obs_ref, sum_ref, seen_ref, masked):
    step = pl.program_id(0)
    count = count_ref[0]

    @pl.when(step == 0)
    def _():
        def fill(i, _):
            r = pl.ds(pl.multiple_of(i * 256, 256), 256)
            channel = lax.broadcasted_iota(jnp.int32, (256, CHAN), 1)
            active = channel < 2 * pairs_ref[r, :]
            masked[r, 0:CHAN] = jnp.where(active, obs_ref[r, :].astype(f32), 0.0).astype(bf16)
            masked[r, CHAN : 2 * CHAN] = jnp.where(active, 1.0, 0.0).astype(bf16)
            return 0

        lax.fori_loop(0, CAP // 256, fill, 0)

    cell = lax.broadcasted_iota(jnp.int32, (SUM_TILE, CAP), 0) + step * SUM_TILE
    slot = lax.broadcasted_iota(jnp.int32, (1, CAP), 1)
    column = jnp.where(slot < count, columns_ref[...], -1)
    hit = jnp.where(cell == column, 1.0, 0.0).astype(bf16)
    sum_ref[...] = dot_nn(hit, masked[:, 0:CHAN])
    seen_ref[...] = dot_nn(hit, masked[:, CHAN : 2 * CHAN])


def column_sums(counts, columns, pairs, obs):
    whole = lambda shape: pl.BlockSpec(shape, lambda i, *_: (0,) * len(shape))
    part = pl.BlockSpec((SUM_TILE, CHAN), lambda i, *_: (i, 0))
    return pl.pallas_call(
        sums_kernel,
        grid_spec=pltpu.PrefetchScalarGridSpec(
            num_scalar_prefetch=1,
            grid=(CELLS // SUM_TILE,),
            in_specs=[whole((1, CAP)), whole((CAP, 1)), whole((CAP, CHAN))],
            out_specs=[part, part],
            scratch_shapes=[pltpu.VMEM((CAP, 2 * CHAN), bf16)],
        ),
        out_shape=[jax.ShapeDtypeStruct((CELLS, CHAN), f32)] * 2,
        compiler_params=params(),
        name="column_sums",
    )(counts, columns, pairs, obs)


J_STEP = 16
TILE = 256
X_ROWS = 16


def silu_and_slope(v):
    half = 0.5 * v
    sig = 0.5 * jnp.tanh(half) + 0.5
    act = v * sig
    return act, sig + act - act * sig


def swap_blocks(v):
    lane = lax.broadcasted_iota(jnp.int32, v[0].shape, 1)
    v = list(v)
    for bit in range(4):
        gap = 1 << bit
        upper = (lane & (8 * gap)) != 0
        for s in range(N_LEV):
            if s & gap:
                continue
            a, b = v[s], v[s + gap]
            v[s] = jnp.where(upper, pltpu.roll(b, 8 * gap, 1), a)
            v[s + gap] = jnp.where(upper, b, pltpu.roll(a, LANES - 8 * gap, 1))
    return v


def network_kernel(
    inc_ref, back_ref, sum_ref, seen_ref, chan_ref, w_in, w_mid, w_out, grad_ref, send_ref, state, grads
):
    for part in range(CLON // X_ROWS):
        x0 = part * X_ROWS
        v = [inc_ref[s * CLON + x0 : s * CLON + x0 + X_ROWS, :].astype(f32) for s in range(N_LEV)]
        v = swap_blocks(v)
        for j in range(J_STEP):
            total = back_ref[j, x0 : x0 + X_ROWS, :].astype(f32) + v[j]
            state[j * CLON + x0 : j * CLON + x0 + X_ROWS, :] = total.astype(bf16)
    for i in range(J_STEP * CLON // TILE):
        r = slice(i * TILE, (i + 1) * TILE)
        act1, slope1 = silu_and_slope(dot_nn(state[r, :], w_in[...]))
        act2, slope2 = silu_and_slope(dot_nn(act1.astype(bf16), w_mid[...]))
        evolved = dot_nn(act2.astype(bf16), w_out[...])
        misfit = (chan_ref[...] * (seen_ref[r, :] * evolved - sum_ref[r, :])).astype(bf16)
        back2 = (dot_nt(misfit, w_out[...]) * slope2).astype(bf16)
        back1 = (dot_nt(back2, w_mid[...]) * slope1).astype(bf16)
        grads[r, :] = dot_nt(back1, w_in[...])
    for j in range(J_STEP):
        grad_ref[j] = grads[j * CLON : (j + 1) * CLON, :]
    for part in range(CLON // X_ROWS):
        x0 = part * X_ROWS
        v = [grads[j * CLON + x0 : j * CLON + x0 + X_ROWS, :] for j in range(J_STEP)]
        v = swap_blocks(v)
        for s in range(N_LEV):
            send_ref[s * CLON + x0 : s * CLON + x0 + X_ROWS, :] = v[s].astype(bf16)


def network(inc, background, sums, seen, channel_weight, w_in, w_mid, w_out):
    whole = lambda shape: pl.BlockSpec(shape, lambda i: (0,) * len(shape))
    cells = J_STEP * CLON
    return pl.pallas_call(
        network_kernel,
        grid=(CLAT // J_STEP,),
        in_specs=[
            pl.BlockSpec((NLON, LANES), lambda i: (0, i)),
            pl.BlockSpec((J_STEP, CLON, LEV), lambda i: (i, 0, 0)),
            pl.BlockSpec((cells, CHAN), lambda i: (i, 0)),
            pl.BlockSpec((cells, CHAN), lambda i: (i, 0)),
            whole((1, CHAN)),
            whole(w_in.shape),
            whole(w_mid.shape),
            whole(w_out.shape),
        ],
        out_specs=[
            pl.BlockSpec((J_STEP, CLON, LEV), lambda i: (i, 0, 0)),
            pl.BlockSpec((NLON, LANES), lambda i: (0, i)),
        ],
        out_shape=[
            jax.ShapeDtypeStruct((CLAT, CLON, LEV), f32),
            jax.ShapeDtypeStruct((NLON, JL), bf16),
        ],
        scratch_shapes=[pltpu.VMEM((cells, LEV), bf16), pltpu.VMEM((cells, LEV), f32)],
        compiler_params=params(),
        name="network",
    )(inc, background, sums, seen, channel_weight, w_in, w_mid, w_out)


def exchange(rows, axis):
    return lax.all_to_all(rows, axis, split_axis=0, concat_axis=0, tiled=True)


def per_device(
    spectral,
    background,
    columns,
    counts,
    radiances,
    used_pairs,
    channel_weight,
    weight_in,
    weight_mid,
    weight_out,
):
    table = wave_table()
    lat_index = lax.axis_index("lat").astype(jnp.int32).reshape(1)
    legendre, fourier = legendre_transform(lat_index, spectral)
    fourier = exchange(fourier, "lat")
    sums, seen = column_sums(counts, columns, used_pairs.reshape(CAP, 1), radiances[0])
    increment = exchange(waves_to_grid(fourier, table), "lev")
    grid_grad, send = network(
        increment,
        background,
        sums,
        seen,
        channel_weight.reshape(1, CHAN),
        weight_in,
        weight_mid,
        weight_out,
    )
    coeff = exchange(grid_to_waves(exchange(send, "lev"), table), "lat")
    return (legendre_adjoint(legendre, coeff), grid_grad)


def solution(mesh):
    in_specs = (
        P(None, "lev", "lat", None),
        P("lat", "lev", None),
        P(("lat", "lev"), None),
        P(("lat", "lev")),
        P(("lat", "lev"), None, None),
        P(("lat", "lev"), None),
        P(),
        P(),
        P(),
        P(),
    )
    out_specs = (P(None, "lev", "lat", None), P("lat", "lev", None))
    return jax.shard_map(
        per_device, mesh=mesh, in_specs=in_specs, out_specs=out_specs, check_vma=False
    )
```

time: 658 us -> 129 us (0.20); the launches traced: 645 us -> 128 us
  loops' own time: 163 us -> 0 us
  local copies, waits for them, and re-layouts: 169 us -> 6.96 us
  other arithmetic: 85.6 us -> 0 us
  blocking collectives: 125 us -> 46 us
  Pallas kernels: 0 us -> 65.8 us
  matrix products: 55.4 us -> 0 us
  starting transfers between devices: 33.9 us -> 7.77 us
  waiting for transfers between devices: 8.66 us -> 0.01 us
    another operation x1 -> x0, loops' own time: 163 us -> none  [legendre_table(): lax.scan(advance, (zeros, zeros, zeros), jnp.arange(degree_total, dtype=j...]
    unnamed x1 -> x0, blocking collectives: 69.5 us -> none
    pallas_call x0 -> x6, Pallas kernels: none -> 65.8 us  [the longest x1 25.3 us: network(): pl.pallas_call(network_kernel, grid=(CLAT // J_STEP,), in_specs=[pl.Block...]
    dot_general x7 -> x0, matrix products: 41 us -> none  [the longest x1 13.3 us: per_device(): jnp.einsum('nmj,clmj->clmn', legendre, coeff_grad, precision=highest)]
    dynamic_update_slice x35 -> x0, local copies, waits for them, and re-layouts: 39.8 us -> none  [the longest x32 25.3 us: legendre_table(): lax.scan(advance, (zeros, zeros, zeros), jnp.arange(degree_total, dtype=j...]
    all_to_all x14 -> x0, local copies, waits for them, and re-layouts: 33.9 us -> none  [the longest x3 9.01 us: per_device(): lax.all_to_all(fourier, 'lat', split_axis=3, concat_axis=2, tiled=True)]
    while x224 -> x0, other arithmetic: 31.7 us -> none
    gather x5 -> x0, local copies, waits for them, and re-layouts: 28.1 us -> none  [the longest x1 7.03 us: dealt(): jnp.take(flat_observed, flat_pos, axis=0)]
  transfers between devices with their start and end apart: 5 -> 1, of which waited for: 1 -> 0; matrix products, arithmetic and copies ran while one was open for 16% -> 1% of each run, Pallas kernels for 0% -> 12%
where the time goes in v1:
time: 129 us; the launch traced here: 128 us
  Pallas kernels  65.8 us (51%)
  blocking collectives  46 us (36%)
  starting transfers between devices  7.77 us (6%)
  local copies, waits for them, and re-layouts  6.96 us (5%)
  between operations  1.32 us (1%)
    all_to_all x3, blocking collectives, exchange(): return lax.all_to_all(rows, axis, split_axis=0, concat_axis=0, tiled=True)  46 us
    pallas_call x1, Pallas kernels, network(): pl.pallas_call(network_kernel, grid=(CLAT // J_STEP,), in_specs=[pl.Block...  25.3 us
    pallas_call x1, Pallas kernels, column_sums(): pl.pallas_call(sums_kernel, grid_spec=pltpu.PrefetchScalarGridSpec(num_sc...  15.6 us
    pallas_call x1, Pallas kernels, legendre_transform(): pl.pallas_call(legendre_kernel, grid_spec=pltpu.PrefetchScalarGridSpec(nu...  12.3 us
    all_to_all x1, starting transfers between devices, exchange(): return lax.all_to_all(rows, axis, split_axis=0, concat_axis=0, tiled=True)  7.77 us
    pallas_call x1, Pallas kernels, legendre_adjoint(): pl.pallas_call(adjoint_kernel, grid=(ML // M_STEP,), in_specs=[pl.BlockSp...  7.08 us
    pallas_call x1, Pallas kernels, waves_to_grid(): pl.pallas_call(waves_kernel, out_shape=jax.ShapeDtypeStruct((NLON, JL), b...  2.82 us
    pallas_call x1, Pallas kernels, grid_to_waves(): pl.pallas_call(waves_adjoint_kernel, out_shape=jax.ShapeDtypeStruct((NLAT...  2.71 us
  transfers between devices with their start and end apart: 1, of which 0 were waited for; matrix products, arithmetic and copies ran while one was open for 1% of the time, Pallas kernels for 12%

profile of v1, /device:TPU:1, one launch (start us, length us, event | category | flops | bytes accessed | tf_op | source)
XLA Modules:
  0.0 127.8 jit_solution(11299428916853626288)
XLA Ops:
  0.6 0.0 copy-start.1
  0.6 1.3 %reshape.28 = f32[512,2,128]{2,1,0:T(2,128)S(1)} reshape(f32[2,8,32,256]{3,2,1,0:T(8,128)} %param.13) | data formatting | bytes 1048576 | tf_op jit(solution)/shard_map/reshape | solution.py:174
  1.9 0.8 copy.19
  2.8 12.3 %legendre.1 = (bf16[32,256,256]{2,1,0:T(8,128)(2,1)}, bf16[384,512]{1,0:T(8,128)(2,1)}) custom-call(s32[1]{0:T(128)} %bitcast.lat_ref, f32[8,256]{1,0:T(8,128)} %constant.13.clone.geo_ref, f32[256,128]{1,0:T(8,128)} %constant.14.clone.norm_ref, f32[2,512,128]{2,1,0:T(8,128)} %bitcast.23), custom_call_target="tpu_custom_call" | custom-call | tf_op jit(solution)/shard_map/legendre/pallas_call | solution.py:176
  15.1 13.9 %all_to_all.44 = bf16[8,48,512]{2,1,0:T(8,128)(2,1)} all-to-all(bf16[8,48,512]{2,1,0:T(8,128)(2,1)} %bitcast.28), channel_id=1, replica_groups=mesh['lat'=8,'lev'=16] {'lat'}, dimensions={0} | all-to-all | bytes 786432 | tf_op jit(solution)/shard_map/all_to_all | solution.py:428
  29.0 2.8 %waves.1 = bf16[768,384]{1,0:T(8,128)(2,1)} custom-call(bf16[384,512]{1,0:T(8,128)(2,1)} %bitcast.26, bf16[768,512]{1,0:T(8,128)(2,1)} %constant.20.table_ref), custom_call_target="tpu_custom_call" | custom-call | tf_op jit(solution)/shard_map/waves/pallas_call | solution.py:264
  31.9 7.8 %all-to-all-start.1 = ((bf16[16,48,384]{2,1,0:T(8,128)(2,1)}), bf16[16,48,384]{2,1,0:T(8,128)(2,1)S(1)}, u32[]{:S(2)}, u32[]{:S(2)}) async-start(bf16[16,48,384]{2,1,0:T(8,128)(2,1)} %bitcast.19), calls=%async_computation.1 | async-start | bytes 1179648 | tf_op jit(solution)/shard_map/all_to_all | solution.py:428
  40.3 0.0 copy-done.1
  40.3 1.3 %copy.16.pairs_ref = s32[2048,1]{1,0:T(8,128)} copy(s32[2048,1]{0,1:T(1,128)S(1)} %bitcast.29) | data formatting | bytes 16384 | tf_op jit(solution)/shard_map/reshape | solution.py:447
  41.6 15.6 %column_sums.1 = (f32[2304,512]{1,0:T(8,128)}, f32[2304,512]{1,0:T(8,128)}) custom-call(s32[1]{0:T(128)S(6)} %copy.20.count_ref, s32[1,2048]{1,0:T(1,128)} %columns_ref.1, s32[2048,1]{1,0:T(8,128)} %copy.16.pairs_ref, bf16[2048,512]{1,0:T(8,128)(2,1)} %bitcast.22), custom_call_target="tpu_custom_call" | custom-call | tf_op jit(solution)/shard_map/column_sums/pallas_call | solution.py:326
  57.2 0.0 all-to-all-done.1
  57.2 0.0 copy-start
  57.2 0.8 copy-done
  58.0 25.3 %network.1 = (f32[48,48,128]{2,1,0:T(8,128)}, bf16[768,384]{1,0:T(8,128)(2,1)}) custom-call(bf16[768,384]{1,0:T(8,128)(2,1)} %bitcast.18, bf16[48,48,128]{2,1,0:T(8,128)(2,1)} %back_ref.1, f32[2304,512]{1,0:T(8,128)} %get-tuple-element.10.sum_ref, f32[2304,512]{1,0:T(8,128)} %get-tuple-element.11.seen_ref, f32[1,512]{1,0:T(1,128)} %bitcast.30, ...), custom_call_target="tpu_custom_call" | custom-call | tf_op jit(solution)/shard_map/network/pallas_call | solution.py:400
  83.3 17.1 %all_to_all.45 = bf16[16,48,384]{2,1,0:T(8,128)(2,1)} all-to-all(bf16[16,48,384]{2,1,0:T(8,128)(2,1)} %bitcast.27), channel_id=1, replica_groups=mesh['lat'=8,'lev'=16] {'lev'}, dimensions={0} | all-to-all | bytes 1179648 | tf_op jit(solution)/shard_map/all_to_all | solution.py:428
  100.4 2.7 %waves_adjoint.1 = bf16[384,512]{1,0:T(8,128)(2,1)} custom-call(bf16[768,384]{1,0:T(8,128)(2,1)} %bitcast.20, bf16[768,512]{1,0:T(8,128)(2,1)} %constant.20.table_ref), custom_call_target="tpu_custom_call" | custom-call | tf_op jit(solution)/shard_map/waves_adjoint/pallas_call | solution.py:287
  103.1 15.0 %all_to_all.46 = bf16[8,48,512]{2,1,0:T(8,128)(2,1)} all-to-all(bf16[8,48,512]{2,1,0:T(8,128)(2,1)} %bitcast.25), channel_id=1, replica_groups=mesh['lat'=8,'lev'=16] {'lat'}, dimensions={0} | all-to-all | bytes 786432 | tf_op jit(solution)/shard_map/all_to_all | solution.py:428
  118.1 7.1 %legendre_adjoint.1 = f32[2,512,128]{2,1,0:T(8,128)} custom-call(bf16[32,256,256]{2,1,0:T(8,128)(2,1)} %get-tuple-element.8.p_ref, bf16[384,512]{1,0:T(8,128)(2,1)} %bitcast.24), custom_call_target="tpu_custom_call" | custom-call | tf_op jit(solution)/shard_map/legendre_adjoint/pallas_call | solution.py:238
  125.1 1.4 %copy.17 = f32[512,2,128]{2,1,0:T(2,128)S(1)} copy(f32[512,2,128]{2,0,1:T(8,128)} %bitcast.21) | data formatting | bytes 1048576 | tf_op jit(solution)/shard_map/transpose | solution.py:248
  126.6 1.2 reshape.31
Async XLA Ops:
  0.6 39.7 %copy-start.1 = (s32[1,2048]{1,0:T(1,128)S(1)}, s32[1,2048]{1,0:T(1,128)}, u32[]{:S(2)}) copy-start(s32[1,2048]{1,0:T(1,128)} %param.18) | copy-start | bytes 24580
  31.9 25.3 %all-to-all-start.1 = ((bf16[16,48,384]{2,1,0:T(8,128)(2,1)}), bf16[16,48,384]{2,1,0:T(8,128)(2,1)S(1)}, u32[]{:S(2)}, u32[]{:S(2)}) async-start(bf16[16,48,384]{2,1,0:T(8,128)(2,1)} %bitcast.19), calls=%async_computation.1 | async-start | bytes 1179648 | tf_op jit(solution)/shard_map/all_to_all | solution.py:428
  57.2 0.8 copy-start

commit v2 on v1

--- a/solution.py
+++ b/solution.py
@@ -1,3 +1,4 @@
+import functools
 import math
 
 import jax
@@ -37,8 +38,19 @@
 f32 = jnp.float32
 
 
-def params(**kwargs):
-    return pltpu.CompilerParams(vmem_limit_bytes=56 << 20, **kwargs)
+def params(mib):
+    return pltpu.CompilerParams(vmem_limit_bytes=mib << 20)
+
+
+def on_chip(array):
+    return pltpu.with_memory_space_constraint(array, pltpu.VMEM)
+
+
+def in_hbm(array):
+    return pltpu.with_memory_space_constraint(array, pltpu.HBM)
+
+
+VMEM_SPEC = pl.BlockSpec(memory_space=pltpu.VMEM)
 
 
 def dot_nt(a, b):
@@ -75,15 +87,18 @@
     return jnp.asarray(table, f32).astype(bf16)
 
 
-M_STEP = 4
-
-
-def legendre_kernel(lat_ref, geo_ref, norm_ref, spec_ref, p_ref, four_ref, table, waves):
+M_STEP = 8
+ADJOINT_STEP = 16
+
+
+def legendre_kernel(lat_ref, geo_ref, norm_ref, spec_ref, p_ref, four_ref, table, waves, halves):
     step = pl.program_id(0)
     groups = range(ML // 8)
 
     @pl.when(step == 0)
     def _():
+        for h in (0, 1):
+            halves[h] = spec_ref[:, h * LANES : (h + 1) * LANES]
         m0 = lat_ref[0] * ML
         sub = lax.broadcasted_iota(jnp.int32, (8, LANES), 0)
         mf = [(sub + (m0 + 8 * g)).astype(f32) for g in groups]
@@ -148,9 +163,12 @@
             [table[h, pl.ds(m, N, stride=ML), :].astype(bf16) for h in (0, 1)], axis=1
         )
         p_ref[k] = p_m
-        s = jnp.concatenate([spec_ref[h, pl.ds(m, 2 * LL, stride=ML), :] for h in (0, 1)], axis=1)
-        signed = s * (alternate if k % 2 == 0 else -alternate)
-        out = dot_nn(jnp.concatenate([s, signed], axis=0).astype(bf16), p_m)
+        s = jnp.concatenate([halves[h, pl.ds(m, 2 * LL, stride=ML), :] for h in (0, 1)], axis=1)
+        s = jnp.concatenate([s, s * (alternate if k % 2 == 0 else -alternate)], axis=0)
+        high = s.astype(bf16)
+        low = (s - high.astype(f32)).astype(bf16)
+        out = dot_nn(jnp.concatenate([high, low], axis=0), p_m)
+        out = out[: 4 * LL] + out[4 * LL :]
         for hemi in (0, 1):
             for c in (0, 1):
                 first = (hemi * 2 + c) * LL
@@ -171,14 +189,13 @@
 
 def legendre_transform(lat_index, spectral):
     geo, norm = geometry()
-    spec = spectral.reshape(ROWS, 2, LANES).transpose(1, 0, 2)
     whole = lambda shape: pl.BlockSpec(shape, lambda i, *_: (0,) * len(shape))
     return pl.pallas_call(
         legendre_kernel,
         grid_spec=pltpu.PrefetchScalarGridSpec(
             num_scalar_prefetch=1,
             grid=(ML // M_STEP,),
-            in_specs=[whole((8, 256)), whole((M, LANES)), whole((2, ROWS, LANES))],
+            in_specs=[whole((8, 256)), whole((M, LANES)), whole((ROWS, N))],
             out_specs=[
                 pl.BlockSpec((M_STEP, N, 256), lambda i, *_: (i, 0, 0)),
                 whole((NLAT, ROWS)),
@@ -186,18 +203,19 @@
             scratch_shapes=[
                 pltpu.VMEM((2, N * ML, LANES), f32),
                 pltpu.VMEM((2, 2, ROWS, LANES), f32),
+                pltpu.VMEM((2, ROWS, LANES), f32),
             ],
         ),
         out_shape=[
-            jax.ShapeDtypeStruct((ML, N, 256), bf16),
-            jax.ShapeDtypeStruct((NLAT, ROWS), bf16),
+            pltpu.HBM((ML, N, 256), bf16),
+            pltpu.HBM((NLAT, ROWS), bf16),
         ],
-        compiler_params=params(),
+        compiler_params=params(18),
         name="legendre",
-    )(lat_index, jnp.asarray(geo), jnp.asarray(norm), spec)
-
-
-def adjoint_kernel(p_ref, rows_ref, out_ref, folded):
+    )(lat_index, in_hbm(jnp.asarray(geo)), in_hbm(jnp.asarray(norm)), in_hbm(spectral.reshape(ROWS, N)))
+
+
+def adjoint_kernel(p_ref, rows_ref, out_ref, folded, held):
     step = pl.program_id(0)
 
     @pl.when(step == 0)
@@ -213,8 +231,8 @@
                 folded[part, h] = value[:, h * LANES : (h + 1) * LANES]
 
     lane = lax.broadcasted_iota(jnp.int32, (2 * LL, N), 1)
-    for k in range(M_STEP):
-        m = step * M_STEP + k
+    for k in range(ADJOINT_STEP):
+        m = step * ADJOINT_STEP + k
         pieces = []
         for part in (0, 1):
             for c in (0, 1):
@@ -227,28 +245,40 @@
                         axis=1,
                     )
                 )
-        value = dot_nt(jnp.concatenate(pieces, axis=0).astype(bf16), p_ref[k])
+        value = dot_nt(jnp.concatenate(pieces, axis=0).astype(bf16), p_ref[m])
         picked = jnp.where(lane % 2 == k % 2, value[: 2 * LL], value[2 * LL :])
         for h in (0, 1):
-            out_ref[h, pl.ds(m, 2 * LL, stride=ML), :] = picked[:, h * LANES : (h + 1) * LANES]
+            held[h, pl.ds(m, 2 * LL, stride=ML), :] = picked[:, h * LANES : (h + 1) * LANES]
+
+    @pl.when(step == pl.num_programs(0) - 1)
+    def _():
+        for h in (0, 1):
+            out_ref[:, h * LANES : (h + 1) * LANES] = held[h]
 
 
 def legendre_adjoint(table, rows):
     whole = lambda shape: pl.BlockSpec(shape, lambda i: (0,) * len(shape))
     out = pl.pallas_call(
         adjoint_kernel,
-        grid=(ML // M_STEP,),
-        in_specs=[pl.BlockSpec((M_STEP, N, 256), lambda i: (i, 0, 0)), whole((NLAT, ROWS))],
-        out_specs=whole((2, ROWS, LANES)),
-        scratch_shapes=[pltpu.VMEM((2, 2, ROWS, LANES), f32)],
-        out_shape=jax.ShapeDtypeStruct((2, ROWS, LANES), f32),
-        compiler_params=params(),
+        grid=(ML // ADJOINT_STEP,),
+        in_specs=[
+            VMEM_SPEC,
+            VMEM_SPEC,
+        ],
+        out_specs=whole((ROWS, N)),
+        scratch_shapes=[
+            pltpu.VMEM((2, 2, ROWS, LANES), f32),
+            pltpu.VMEM((2, ROWS, LANES), f32),
+        ],
+        out_shape=jax.ShapeDtypeStruct((ROWS, N), f32),
+        compiler_params=params(12),
         name="legendre_adjoint",
-    )(table, rows)
-    return out.transpose(1, 0, 2).reshape(2, LL, ML, N)
-
-
-def waves_kernel(rows_ref, table_ref, out_ref, held):
+    )(on_chip(table), rows)
+    return out.reshape(2, LL, ML, N)
+
+
+def waves_kernel(rows_ref, table_ref, after_ref, out_ref, held):
+    del after_ref
     for pair in range(N_LAT // 2):
         for l in range(LL):
             pieces = [
@@ -260,14 +290,15 @@
     out_ref[...] = dot_nt(table_ref[...], waves).astype(bf16)
 
 
-def waves_to_grid(rows, table):
+def waves_to_grid(rows, table, after):
     return pl.pallas_call(
         waves_kernel,
-        out_shape=jax.ShapeDtypeStruct((NLON, JL), bf16),
+        in_specs=[VMEM_SPEC, VMEM_SPEC, pl.BlockSpec(memory_space=pl.ANY)],
+        out_shape=pltpu.HBM((NLON, JL), bf16),
         scratch_shapes=[pltpu.VMEM((N_LAT // 2, JL, LANES), f32)],
-        compiler_params=params(),
+        compiler_params=params(12),
         name="waves",
-    )(rows, table)
+    )(rows, table, in_hbm(after))
 
 
 def waves_adjoint_kernel(grid_ref, table_ref, out_ref, held):
@@ -286,60 +317,165 @@
 def grid_to_waves(grid, table):
     return pl.pallas_call(
         waves_adjoint_kernel,
-        out_shape=jax.ShapeDtypeStruct((NLAT, ROWS), bf16),
+        in_specs=[VMEM_SPEC, VMEM_SPEC],
+        out_shape=pltpu.HBM((NLAT, ROWS), bf16),
         scratch_shapes=[pltpu.VMEM((N_LAT // 2, JL, LANES), f32)],
-        compiler_params=params(),
+        compiler_params=params(12),
         name="waves_adjoint",
     )(grid, table)
 
 
-SUM_TILE = 256
-
-
-def sums_kernel(count_ref, columns_ref, pairs_ref, obs_ref, sum_ref, seen_ref, masked):
+GROUP = 256
+GROUPS = CELLS // GROUP
+TILE = 240
+SUM_TILE = 2 * TILE
+ROW_TILES = -(-(CAP + 7 * GROUPS) // SUM_TILE)
+MAX_ROWS = ROW_TILES * SUM_TILE
+
+
+def assign_rows(count, columns):
+    slot = lax.broadcasted_iota(jnp.int32, (1, CAP), 1)
+    valid = slot < count
+    group = jnp.where(valid, lax.shift_right_logical(columns, 8), -1)
+    inner = lax.broadcasted_iota(jnp.int32, (GROUP, CAP), 0) == (columns & (GROUP - 1))
+    inner = jnp.where(inner, 1.0, 0.0).astype(bf16)
+    in_group = lax.broadcasted_iota(jnp.int32, (16, CAP), 0) == group
+    seen = dot_nt(jnp.where(in_group, 1.0, 0.0).astype(bf16), inner)
+    used = jnp.where(seen > 0.5, 1.0, 0.0)
+    before = lax.broadcasted_iota(jnp.int32, (GROUP, GROUP), 0) < lax.broadcasted_iota(
+        jnp.int32, (GROUP, GROUP), 1
+    )
+    rank = dot_nn(used.astype(bf16), jnp.where(before, 1.0, 0.0).astype(bf16))
+    padded = jnp.floor((jnp.sum(used, axis=1, keepdims=True) + 7.0) * 0.125) * 8.0
+    padded = jnp.broadcast_to(padded, (16, LANES))
+    sub = lax.broadcasted_iota(jnp.int32, (16, LANES), 0)
+    first = jnp.zeros((16, LANES), f32)
+    for g in range(GROUPS):
+        first = first + jnp.where(sub > g, padded[g : g + 1, :], 0.0)
+    of_slot = dot_nn(rank.astype(bf16), inner) + first[:, 0:1]
+    row = jnp.sum(jnp.where(in_group, of_slot, 0.0), axis=0, keepdims=True)
+    row = jnp.where(valid, row, -1.0).astype(jnp.int32)
+    return row, jnp.where(used > 0.5, rank, -1.0), first
+
+
+def sum_rows(step, total, row_of_slot, masked, sum_ref):
+    @pl.when(step * SUM_TILE < total)
+    def _():
+        row = lax.broadcasted_iota(jnp.int32, (SUM_TILE, CAP), 0) + step * SUM_TILE
+        hit = jnp.where(row == row_of_slot, 1.0, 0.0).astype(bf16)
+        sum_ref[...] = dot_nn(hit, masked[...])
+
+
+def active_channels(pairs_ref, value, masked):
+    channel = lax.broadcasted_iota(jnp.int32, (LANES, LANES), 1)
+    for i in range(CAP // LANES):
+        r = slice(i * LANES, (i + 1) * LANES)
+        used = jnp.transpose(jnp.broadcast_to(2 * pairs_ref[:, r], (LANES, LANES)))
+        for c in range(CHAN // LANES):
+            lanes = slice(c * LANES, (c + 1) * LANES)
+            masked[r, lanes] = jnp.where(
+                channel + c * LANES < used, value(r, lanes), 0.0
+            ).astype(bf16)
+
+
+def sums_kernel(
+    count_ref,
+    columns_ref,
+    pairs_ref,
+    obs_ref,
+    after_ref,
+    sum_ref,
+    row_ref,
+    rank_ref,
+    first_ref,
+    masked,
+    total_ref,
+):
+    del after_ref
     step = pl.program_id(0)
-    count = count_ref[0]
 
     @pl.when(step == 0)
     def _():
-        def fill(i, _):
-            r = pl.ds(pl.multiple_of(i * 256, 256), 256)
-            channel = lax.broadcasted_iota(jnp.int32, (256, CHAN), 1)
-            active = channel < 2 * pairs_ref[r, :]
-            masked[r, 0:CHAN] = jnp.where(active, obs_ref[r, :].astype(f32), 0.0).astype(bf16)
-            masked[r, CHAN : 2 * CHAN] = jnp.where(active, 1.0, 0.0).astype(bf16)
-            return 0
-
-        lax.fori_loop(0, CAP // 256, fill, 0)
-
-    cell = lax.broadcasted_iota(jnp.int32, (SUM_TILE, CAP), 0) + step * SUM_TILE
-    slot = lax.broadcasted_iota(jnp.int32, (1, CAP), 1)
-    column = jnp.where(slot < count, columns_ref[...], -1)
-    hit = jnp.where(cell == column, 1.0, 0.0).astype(bf16)
-    sum_ref[...] = dot_nn(hit, masked[:, 0:CHAN])
-    seen_ref[...] = dot_nn(hit, masked[:, CHAN : 2 * CHAN])
-
-
-def column_sums(counts, columns, pairs, obs):
+        row, rank, first = assign_rows(count_ref[0], columns_ref[...])
+        row_ref[...] = row
+        rank_ref[...] = rank
+        first_ref[...] = first.astype(jnp.int32)
+        total_ref[0] = jnp.max(first).astype(jnp.int32)
+        active_channels(pairs_ref, lambda r, lanes: obs_ref[r, lanes].astype(f32), masked)
+
+    sum_rows(step, total_ref[0], row_ref[...], masked, sum_ref)
+
+
+def seen_kernel(first_ref, pairs_ref, row_ref, after_ref, sum_ref, masked):
+    del after_ref
+    step = pl.program_id(0)
+
+    @pl.when(step == 0)
+    def _():
+        active_channels(pairs_ref, lambda r, lanes: 1.0, masked)
+
+    sum_rows(step, first_ref[GROUPS, 0], row_ref[...], masked, sum_ref)
+
+
+ROW_COST = pl.CostEstimate(
+    flops=2 * MAX_ROWS * CAP * CHAN, transcendentals=0, bytes_accessed=MAX_ROWS * CHAN * 4
+)
+
+
+def row_sums(counts, columns, pairs, obs, after):
     whole = lambda shape: pl.BlockSpec(shape, lambda i, *_: (0,) * len(shape))
-    part = pl.BlockSpec((SUM_TILE, CHAN), lambda i, *_: (i, 0))
     return pl.pallas_call(
         sums_kernel,
         grid_spec=pltpu.PrefetchScalarGridSpec(
             num_scalar_prefetch=1,
-            grid=(CELLS // SUM_TILE,),
-            in_specs=[whole((1, CAP)), whole((CAP, 1)), whole((CAP, CHAN))],
-            out_specs=[part, part],
-            scratch_shapes=[pltpu.VMEM((CAP, 2 * CHAN), bf16)],
+            grid=(ROW_TILES,),
+            in_specs=[
+                whole((1, CAP)),
+                whole((1, CAP)),
+                whole((CAP, CHAN)),
+                pl.BlockSpec(memory_space=pl.ANY),
+            ],
+            out_specs=[
+                pl.BlockSpec((SUM_TILE, CHAN), lambda i, *_: (i, 0)),
+                whole((1, CAP)),
+                whole((16, GROUP)),
+                whole((16, LANES)),
+            ],
+            scratch_shapes=[pltpu.VMEM((CAP, CHAN), bf16), pltpu.SMEM((1,), jnp.int32)],
         ),
-        out_shape=[jax.ShapeDtypeStruct((CELLS, CHAN), f32)] * 2,
-        compiler_params=params(),
-        name="column_sums",
-    )(counts, columns, pairs, obs)
+        out_shape=[
+            pltpu.HBM((MAX_ROWS, CHAN), f32),
+            pltpu.HBM((1, CAP), jnp.int32),
+            pltpu.HBM((16, GROUP), f32),
+            pltpu.HBM((16, LANES), jnp.int32),
+        ],
+        compiler_params=params(24),
+        cost_estimate=ROW_COST,
+        name="row_sums",
+    )(counts, in_hbm(columns), in_hbm(pairs), in_hbm(obs), in_hbm(after))
+
+
+def row_seen(first, pairs, row, after):
+    whole = lambda shape: pl.BlockSpec(shape, lambda i: (0,) * len(shape))
+    return pl.pallas_call(
+        seen_kernel,
+        grid=(ROW_TILES,),
+        in_specs=[
+            pl.BlockSpec(memory_space=pltpu.SMEM),
+            whole((1, CAP)),
+            whole((1, CAP)),
+            pl.BlockSpec(memory_space=pl.ANY),
+        ],
+        out_specs=pl.BlockSpec((SUM_TILE, CHAN), lambda i: (i, 0)),
+        scratch_shapes=[pltpu.VMEM((CAP, CHAN), bf16)],
+        out_shape=pltpu.HBM((MAX_ROWS, CHAN), f32),
+        compiler_params=params(24),
+        cost_estimate=ROW_COST,
+        name="row_seen",
+    )(first, in_hbm(pairs), in_hbm(row), in_hbm(after))
 
 
 J_STEP = 16
-TILE = 256
 X_ROWS = 16
 
 
@@ -366,66 +502,157 @@
 
 
 def network_kernel(
-    inc_ref, back_ref, sum_ref, seen_ref, chan_ref, w_in, w_mid, w_out, grad_ref, send_ref, state, grads
+    first_ref,
+    inc_ref,
+    back_ref,
+    rank_ref,
+    sum_hbm,
+    seen_hbm,
+    chan_ref,
+    w_in,
+    w_mid,
+    w_out,
+    grad_ref,
+    send_ref,
+    state,
+    packed,
+    packed_grad,
+    w_twice,
+    sum_buf,
+    seen_buf,
+    sems,
 ):
-    for part in range(CLON // X_ROWS):
-        x0 = part * X_ROWS
-        v = [inc_ref[s * CLON + x0 : s * CLON + x0 + X_ROWS, :].astype(f32) for s in range(N_LEV)]
-        v = swap_blocks(v)
-        for j in range(J_STEP):
-            total = back_ref[j, x0 : x0 + X_ROWS, :].astype(f32) + v[j]
-            state[j * CLON + x0 : j * CLON + x0 + X_ROWS, :] = total.astype(bf16)
-    for i in range(J_STEP * CLON // TILE):
-        r = slice(i * TILE, (i + 1) * TILE)
-        act1, slope1 = silu_and_slope(dot_nn(state[r, :], w_in[...]))
+    total = first_ref[GROUPS, 0]
+    tiles = (total + (TILE - 1)) // TILE
+
+    def fetches(t, slot):
+        r = pl.ds(pl.multiple_of(t * TILE, 8), TILE)
+        return (
+            pltpu.make_async_copy(sum_hbm.at[r, :], sum_buf.at[slot], sems.at[0, slot]),
+            pltpu.make_async_copy(seen_hbm.at[r, :], seen_buf.at[slot], sems.at[1, slot]),
+        )
+
+    for fetch in fetches(0, 0):
+        fetch.start()
+    w_twice[:LEV] = w_in[...]
+    w_twice[LEV:] = w_in[...]
+
+    def to_state(jc, _):
+        lanes = pl.ds(pl.multiple_of(jc * LANES, LANES), LANES)
+        for part in range(CLON // X_ROWS):
+            x0 = part * X_ROWS
+            v = [
+                inc_ref[s * CLON + x0 : s * CLON + x0 + X_ROWS, lanes].astype(f32)
+                for s in range(N_LEV)
+            ]
+            v = swap_blocks(v)
+            for j in range(J_STEP):
+                r = pl.ds(pl.multiple_of((jc * J_STEP + j) * CLON + x0, 16), X_ROWS)
+                grid_state = back_ref[r, :].astype(f32) + v[j]
+                high = grid_state.astype(bf16)
+                state[r, :LEV] = high
+                state[r, LEV:] = (grid_state - high.astype(f32)).astype(bf16)
+        return 0
+
+    lax.fori_loop(0, CLAT // J_STEP, to_state, 0)
+
+    def group_rows(g):
+        first = pl.ds(pl.multiple_of(first_ref[g, 0], 8), GROUP)
+        row = lax.broadcasted_iota(jnp.int32, (GROUP, GROUP), 0).astype(f32)
+        pick = jnp.where(row == rank_ref[g : g + 1, :], 1.0, 0.0).astype(bf16)
+        return first, slice(g * GROUP, (g + 1) * GROUP), pick
+
+    for g in range(GROUPS):
+        rows, cells, pick = group_rows(g)
+        packed[rows, :] = dot_nn(pick, state[cells, :])
+    packed[pl.ds(pl.multiple_of(total, 8), TILE), :] = jnp.zeros((TILE, 2 * LEV), f32)
+
+    def one_tile(t, _):
+        slot = lax.rem(t, 2)
+        for fetch in fetches(t, slot):
+            fetch.wait()
+
+        @pl.when(t + 1 < tiles)
+        def _():
+            for fetch in fetches(t + 1, 1 - slot):
+                fetch.start()
+
+        r = pl.ds(pl.multiple_of(t * TILE, 8), TILE)
+        act1, slope1 = silu_and_slope(dot_nn(packed[r, :].astype(bf16), w_twice[...]))
         act2, slope2 = silu_and_slope(dot_nn(act1.astype(bf16), w_mid[...]))
         evolved = dot_nn(act2.astype(bf16), w_out[...])
-        misfit = (chan_ref[...] * (seen_ref[r, :] * evolved - sum_ref[r, :])).astype(bf16)
+        misfit = (chan_ref[...] * (seen_buf[slot] * evolved - sum_buf[slot])).astype(bf16)
         back2 = (dot_nt(misfit, w_out[...]) * slope2).astype(bf16)
         back1 = (dot_nt(back2, w_mid[...]) * slope1).astype(bf16)
-        grads[r, :] = dot_nt(back1, w_in[...])
-    for j in range(J_STEP):
-        grad_ref[j] = grads[j * CLON : (j + 1) * CLON, :]
-    for part in range(CLON // X_ROWS):
-        x0 = part * X_ROWS
-        v = [grads[j * CLON + x0 : j * CLON + x0 + X_ROWS, :] for j in range(J_STEP)]
-        v = swap_blocks(v)
-        for s in range(N_LEV):
-            send_ref[s * CLON + x0 : s * CLON + x0 + X_ROWS, :] = v[s].astype(bf16)
-
-
-def network(inc, background, sums, seen, channel_weight, w_in, w_mid, w_out):
-    whole = lambda shape: pl.BlockSpec(shape, lambda i: (0,) * len(shape))
-    cells = J_STEP * CLON
-    return pl.pallas_call(
+        packed_grad[r, :] = dot_nt(back1, w_in[...])
+        return 0
+
+    lax.fori_loop(0, tiles, one_tile, 0)
+    packed_grad[pl.ds(pl.multiple_of(tiles * TILE, 8), GROUP), :] = jnp.zeros((GROUP, LEV), f32)
+    for g in range(GROUPS):
+        rows, cells, pick = group_rows(g)
+        value = packed_grad[rows, :]
+        high = value.astype(bf16)
+        low = (value - high.astype(f32)).astype(bf16)
+        value = dot_tn(pick, jnp.concatenate([high, low], axis=1))
+        grad_ref[cells, :] = value[:, :LEV] + value[:, LEV:]
+
+    def to_send(jc, _):
+        lanes = pl.ds(pl.multiple_of(jc * LANES, LANES), LANES)
+        for part in range(CLON // X_ROWS):
+            x0 = part * X_ROWS
+            v = [
+                grad_ref[pl.ds(pl.multiple_of((jc * J_STEP + j) * CLON + x0, 16), X_ROWS), :]
+                for j in range(J_STEP)
+            ]
+            v = swap_blocks(v)
+            for s in range(N_LEV):
+                send_ref[s * CLON + x0 : s * CLON + x0 + X_ROWS, lanes] = v[s].astype(bf16)
+        return 0
+
+    lax.fori_loop(0, CLAT // J_STEP, to_send, 0)
+
+
+def network(first, inc, background, rank, sums, seen, channel_weight, w_in, w_mid, w_out):
+    anywhere = pl.BlockSpec(memory_space=pl.ANY)
+    grad, send = pl.pallas_call(
         network_kernel,
-        grid=(CLAT // J_STEP,),
-        in_specs=[
-            pl.BlockSpec((NLON, LANES), lambda i: (0, i)),
-            pl.BlockSpec((J_STEP, CLON, LEV), lambda i: (i, 0, 0)),
-            pl.BlockSpec((cells, CHAN), lambda i: (i, 0)),
-            pl.BlockSpec((cells, CHAN), lambda i: (i, 0)),
-            whole((1, CHAN)),
-            whole(w_in.shape),
-            whole(w_mid.shape),
-            whole(w_out.shape),
+        in_specs=[pl.BlockSpec(memory_space=pltpu.SMEM), VMEM_SPEC, VMEM_SPEC, VMEM_SPEC]
+        + [anywhere] * 2
+        + [VMEM_SPEC] * 4,
+        out_specs=[VMEM_SPEC, VMEM_SPEC],
+        out_shape=[
+            jax.ShapeDtypeStruct((CELLS, LEV), f32),
+            pltpu.HBM((NLON, JL), bf16),
         ],
-        out_specs=[
-            pl.BlockSpec((J_STEP, CLON, LEV), lambda i: (i, 0, 0)),
-            pl.BlockSpec((NLON, LANES), lambda i: (0, i)),
+        scratch_shapes=[
+            pltpu.VMEM((CELLS, 2 * LEV), bf16),
+            pltpu.VMEM((MAX_ROWS + GROUP, 2 * LEV), f32),
+            pltpu.VMEM((MAX_ROWS + GROUP, LEV), f32),
+            pltpu.VMEM((2 * LEV, w_in.shape[1]), bf16),
+            pltpu.VMEM((2, TILE, CHAN), f32),
+            pltpu.VMEM((2, TILE, CHAN), f32),
+            pltpu.SemaphoreType.DMA((2, 2)),
         ],
-        out_shape=[
-            jax.ShapeDtypeStruct((CLAT, CLON, LEV), f32),
-            jax.ShapeDtypeStruct((NLON, JL), bf16),
-        ],
-        scratch_shapes=[pltpu.VMEM((cells, LEV), bf16), pltpu.VMEM((cells, LEV), f32)],
-        compiler_params=params(),
+        compiler_params=params(30),
         name="network",
-    )(inc, background, sums, seen, channel_weight, w_in, w_mid, w_out)
+    )(
+        first,
+        inc,
+        in_hbm(background),
+        in_hbm(rank),
+        in_hbm(sums),
+        in_hbm(seen),
+        channel_weight,
+        in_hbm(w_in),
+        on_chip(w_mid),
+        in_hbm(w_out),
+    )
+    return grad.reshape(CLAT, CLON, LEV), send
 
 
 def exchange(rows, axis):
-    return lax.all_to_all(rows, axis, split_axis=0, concat_axis=0, tiled=True)
+    return on_chip(lax.all_to_all(rows, axis, split_axis=0, concat_axis=0, tiled=True))
 
 
 def per_device(
@@ -440,15 +667,18 @@
     weight_mid,
     weight_out,
 ):
-    table = wave_table()
+    table = on_chip(wave_table())
     lat_index = lax.axis_index("lat").astype(jnp.int32).reshape(1)
     legendre, fourier = legendre_transform(lat_index, spectral)
-    fourier = exchange(fourier, "lat")
-    sums, seen = column_sums(counts, columns, used_pairs.reshape(CAP, 1), radiances[0])
-    increment = exchange(waves_to_grid(fourier, table), "lev")
+    sums, row, rank, first = row_sums(counts, columns, used_pairs, radiances[0], fourier)
+    waves = waves_to_grid(exchange(fourier, "lat"), table, first)
+    seen = row_seen(first, used_pairs, row, waves)
+    increment = exchange(waves, "lev")
     grid_grad, send = network(
+        first,
         increment,
-        background,
+        background.reshape(CELLS, LEV),
+        rank,
         sums,
         seen,
         channel_weight.reshape(1, CHAN),

time: 129 us -> 101 us (0.78)
  blocking collectives: 46 us -> 30.3 us
  Pallas kernels: 65.8 us -> 50.6 us
  local copies, waits for them, and re-layouts: 6.96 us -> 0.71 us
  starting transfers between devices: 7.77 us -> 13.6 us
  waiting for transfers between devices: 0.01 us -> 3.1 us
    all_to_all x3 -> x2, blocking collectives: 46 us -> 30.3 us  [exchange(): lax.all_to_all(rows, axis, split_axis=0, concat_axis=0, tiled=True)]
    pallas_call x5 -> x6, Pallas kernels: 53.5 us -> 38.6 us  [the longest x1 17.3 us: network(): pl.pallas_call(network_kernel, in_specs=[pl.BlockSpec(memory_space=pltpu....]
    all_to_all x1 -> x2, starting transfers between devices: 7.77 us -> 13.6 us  [exchange(): lax.all_to_all(rows, axis, split_axis=0, concat_axis=0, tiled=True)]
    reshape x4 -> x0, local copies, waits for them, and re-layouts: 4.69 us -> none  [the longest x2 2.13 us: legendre_transform(): spec = spectral.reshape(ROWS, 2, LANES).transpose(1, 0, 2)]
    all_to_all x1 -> x2, waiting for transfers between devices: 0.01 us -> 3.1 us  [exchange(): lax.all_to_all(rows, axis, split_axis=0, concat_axis=0, tiled=True)]
    transpose x1 -> x0, local copies, waits for them, and re-layouts: 1.45 us -> none  [legendre_adjoint(): return out.transpose(1, 0, 2).reshape(2, LL, ML, N)]
  transfers between devices with their start and end apart: 1 -> 2, of which waited for: 0 -> 1; matrix products, arithmetic and copies ran while one was open for 1% -> 0% of each run, Pallas kernels for 12% -> 15%
where the time goes in v2:
time: 101 us; the launch traced here: 99.6 us
  Pallas kernels  50.6 us (50%)
  blocking collectives  30.3 us (30%)
  starting transfers between devices  13.6 us (13%)
  waiting for transfers between devices  3.1 us (3%)
  between operations  1.34 us (1%)
    all_to_all x2, blocking collectives, exchange(): lax.all_to_all(rows, axis, split_axis=0, concat_axis=0, tiled=True)  30.3 us
    pallas_call x1, Pallas kernels, network(): pl.pallas_call(network_kernel, in_specs=[pl.BlockSpec(memory_space=pltpu....  17.3 us
    all_to_all x2, starting transfers between devices, exchange(): lax.all_to_all(rows, axis, split_axis=0, concat_axis=0, tiled=True)  13.6 us
    pallas_call x1, Pallas kernels, legendre_transform(): pl.pallas_call(legendre_kernel, grid_spec=pltpu.PrefetchScalarGridSpec(nu...  11.9 us
    pallas_call x1, Pallas kernels, row_sums(): pl.pallas_call(sums_kernel, grid_spec=pltpu.PrefetchScalarGridSpec(num_sc...  8.48 us
    pallas_call x1, Pallas kernels, row_seen(): pl.pallas_call(seen_kernel, grid=(ROW_TILES,), in_specs=[pl.BlockSpec(mem...  6.94 us
    all_to_all x2, waiting for transfers between devices, exchange(): lax.all_to_all(rows, axis, split_axis=0, concat_axis=0, tiled=True)  3.1 us
    pallas_call x1, Pallas kernels, legendre_adjoint(): pl.pallas_call(adjoint_kernel, grid=(ML // ADJOINT_STEP,), in_specs=[VMEM...  2.94 us
  transfers between devices with their start and end apart: 2, of which 1 were waited for; matrix products, arithmetic and copies ran while one was open for 0% of the time, Pallas kernels for 15%

profile of v2, /device:TPU:1, one launch (start us, length us, event | category | flops | bytes accessed | tf_op | source)
XLA Modules:
  0.0 99.6 jit_solution(13002776194230793389)
XLA Ops:
  0.6 11.9 %legendre.1 = (bf16[32,256,256]{2,1,0:T(8,128)(2,1)}, bf16[384,512]{1,0:T(8,128)(2,1)}) custom-call(s32[1]{0:T(128)} %bitcast.lat_ref, f32[8,256]{1,0:T(8,128)} %constant.13.clone.geo_ref, f32[256,128]{1,0:T(8,128)} %constant.14.clone.norm_ref, f32[512,256]{1,0:T(8,128)} %bitcast.25), custom_call_target="tpu_custom_call" | custom-call | tf_op jit(solution)/shard_map/legendre/pallas_call | solution.py:193
  12.6 5.8 %all-to-all-start = ((bf16[8,48,512]{2,1,0:T(8,128)(2,1)}), bf16[8,48,512]{2,1,0:T(8,128)(2,1)S(1)}, u32[]{:S(2)}, u32[]{:S(2)}) async-start(bf16[8,48,512]{2,1,0:T(8,128)(2,1)} %bitcast.26), calls=%async_computation | async-start | bytes 786432 | tf_op jit(solution)/shard_map/all_to_all | solution.py:655
  19.0 0.0 copy-start.1
  19.0 8.5 %row_sums.1 = (f32[2400,512]{1,0:T(8,128)}, s32[1,2048]{1,0:T(1,128)}, f32[16,256]{1,0:T(8,128)}, s32[16,128]{1,0:T(8,128)}) custom-call(s32[1]{0:T(128)S(6)} %copy.15.count_ref, s32[1,2048]{1,0:T(1,128)} %columns_ref.1, s32[1,2048]{1,0:T(1,128)} %pairs_ref.3, bf16[2048,512]{1,0:T(8,128)(2,1)} %bitcast.27, bf16[384,512]{1,0:T(8,128)(2,1)} %get-tuple-element.11.after_ref), custom_call_target="tpu_custom_call" | custom-call | flops 5033164800 | bytes 4915200 | tf_op jit(solution)/shard_map/row_sums/pallas_call | solution.py:427
  27.5 0.0 all-to-all-done
  27.5 0.0 copy-done.1
  27.5 1.5 %waves.1.after_ref = bf16[768,384]{1,0:T(8,128)(2,1)} custom-call(bf16[384,512]{1,0:T(8,128)(2,1)S(1)} %bitcast.17, bf16[768,512]{1,0:T(8,128)(2,1)S(1)} %copy-done.1, s32[16,128]{1,0:T(8,128)} %get-tuple-element.12.after_ref.first_ref), custom_call_target="tpu_custom_call" | custom-call | tf_op jit(solution)/shard_map/waves/pallas_call | solution.py:294
  29.1 7.8 %all-to-all-start.1 = ((bf16[16,48,384]{2,1,0:T(8,128)(2,1)}), bf16[16,48,384]{2,1,0:T(8,128)(2,1)S(1)}, u32[]{:S(2)}, u32[]{:S(2)}) async-start(bf16[16,48,384]{2,1,0:T(8,128)(2,1)} %bitcast.20), calls=%async_computation.1 | async-start | bytes 1179648 | tf_op jit(solution)/shard_map/all_to_all | solution.py:655
  36.8 0.0 copy-start.3
  36.9 0.7 copy-done.3
  37.5 0.0 copy-start.2
  37.5 0.0 copy-start.4
  37.5 0.0 copy-start.5
  37.6 6.9 %row_seen.1.seen_hbm = f32[2400,512]{1,0:T(8,128)} custom-call(s32[16,128]{1,0:T(8,128)S(1)} %copy-done.3, s32[1,2048]{1,0:T(1,128)} %pairs_ref.3, s32[1,2048]{1,0:T(1,128)} %get-tuple-element.15.row_ref, bf16[768,384]{1,0:T(8,128)(2,1)} %waves.1.after_ref), custom_call_target="tpu_custom_call" | custom-call | flops 5033164800 | bytes 4915200 | tf_op jit(solution)/shard_map/row_seen/pallas_call | solution.py:460
  44.5 3.1 %all-to-all-done.1 = bf16[16,48,384]{2,1,0:T(8,128)(2,1)S(1)} async-done(((bf16[16,48,384]{2,1,0:T(8,128)(2,1)}), bf16[16,48,384]{2,1,0:T(8,128)(2,1)S(1)}, u32[]{:S(2)}, u32[]{:S(2)}) %all-to-all-start.1) | async-done | bytes 589856 | tf_op jit(solution)/shard_map/all_to_all | solution.py:655
  47.6 0.0 copy-done.2
  47.6 0.0 copy-done.4
  47.6 0.0 copy-done.5
  47.6 0.0 copy-start
  47.6 17.3 %network.1 = (f32[2304,128]{1,0:T(8,128)}, bf16[768,384]{1,0:T(8,128)(2,1)}) custom-call(s32[16,128]{1,0:T(8,128)S(1)} %copy-done.4, bf16[768,384]{1,0:T(8,128)(2,1)S(1)} %bitcast.16, bf16[2304,128]{1,0:T(8,128)(2,1)} %bitcast.23, f32[16,256]{1,0:T(8,128)} %get-tuple-element.13.rank_ref, f32[2400,512]{1,0:T(8,128)} %get-tuple-element.14.sum_hbm, ...), custom_call_target="tpu_custom_call" | custom-call | tf_op jit(solution)/shard_map/network/pallas_call | solution.py:618
  64.9 15.7 %all_to_all.44 = bf16[16,48,384]{2,1,0:T(8,128)(2,1)S(1)} all-to-all(bf16[16,48,384]{2,1,0:T(8,128)(2,1)} %bitcast.22), channel_id=1, replica_groups=mesh['lat'=8,'lev'=16] {'lev'}, dimensions={0} | all-to-all | bytes 1179648 | tf_op jit(solution)/shard_map/all_to_all | solution.py:655
  80.7 1.4 %waves_adjoint.1 = bf16[384,512]{1,0:T(8,128)(2,1)} custom-call(bf16[768,384]{1,0:T(8,128)(2,1)S(1)} %bitcast.15, bf16[768,512]{1,0:T(8,128)(2,1)S(1)} %copy-done.1), custom_call_target="tpu_custom_call" | custom-call | tf_op jit(solution)/shard_map/waves_adjoint/pallas_call | solution.py:318
  82.1 14.6 %all_to_all.45 = bf16[8,48,512]{2,1,0:T(8,128)(2,1)S(1)} all-to-all(bf16[8,48,512]{2,1,0:T(8,128)(2,1)} %bitcast.21), channel_id=1, replica_groups=mesh['lat'=8,'lev'=16] {'lat'}, dimensions={0} | all-to-all | bytes 786432 | tf_op jit(solution)/shard_map/all_to_all | solution.py:655
  96.6 0.0 copy-done
  96.6 2.9 %legendre_adjoint.1 = f32[512,256]{1,0:T(8,128)} custom-call(bf16[32,256,256]{2,1,0:T(8,128)(2,1)S(1)} %copy-done, bf16[384,512]{1,0:T(8,128)(2,1)S(1)} %bitcast.18), custom_call_target="tpu_custom_call" | custom-call | tf_op jit(solution)/shard_map/legendre_adjoint/pallas_call | solution.py:261
Async XLA Ops:
  12.6 14.9 %all-to-all-start = ((bf16[8,48,512]{2,1,0:T(8,128)(2,1)}), bf16[8,48,512]{2,1,0:T(8,128)(2,1)S(1)}, u32[]{:S(2)}, u32[]{:S(2)}) async-start(bf16[8,48,512]{2,1,0:T(8,128)(2,1)} %bitcast.26), calls=%async_computation | async-start | bytes 786432 | tf_op jit(solution)/shard_map/all_to_all | solution.py:655
  19.0 8.5 %copy-start.1 = (bf16[768,512]{1,0:T(8,128)(2,1)S(1)}, bf16[768,512]{1,0:T(8,128)(2,1)}, u32[]{:S(2)}) copy-start(bf16[768,512]{1,0:T(8,128)(2,1)} %constant.20.table_ref) | copy-start | bytes 2359300
  29.1 18.5 %all-to-all-start.1 = ((bf16[16,48,384]{2,1,0:T(8,128)(2,1)}), bf16[16,48,384]{2,1,0:T(8,128)(2,1)S(1)}, u32[]{:S(2)}, u32[]{:S(2)}) async-start(bf16[16,48,384]{2,1,0:T(8,128)(2,1)} %bitcast.20), calls=%async_computation.1 | async-start | bytes 1179648 | tf_op jit(solution)/shard_map/all_to_all | solution.py:655
  36.8 0.7 copy-start.3
  37.5 10.1 %copy-start.2 = (bf16[1024,1024]{1,0:T(8,128)(2,1)S(1)}, bf16[1024,1024]{1,0:T(8,128)(2,1)}, u32[]{:S(2)}) copy-start(bf16[1024,1024]{1,0:T(8,128)(2,1)} %w_mid.1) | copy-start | bytes 6291460
  37.5 10.1 %copy-start.4 = (s32[16,128]{1,0:T(8,128)S(1)}, s32[16,128]{1,0:T(8,128)}, u32[]{:S(2)}) copy-start(s32[16,128]{1,0:T(8,128)} %get-tuple-element.12.after_ref.first_ref) | copy-start | bytes 24580
  37.5 10.1 %copy-start.5 = (f32[512]{0:T(512)S(1)}, f32[512]{0:T(512)}, u32[]{:S(2)}) copy-start(f32[512]{0:T(512)} %param.19) | copy-start | bytes 6148
  47.6 49.0 %copy-start = (bf16[32,256,256]{2,1,0:T(8,128)(2,1)S(1)}, bf16[32,256,256]{2,1,0:T(8,128)(2,1)}, u32[]{:S(2)}) copy-start(bf16[32,256,256]{2,1,0:T(8,128)(2,1)} %get-tuple-element.10.p_ref) | copy-start | bytes 12582916

commit v3 on v2

--- a/solution.py
+++ b/solution.py
@@ -27,6 +27,8 @@
 CHAN = 512
 JL = CLAT * LL
 KM = 2 * M
+M_PITCH = ML + 8
+L_PITCH = 2 * ML + 8
 ROWS = 2 * LL * ML
 
 RESCALE_TOP = 2.0**30
@@ -98,7 +100,10 @@
     @pl.when(step == 0)
     def _():
         for h in (0, 1):
-            halves[h] = spec_ref[:, h * LANES : (h + 1) * LANES]
+            for k in range(2 * LL):
+                halves[h, k * M_PITCH : k * M_PITCH + ML, :] = spec_ref[
+                    k * ML : (k + 1) * ML, h * LANES : (h + 1) * LANES
+                ]
         m0 = lat_ref[0] * ML
         sub = lax.broadcasted_iota(jnp.int32, (8, LANES), 0)
         mf = [(sub + (m0 + 8 * g)).astype(f32) for g in groups]
@@ -132,7 +137,7 @@
             for k in range(8):
                 n2 = nf * nf
                 inv = 1.0 / jnp.maximum(4.0 * n2 - 1.0, 1.0)
-                at = pl.multiple_of((i * 8 + k) * ML, ML)
+                at = pl.multiple_of((i * 8 + k) * M_PITCH, 8)
                 new = []
                 eps = []
                 for g in groups:
@@ -160,10 +165,10 @@
     for k in range(M_STEP):
         m = step * M_STEP + k
         p_m = jnp.concatenate(
-            [table[h, pl.ds(m, N, stride=ML), :].astype(bf16) for h in (0, 1)], axis=1
+            [table[h, pl.ds(m, N, stride=M_PITCH), :].astype(bf16) for h in (0, 1)], axis=1
         )
         p_ref[k] = p_m
-        s = jnp.concatenate([halves[h, pl.ds(m, 2 * LL, stride=ML), :] for h in (0, 1)], axis=1)
+        s = jnp.concatenate([halves[h, pl.ds(m, 2 * LL, stride=M_PITCH), :] for h in (0, 1)], axis=1)
         s = jnp.concatenate([s, s * (alternate if k % 2 == 0 else -alternate)], axis=0)
         high = s.astype(bf16)
         low = (s - high.astype(f32)).astype(bf16)
@@ -173,7 +178,7 @@
             for c in (0, 1):
                 first = (hemi * 2 + c) * LL
                 for h in (0, 1):
-                    waves[hemi, h, pl.ds(c * ML + m, LL, stride=2 * ML), :] = out[
+                    waves[hemi, h, pl.ds(c * ML + m, LL, stride=L_PITCH), :] = out[
                         first : first + LL, h * LANES : (h + 1) * LANES
                     ]
 
@@ -183,7 +188,19 @@
         col = lax.broadcasted_iota(jnp.int32, (HALF, 256), 1)
         for hemi in (0, 1):
             pick = jnp.where(col == (row if hemi == 0 else HALF - 1 - row), 1.0, 0.0).astype(bf16)
-            values = jnp.concatenate([waves[hemi, h].astype(bf16) for h in (0, 1)], axis=1)
+            values = jnp.concatenate(
+                [
+                    jnp.concatenate(
+                        [
+                            waves[hemi, h, l * L_PITCH : l * L_PITCH + 2 * ML, :].astype(bf16)
+                            for h in (0, 1)
+                        ],
+                        axis=1,
+                    )
+                    for l in range(LL)
+                ],
+                axis=0,
+            )
             four_ref[hemi * HALF : (hemi + 1) * HALF, :] = dot_nt(pick, values).astype(bf16)
 
 
@@ -198,17 +215,17 @@
             in_specs=[whole((8, 256)), whole((M, LANES)), whole((ROWS, N))],
             out_specs=[
                 pl.BlockSpec((M_STEP, N, 256), lambda i, *_: (i, 0, 0)),
-                whole((NLAT, ROWS)),
+                VMEM_SPEC,
             ],
             scratch_shapes=[
-                pltpu.VMEM((2, N * ML, LANES), f32),
-                pltpu.VMEM((2, 2, ROWS, LANES), f32),
-                pltpu.VMEM((2, ROWS, LANES), f32),
+                pltpu.VMEM((2, N * M_PITCH, LANES), f32),
+                pltpu.VMEM((2, 2, LL * L_PITCH, LANES), f32),
+                pltpu.VMEM((2, 2 * LL * M_PITCH, LANES), f32),
             ],
         ),
         out_shape=[
             pltpu.HBM((ML, N, 256), bf16),
-            pltpu.HBM((NLAT, ROWS), bf16),
+            pltpu.VMEM((NLAT, ROWS), bf16),
         ],
         compiler_params=params(18),
         name="legendre",
@@ -228,7 +245,10 @@
         for part, pick in ((0, north + south), (1, north - south)):
             value = dot_tn(rows_ref[...], pick.astype(bf16))
             for h in (0, 1):
-                folded[part, h] = value[:, h * LANES : (h + 1) * LANES]
+                for l in range(LL):
+                    folded[part, h, l * L_PITCH : l * L_PITCH + 2 * ML, :] = value[
+                        l * 2 * ML : (l + 1) * 2 * ML, h * LANES : (h + 1) * LANES
+                    ]
 
     lane = lax.broadcasted_iota(jnp.int32, (2 * LL, N), 1)
     for k in range(ADJOINT_STEP):
@@ -239,7 +259,7 @@
                 pieces.append(
                     jnp.concatenate(
                         [
-                            folded[part, h, pl.ds(c * ML + m, LL, stride=2 * ML), :]
+                            folded[part, h, pl.ds(c * ML + m, LL, stride=L_PITCH), :]
                             for h in (0, 1)
                         ],
                         axis=1,
@@ -248,12 +268,15 @@
         value = dot_nt(jnp.concatenate(pieces, axis=0).astype(bf16), p_ref[m])
         picked = jnp.where(lane % 2 == k % 2, value[: 2 * LL], value[2 * LL :])
         for h in (0, 1):
-            held[h, pl.ds(m, 2 * LL, stride=ML), :] = picked[:, h * LANES : (h + 1) * LANES]
+            held[h, pl.ds(m, 2 * LL, stride=M_PITCH), :] = picked[:, h * LANES : (h + 1) * LANES]
 
     @pl.when(step == pl.num_programs(0) - 1)
     def _():
         for h in (0, 1):
-            out_ref[:, h * LANES : (h + 1) * LANES] = held[h]
+            for k in range(2 * LL):
+                out_ref[k * ML : (k + 1) * ML, h * LANES : (h + 1) * LANES] = held[
+                    h, k * M_PITCH : k * M_PITCH + ML, :
+                ]
 
 
 def legendre_adjoint(table, rows):
@@ -267,8 +290,8 @@
         ],
         out_specs=whole((ROWS, N)),
         scratch_shapes=[
-            pltpu.VMEM((2, 2, ROWS, LANES), f32),
-            pltpu.VMEM((2, ROWS, LANES), f32),
+            pltpu.VMEM((2, 2, LL * L_PITCH, LANES), f32),
+            pltpu.VMEM((2, 2 * LL * M_PITCH, LANES), f32),
         ],
         out_shape=jax.ShapeDtypeStruct((ROWS, N), f32),
         compiler_params=params(12),
@@ -277,8 +300,9 @@
     return out.reshape(2, LL, ML, N)
 
 
-def waves_kernel(rows_ref, table_ref, after_ref, out_ref, held):
+def waves_kernel(rows_ref, table_ref, after_ref, out_ref, token_ref, held):
     del after_ref
+    token_ref[...] = jnp.zeros_like(token_ref)
     for pair in range(N_LAT // 2):
         for l in range(LL):
             pieces = [
@@ -294,7 +318,8 @@
     return pl.pallas_call(
         waves_kernel,
         in_specs=[VMEM_SPEC, VMEM_SPEC, pl.BlockSpec(memory_space=pl.ANY)],
-        out_shape=pltpu.HBM((NLON, JL), bf16),
+        out_shape=[pltpu.VMEM((NLON, JL), bf16), pltpu.HBM((8, LANES), f32)],
+        out_specs=[VMEM_SPEC, VMEM_SPEC],
         scratch_shapes=[pltpu.VMEM((N_LAT // 2, JL, LANES), f32)],
         compiler_params=params(12),
         name="waves",
@@ -318,7 +343,8 @@
     return pl.pallas_call(
         waves_adjoint_kernel,
         in_specs=[VMEM_SPEC, VMEM_SPEC],
-        out_shape=pltpu.HBM((NLAT, ROWS), bf16),
+        out_shape=pltpu.VMEM((NLAT, ROWS), bf16),
+        out_specs=VMEM_SPEC,
         scratch_shapes=[pltpu.VMEM((N_LAT // 2, JL, LANES), f32)],
         compiler_params=params(12),
         name="waves_adjoint",
@@ -472,11 +498,12 @@
         compiler_params=params(24),
         cost_estimate=ROW_COST,
         name="row_seen",
-    )(first, in_hbm(pairs), in_hbm(row), in_hbm(after))
+    )(in_hbm(first), in_hbm(pairs), in_hbm(row), in_hbm(after))
 
 
 J_STEP = 16
 X_ROWS = 16
+PART = J_STEP * CLON
 
 
 def silu_and_slope(v):
@@ -504,23 +531,27 @@
 def network_kernel(
     first_ref,
     inc_ref,
-    back_ref,
+    back_hbm,
     rank_ref,
     sum_hbm,
     seen_hbm,
     chan_ref,
-    w_in,
+    w_in_hbm,
     w_mid,
-    w_out,
-    grad_ref,
+    w_out_hbm,
+    grad_hbm,
     send_ref,
     state,
     packed,
     packed_grad,
     w_twice,
+    w_last,
+    back_buf,
+    grads,
     sum_buf,
     seen_buf,
     sems,
+    part_sems,
 ):
     total = first_ref[GROUPS, 0]
     tiles = (total + (TILE - 1)) // TILE
@@ -532,12 +563,24 @@
             pltpu.make_async_copy(seen_hbm.at[r, :], seen_buf.at[slot], sems.at[1, slot]),
         )
 
+    def part_copy(k, src, dst, jc):
+        r = pl.ds(pl.multiple_of(jc * PART, PART), PART)
+        return pltpu.make_async_copy(src.at[r, :], dst.at[r, :], part_sems.at[k, jc])
+
+    for jc in range(CLAT // J_STEP):
+        part_copy(0, back_hbm, back_buf, jc).start()
+    weights = [
+        pltpu.make_async_copy(w_in_hbm, w_twice.at[pl.ds(0, LEV), :], part_sems.at[2, 0]),
+        pltpu.make_async_copy(w_in_hbm, w_twice.at[pl.ds(LEV, LEV), :], part_sems.at[2, 1]),
+        pltpu.make_async_copy(w_out_hbm, w_last, part_sems.at[2, 2]),
+    ]
+    for fetch in weights:
+        fetch.start()
     for fetch in fetches(0, 0):
         fetch.start()
-    w_twice[:LEV] = w_in[...]
-    w_twice[LEV:] = w_in[...]
 
     def to_state(jc, _):
+        part_copy(0, back_hbm, back_buf, jc).wait()
         lanes = pl.ds(pl.multiple_of(jc * LANES, LANES), LANES)
         for part in range(CLON // X_ROWS):
             x0 = part * X_ROWS
@@ -548,7 +591,7 @@
             v = swap_blocks(v)
             for j in range(J_STEP):
                 r = pl.ds(pl.multiple_of((jc * J_STEP + j) * CLON + x0, 16), X_ROWS)
-                grid_state = back_ref[r, :].astype(f32) + v[j]
+                grid_state = back_buf[r, :].astype(f32) + v[j]
                 high = grid_state.astype(bf16)
                 state[r, :LEV] = high
                 state[r, LEV:] = (grid_state - high.astype(f32)).astype(bf16)
@@ -567,6 +610,9 @@
         packed[rows, :] = dot_nn(pick, state[cells, :])
     packed[pl.ds(pl.multiple_of(total, 8), TILE), :] = jnp.zeros((TILE, 2 * LEV), f32)
 
+    for fetch in weights:
+        fetch.wait()
+
     def one_tile(t, _):
         slot = lax.rem(t, 2)
         for fetch in fetches(t, slot):
@@ -580,11 +626,11 @@
         r = pl.ds(pl.multiple_of(t * TILE, 8), TILE)
         act1, slope1 = silu_and_slope(dot_nn(packed[r, :].astype(bf16), w_twice[...]))
         act2, slope2 = silu_and_slope(dot_nn(act1.astype(bf16), w_mid[...]))
-        evolved = dot_nn(act2.astype(bf16), w_out[...])
+        evolved = dot_nn(act2.astype(bf16), w_last[...])
         misfit = (chan_ref[...] * (seen_buf[slot] * evolved - sum_buf[slot])).astype(bf16)
-        back2 = (dot_nt(misfit, w_out[...]) * slope2).astype(bf16)
+        back2 = (dot_nt(misfit, w_last[...]) * slope2).astype(bf16)
         back1 = (dot_nt(back2, w_mid[...]) * slope1).astype(bf16)
-        packed_grad[r, :] = dot_nt(back1, w_in[...])
+        packed_grad[r, :] = dot_nt(back1, w_twice[:LEV])
         return 0
 
     lax.fori_loop(0, tiles, one_tile, 0)
@@ -595,14 +641,16 @@
         high = value.astype(bf16)
         low = (value - high.astype(f32)).astype(bf16)
         value = dot_tn(pick, jnp.concatenate([high, low], axis=1))
-        grad_ref[cells, :] = value[:, :LEV] + value[:, LEV:]
+        grads[cells, :] = value[:, :LEV] + value[:, LEV:]
+        if (g + 1) * GROUP % PART == 0:
+            part_copy(1, grads, grad_hbm, g * GROUP // PART).start()
 
     def to_send(jc, _):
         lanes = pl.ds(pl.multiple_of(jc * LANES, LANES), LANES)
         for part in range(CLON // X_ROWS):
             x0 = part * X_ROWS
             v = [
-                grad_ref[pl.ds(pl.multiple_of((jc * J_STEP + j) * CLON + x0, 16), X_ROWS), :]
+                grads[pl.ds(pl.multiple_of((jc * J_STEP + j) * CLON + x0, 16), X_ROWS), :]
                 for j in range(J_STEP)
             ]
             v = swap_blocks(v)
@@ -611,33 +659,48 @@
         return 0
 
     lax.fori_loop(0, CLAT // J_STEP, to_send, 0)
+    for jc in range(CLAT // J_STEP):
+        part_copy(1, grads, grad_hbm, jc).wait()
 
 
 def network(first, inc, background, rank, sums, seen, channel_weight, w_in, w_mid, w_out):
     anywhere = pl.BlockSpec(memory_space=pl.ANY)
     grad, send = pl.pallas_call(
         network_kernel,
-        in_specs=[pl.BlockSpec(memory_space=pltpu.SMEM), VMEM_SPEC, VMEM_SPEC, VMEM_SPEC]
-        + [anywhere] * 2
-        + [VMEM_SPEC] * 4,
-        out_specs=[VMEM_SPEC, VMEM_SPEC],
+        in_specs=[
+            pl.BlockSpec(memory_space=pltpu.SMEM),
+            VMEM_SPEC,
+            anywhere,
+            VMEM_SPEC,
+            anywhere,
+            anywhere,
+            VMEM_SPEC,
+            anywhere,
+            VMEM_SPEC,
+            anywhere,
+        ],
+        out_specs=[anywhere, VMEM_SPEC],
         out_shape=[
-            jax.ShapeDtypeStruct((CELLS, LEV), f32),
-            pltpu.HBM((NLON, JL), bf16),
+            pltpu.HBM((CELLS, LEV), f32),
+            pltpu.VMEM((NLON, JL), bf16),
         ],
         scratch_shapes=[
             pltpu.VMEM((CELLS, 2 * LEV), bf16),
             pltpu.VMEM((MAX_ROWS + GROUP, 2 * LEV), f32),
             pltpu.VMEM((MAX_ROWS + GROUP, LEV), f32),
             pltpu.VMEM((2 * LEV, w_in.shape[1]), bf16),
+            pltpu.VMEM(w_out.shape, bf16),
+            pltpu.VMEM((CELLS, LEV), bf16),
+            pltpu.VMEM((CELLS, LEV), f32),
             pltpu.VMEM((2, TILE, CHAN), f32),
             pltpu.VMEM((2, TILE, CHAN), f32),
             pltpu.SemaphoreType.DMA((2, 2)),
+            pltpu.SemaphoreType.DMA((3, 3)),
         ],
         compiler_params=params(30),
         name="network",
     )(
-        first,
+        in_hbm(first),
         inc,
         in_hbm(background),
         in_hbm(rank),
@@ -670,9 +733,9 @@
     table = on_chip(wave_table())
     lat_index = lax.axis_index("lat").astype(jnp.int32).reshape(1)
     legendre, fourier = legendre_transform(lat_index, spectral)
-    sums, row, rank, first = row_sums(counts, columns, used_pairs, radiances[0], fourier)
-    waves = waves_to_grid(exchange(fourier, "lat"), table, first)
-    seen = row_seen(first, used_pairs, row, waves)
+    sums, row, rank, first = row_sums(counts, columns, used_pairs, radiances[0], legendre)
+    waves, token = waves_to_grid(exchange(fourier, "lat"), table, first)
+    seen = row_seen(first, used_pairs, row, token)
     increment = exchange(waves, "lev")
     grid_grad, send = network(
         first,

time: 101 us -> 96.2 us (0.952)
  Pallas kernels: 50.6 us -> 46 us
    pallas_call x1, Pallas kernels: 11.9 us -> 8.64 us  [legendre_transform(): pl.pallas_call(legendre_kernel, grid_spec=pltpu.PrefetchScalarGridSpec(nu...]
  transfers between devices with their start and end apart: 2 -> 2, of which waited for: 1 -> 1; matrix products, arithmetic and copies ran while one was open for 0% -> 0% of each run, Pallas kernels for 15% -> 16%
where the time goes in v3:
time: 96.2 us; the launch traced here: 95.6 us
  Pallas kernels  46 us (48%)
  blocking collectives  30.7 us (32%)
  starting transfers between devices  13.6 us (14%)
  waiting for transfers between devices  4.05 us (4%)
  between operations  1.34 us (1%)
    all_to_all x2, blocking collectives, exchange(): lax.all_to_all(rows, axis, split_axis=0, concat_axis=0, tiled=True)  30.7 us
    pallas_call x1, Pallas kernels, network(): pl.pallas_call(network_kernel, in_specs=[pl.BlockSpec(memory_space=pltpu....  17 us
    all_to_all x2, starting transfers between devices, exchange(): lax.all_to_all(rows, axis, split_axis=0, concat_axis=0, tiled=True)  13.6 us
    pallas_call x1, Pallas kernels, legendre_transform(): pl.pallas_call(legendre_kernel, grid_spec=pltpu.PrefetchScalarGridSpec(nu...  8.64 us
    pallas_call x1, Pallas kernels, row_sums(): pl.pallas_call(sums_kernel, grid_spec=pltpu.PrefetchScalarGridSpec(num_sc...  8.47 us
    pallas_call x1, Pallas kernels, row_seen(): pl.pallas_call(seen_kernel, grid=(ROW_TILES,), in_specs=[pl.BlockSpec(mem...  7 us
    all_to_all x2, waiting for transfers between devices, exchange(): lax.all_to_all(rows, axis, split_axis=0, concat_axis=0, tiled=True)  4.05 us
    pallas_call x1, Pallas kernels, legendre_adjoint(): pl.pallas_call(adjoint_kernel, grid=(ML // ADJOINT_STEP,), in_specs=[VMEM...  2.68 us
  transfers between devices with their start and end apart: 2, of which 1 were waited for; matrix products, arithmetic and copies ran while one was open for 0% of the time, Pallas kernels for 16%

profile of v3, /device:TPU:1, one launch (start us, length us, event | category | flops | bytes accessed | tf_op | source)
XLA Modules:
  0.0 95.6 jit_solution(1629152840127974485)
XLA Ops:
  0.6 8.6 %legendre.1 = (bf16[32,256,256]{2,1,0:T(8,128)(2,1)}, bf16[384,512]{1,0:T(8,128)(2,1)}) custom-call(s32[1]{0:T(128)} %bitcast.lat_ref, f32[8,256]{1,0:T(8,128)} %constant.13.clone.geo_ref, f32[256,128]{1,0:T(8,128)} %constant.14.clone.norm_ref, f32[512,256]{1,0:T(8,128)} %bitcast.24), custom_call_target="tpu_custom_call" | custom-call | tf_op jit(solution)/shard_map/legendre/pallas_call | solution.py:210
  9.3 5.8 %all-to-all-start = ((bf16[8,48,512]{2,1,0:T(8,128)(2,1)}), bf16[8,48,512]{2,1,0:T(8,128)(2,1)S(1)}, u32[]{:S(2)}, u32[]{:S(2)}) async-start(bf16[8,48,512]{2,1,0:T(8,128)(2,1)} %bitcast.3), calls=%async_computation | async-start | bytes 786432 | tf_op jit(solution)/shard_map/all_to_all | solution.py:718
  15.7 0.0 copy-start.1
  15.7 8.5 %row_sums.1 = (f32[2400,512]{1,0:T(8,128)}, s32[1,2048]{1,0:T(1,128)}, f32[16,256]{1,0:T(8,128)}, s32[16,128]{1,0:T(8,128)}) custom-call(s32[1]{0:T(128)S(6)} %copy.15.count_ref, s32[1,2048]{1,0:T(1,128)} %columns_ref.1, s32[1,2048]{1,0:T(1,128)} %pairs_ref.3, bf16[2048,512]{1,0:T(8,128)(2,1)} %bitcast.25, ...), custom_call_target="tpu_custom_call" | custom-call | flops 5033164800 | bytes 4915200 | tf_op jit(solution)/shard_map/row_sums/pallas_call | solution.py:453
  24.2 0.0 all-to-all-done
  24.2 0.0 copy-done.1
  24.2 1.5 %waves.1 = (bf16[768,384]{1,0:T(8,128)(2,1)}, f32[8,128]{1,0:T(8,128)}) custom-call(bf16[384,512]{1,0:T(8,128)(2,1)S(1)} %bitcast.19, bf16[768,512]{1,0:T(8,128)(2,1)S(1)} %copy-done.1, s32[16,128]{1,0:T(8,128)} %get-tuple-element.13.after_ref.first_ref), custom_call_target="tpu_custom_call" | custom-call | tf_op jit(solution)/shard_map/waves/pallas_call | solution.py:318
  25.7 7.8 %all-to-all-start.1 = ((bf16[16,48,384]{2,1,0:T(8,128)(2,1)}), bf16[16,48,384]{2,1,0:T(8,128)(2,1)S(1)}, u32[]{:S(2)}, u32[]{:S(2)}) async-start(bf16[16,48,384]{2,1,0:T(8,128)(2,1)} %bitcast.5), calls=%async_computation.1 | async-start | bytes 1179648 | tf_op jit(solution)/shard_map/all_to_all | solution.py:718
  33.5 0.0 copy-start.2
  33.5 0.0 copy-start.3
  33.5 7.0 %row_seen.1.seen_hbm = f32[2400,512]{1,0:T(8,128)} custom-call(s32[16,128]{1,0:T(8,128)} %get-tuple-element.13.after_ref.first_ref, s32[1,2048]{1,0:T(1,128)} %pairs_ref.3, s32[1,2048]{1,0:T(1,128)} %get-tuple-element.18.row_ref, f32[8,128]{1,0:T(8,128)} %get-tuple-element.19.after_ref), custom_call_target="tpu_custom_call" | custom-call | flops 5033164800 | bytes 4915200 | tf_op jit(solution)/shard_map/row_seen/pallas_call | solution.py:486
  40.6 4.1 %all-to-all-done.1 = bf16[16,48,384]{2,1,0:T(8,128)(2,1)S(1)} async-done(((bf16[16,48,384]{2,1,0:T(8,128)(2,1)}), bf16[16,48,384]{2,1,0:T(8,128)(2,1)S(1)}, u32[]{:S(2)}, u32[]{:S(2)}) %all-to-all-start.1) | async-done | bytes 589856 | tf_op jit(solution)/shard_map/all_to_all | solution.py:718
  44.6 0.0 copy-done.2
  44.6 0.0 copy-done.3
  44.6 0.0 copy-start
  44.6 17.0 %network.1 = (f32[2304,128]{1,0:T(8,128)}, bf16[768,384]{1,0:T(8,128)(2,1)S(1)}) custom-call(s32[16,128]{1,0:T(8,128)} %get-tuple-element.13.after_ref.first_ref, bf16[768,384]{1,0:T(8,128)(2,1)S(1)} %bitcast.16, bf16[2304,128]{1,0:T(8,128)(2,1)} %bitcast.22, f32[16,256]{1,0:T(8,128)} %get-tuple-element.16.rank_ref, f32[2400,512]{1,0:T(8,128)} %get-tuple-element.17.sum_hbm, ...), custom_call_target="tpu_custom_call" | custom-call | tf_op jit(solution)/shard_map/network/pallas_call | solution.py:668
  61.6 18.2 %all_to_all.44 = bf16[16,48,384]{2,1,0:T(8,128)(2,1)S(1)} all-to-all(bf16[16,48,384]{2,1,0:T(8,128)(2,1)S(1)} %bitcast.20), channel_id=1, replica_groups=mesh['lat'=8,'lev'=16] {'lev'}, dimensions={0} | all-to-all | bytes 1179648 | tf_op jit(solution)/shard_map/all_to_all | solution.py:718
  79.8 0.6 waves_adjoint.1
  80.5 12.5 %all_to_all.45 = bf16[8,48,512]{2,1,0:T(8,128)(2,1)S(1)} all-to-all(bf16[8,48,512]{2,1,0:T(8,128)(2,1)S(1)} %bitcast.17), channel_id=1, replica_groups=mesh['lat'=8,'lev'=16] {'lat'}, dimensions={0} | all-to-all | bytes 786432 | tf_op jit(solution)/shard_map/all_to_all | solution.py:718
  93.0 0.0 copy-done
  93.0 2.7 %legendre_adjoint.1 = f32[512,256]{1,0:T(8,128)} custom-call(bf16[32,256,256]{2,1,0:T(8,128)(2,1)S(1)} %copy-done, bf16[384,512]{1,0:T(8,128)(2,1)S(1)} %bitcast.18), custom_call_target="tpu_custom_call" | custom-call | tf_op jit(solution)/shard_map/legendre_adjoint/pallas_call | solution.py:284
Async XLA Ops:
  9.3 14.9 %all-to-all-start = ((bf16[8,48,512]{2,1,0:T(8,128)(2,1)}), bf16[8,48,512]{2,1,0:T(8,128)(2,1)S(1)}, u32[]{:S(2)}, u32[]{:S(2)}) async-start(bf16[8,48,512]{2,1,0:T(8,128)(2,1)} %bitcast.3), calls=%async_computation | async-start | bytes 786432 | tf_op jit(solution)/shard_map/all_to_all | solution.py:718
  15.7 8.5 %copy-start.1 = (bf16[768,512]{1,0:T(8,128)(2,1)S(1)}, bf16[768,512]{1,0:T(8,128)(2,1)}, u32[]{:S(2)}) copy-start(bf16[768,512]{1,0:T(8,128)(2,1)} %constant.20.table_ref) | copy-start | bytes 2359300
  25.7 18.9 %all-to-all-start.1 = ((bf16[16,48,384]{2,1,0:T(8,128)(2,1)}), bf16[16,48,384]{2,1,0:T(8,128)(2,1)S(1)}, u32[]{:S(2)}, u32[]{:S(2)}) async-start(bf16[16,48,384]{2,1,0:T(8,128)(2,1)} %bitcast.5), calls=%async_computation.1 | async-start | bytes 1179648 | tf_op jit(solution)/shard_map/all_to_all | solution.py:718
  33.5 11.1 %copy-start.2 = (bf16[1024,1024]{1,0:T(8,128)(2,1)S(1)}, bf16[1024,1024]{1,0:T(8,128)(2,1)}, u32[]{:S(2)}) copy-start(bf16[1024,1024]{1,0:T(8,128)(2,1)} %w_mid.1) | copy-start | bytes 6291460
  33.5 11.1 %copy-start.3 = (f32[512]{0:T(512)S(1)}, f32[512]{0:T(512)}, u32[]{:S(2)}) copy-start(f32[512]{0:T(512)} %param.19) | copy-start | bytes 6148
  44.6 48.4 %copy-start = (bf16[32,256,256]{2,1,0:T(8,128)(2,1)S(1)}, bf16[32,256,256]{2,1,0:T(8,128)(2,1)}, u32[]{:S(2)}) copy-start(bf16[32,256,256]{2,1,0:T(8,128)(2,1)} %get-tuple-element.12.after_ref.p_ref) | copy-start | bytes 12582916

commit v4 on v3

--- a/solution.py
+++ b/solution.py
@@ -90,144 +90,153 @@
 
 
 M_STEP = 8
-ADJOINT_STEP = 16
-
-
-def legendre_kernel(lat_ref, geo_ref, norm_ref, spec_ref, p_ref, four_ref, table, waves, halves):
-    step = pl.program_id(0)
+ADJOINT_STEP = 32
+
+
+def legendre_kernel(
+    lat_ref, geo_ref, norm_ref, spec_ref, p_hbm, four_ref, table, waves, halves, p_buf, sems
+):
     groups = range(ML // 8)
 
-    @pl.when(step == 0)
-    def _():
-        for h in (0, 1):
-            for k in range(2 * LL):
-                halves[h, k * M_PITCH : k * M_PITCH + ML, :] = spec_ref[
-                    k * ML : (k + 1) * ML, h * LANES : (h + 1) * LANES
-                ]
-        m0 = lat_ref[0] * ML
-        sub = lax.broadcasted_iota(jnp.int32, (8, LANES), 0)
-        mf = [(sub + (m0 + 8 * g)).astype(f32) for g in groups]
-        m2 = [v * v for v in mf]
-        zero = jnp.zeros((8, LANES), f32)
-        x = [jnp.broadcast_to(geo_ref[0:1, h * LANES : (h + 1) * LANES], (8, LANES)) for h in (0, 1)]
-        log_cos = [
-            jnp.broadcast_to(geo_ref[1:2, h * LANES : (h + 1) * LANES], (8, LANES)) for h in (0, 1)
+    for h in (0, 1):
+        for k in range(2 * LL):
+            halves[h, k * M_PITCH : k * M_PITCH + ML, :] = spec_ref[
+                k * ML : (k + 1) * ML, h * LANES : (h + 1) * LANES
+            ]
+    m0 = lat_ref[0] * ML
+    sub = lax.broadcasted_iota(jnp.int32, (8, LANES), 0)
+    mf = [(sub + (m0 + 8 * g)).astype(f32) for g in groups]
+    m2 = [v * v for v in mf]
+    zero = jnp.zeros((8, LANES), f32)
+    x = [jnp.broadcast_to(geo_ref[0:1, h * LANES : (h + 1) * LANES], (8, LANES)) for h in (0, 1)]
+    log_cos = [
+        jnp.broadcast_to(geo_ref[1:2, h * LANES : (h + 1) * LANES], (8, LANES)) for h in (0, 1)
+    ]
+    valid = [
+        jnp.broadcast_to(geo_ref[2:3, h * LANES : (h + 1) * LANES], (8, LANES)) for h in (0, 1)
+    ]
+    logs = [
+        [norm_ref[pl.ds(m0 + 8 * g, 8), :] + mf[g] * log_cos[h] for h in (0, 1)] for g in groups
+    ]
+
+    def block(i, carry):
+        prev, earlier, logs, eps_prev, nf = carry
+        big = [
+            [jnp.maximum(jnp.abs(prev[g][h]), jnp.abs(earlier[g][h])) > RESCALE_TOP for h in (0, 1)]
+            for g in groups
         ]
-        valid = [
-            jnp.broadcast_to(geo_ref[2:3, h * LANES : (h + 1) * LANES], (8, LANES)) for h in (0, 1)
+        shrink = [[jnp.where(big[g][h], RESCALE_BY, 1.0) for h in (0, 1)] for g in groups]
+        prev = [[prev[g][h] * shrink[g][h] for h in (0, 1)] for g in groups]
+        earlier = [[earlier[g][h] * shrink[g][h] for h in (0, 1)] for g in groups]
+        logs = [
+            [jnp.where(big[g][h], logs[g][h] + RESCALE_LOG, logs[g][h]) for h in (0, 1)]
+            for g in groups
         ]
-        logs = [
-            [norm_ref[pl.ds(m0 + 8 * g, 8), :] + mf[g] * log_cos[h] for h in (0, 1)] for g in groups
-        ]
-
-        def block(i, carry):
-            prev, earlier, logs, eps_prev, nf = carry
-            big = [
-                [jnp.maximum(jnp.abs(prev[g][h]), jnp.abs(earlier[g][h])) > RESCALE_TOP for h in (0, 1)]
-                for g in groups
-            ]
-            shrink = [[jnp.where(big[g][h], RESCALE_BY, 1.0) for h in (0, 1)] for g in groups]
-            prev = [[prev[g][h] * shrink[g][h] for h in (0, 1)] for g in groups]
-            earlier = [[earlier[g][h] * shrink[g][h] for h in (0, 1)] for g in groups]
-            logs = [
-                [jnp.where(big[g][h], logs[g][h] + RESCALE_LOG, logs[g][h]) for h in (0, 1)]
-                for g in groups
-            ]
-            scale = [[jnp.exp(logs[g][h]) * valid[h] for h in (0, 1)] for g in groups]
-            for k in range(8):
-                n2 = nf * nf
-                inv = 1.0 / jnp.maximum(4.0 * n2 - 1.0, 1.0)
-                at = pl.multiple_of((i * 8 + k) * M_PITCH, 8)
-                new = []
-                eps = []
-                for g in groups:
-                    t = n2 - m2[g]
-                    q = jnp.maximum(t, 1.0) * inv
-                    a = lax.rsqrt(q)
-                    eps.append(jnp.where(t > 0.0, q * a, 0.0))
-                    diag = nf == mf[g]
-                    row = []
-                    for h in (0, 1):
-                        cur = (x[h] * prev[g][h] - eps_prev[g] * earlier[g][h]) * a
-                        cur = jnp.where(diag, 1.0, cur)
-                        table[h, pl.ds(at + 8 * g, 8), :] = cur * scale[g][h]
-                        row.append(cur)
-                    new.append(row)
-                prev, earlier, eps_prev = new, prev, eps
-                nf = nf + 1.0
-            return prev, earlier, logs, eps_prev, nf
-
-        empty = [[zero, zero] for _ in groups]
-        lax.fori_loop(0, N // 8, block, (empty, empty, logs, [zero for _ in groups], zero))
+        scale = [[jnp.exp(logs[g][h]) * valid[h] for h in (0, 1)] for g in groups]
+        for k in range(8):
+            n2 = nf * nf
+            inv = 1.0 / jnp.maximum(4.0 * n2 - 1.0, 1.0)
+            at = pl.multiple_of((i * 8 + k) * M_PITCH, 8)
+            new = []
+            eps = []
+            for g in groups:
+                t = n2 - m2[g]
+                q = jnp.maximum(t, 1.0) * inv
+                a = lax.rsqrt(q)
+                eps.append(jnp.where(t > 0.0, q * a, 0.0))
+                diag = nf == mf[g]
+                row = []
+                for h in (0, 1):
+                    cur = (x[h] * prev[g][h] - eps_prev[g] * earlier[g][h]) * a
+                    cur = jnp.where(diag, 1.0, cur)
+                    table[h, pl.ds(at + 8 * g, 8), :] = cur * scale[g][h]
+                    row.append(cur)
+                new.append(row)
+            prev, earlier, eps_prev = new, prev, eps
+            nf = nf + 1.0
+        return prev, earlier, logs, eps_prev, nf
+
+    empty = [[zero, zero] for _ in groups]
+    lax.fori_loop(0, N // 8, block, (empty, empty, logs, [zero for _ in groups], zero))
 
     lane = lax.broadcasted_iota(jnp.int32, (1, N), 1)
     alternate = jnp.where(lane % 2 == 0, 1.0, -1.0)
-    for k in range(M_STEP):
-        m = step * M_STEP + k
-        p_m = jnp.concatenate(
-            [table[h, pl.ds(m, N, stride=M_PITCH), :].astype(bf16) for h in (0, 1)], axis=1
+    def store(step):
+        slot = lax.rem(step, 2)
+        m = pl.ds(step * M_STEP, M_STEP)
+        return pltpu.make_async_copy(p_buf.at[slot], p_hbm.at[m], sems.at[slot])
+
+    def transform(step, _):
+        slot = lax.rem(step, 2)
+
+        @pl.when(step >= 2)
+        def _():
+            store(step - 2).wait()
+
+        for k in range(M_STEP):
+            m = step * M_STEP + k
+            p_m = jnp.concatenate(
+                [table[h, pl.ds(m, N, stride=M_PITCH), :].astype(bf16) for h in (0, 1)], axis=1
+            )
+            p_buf[slot, k] = p_m
+            s = jnp.concatenate([halves[h, pl.ds(m, 2 * LL, stride=M_PITCH), :] for h in (0, 1)], axis=1)
+            s = jnp.concatenate([s, s * (alternate if k % 2 == 0 else -alternate)], axis=0)
+            high = s.astype(bf16)
+            low = (s - high.astype(f32)).astype(bf16)
+            out = dot_nn(jnp.concatenate([high, low], axis=0), p_m)
+            out = out[: 4 * LL] + out[4 * LL :]
+            for hemi in (0, 1):
+                for c in (0, 1):
+                    first = (hemi * 2 + c) * LL
+                    for h in (0, 1):
+                        waves[hemi, h, pl.ds(c * ML + m, LL, stride=L_PITCH), :] = out[
+                            first : first + LL, h * LANES : (h + 1) * LANES
+                        ]
+        store(step).start()
+        return 0
+
+    steps = ML // M_STEP
+    lax.fori_loop(0, steps, transform, 0)
+    row = lax.broadcasted_iota(jnp.int32, (HALF, 256), 0)
+    col = lax.broadcasted_iota(jnp.int32, (HALF, 256), 1)
+    for hemi in (0, 1):
+        pick = jnp.where(col == (row if hemi == 0 else HALF - 1 - row), 1.0, 0.0).astype(bf16)
+        values = jnp.concatenate(
+            [
+                jnp.concatenate(
+                    [
+                        waves[hemi, h, l * L_PITCH : l * L_PITCH + 2 * ML, :].astype(bf16)
+                        for h in (0, 1)
+                    ],
+                    axis=1,
+                )
+                for l in range(LL)
+            ],
+            axis=0,
         )
-        p_ref[k] = p_m
-        s = jnp.concatenate([halves[h, pl.ds(m, 2 * LL, stride=M_PITCH), :] for h in (0, 1)], axis=1)
-        s = jnp.concatenate([s, s * (alternate if k % 2 == 0 else -alternate)], axis=0)
-        high = s.astype(bf16)
-        low = (s - high.astype(f32)).astype(bf16)
-        out = dot_nn(jnp.concatenate([high, low], axis=0), p_m)
-        out = out[: 4 * LL] + out[4 * LL :]
-        for hemi in (0, 1):
-            for c in (0, 1):
-                first = (hemi * 2 + c) * LL
-                for h in (0, 1):
-                    waves[hemi, h, pl.ds(c * ML + m, LL, stride=L_PITCH), :] = out[
-                        first : first + LL, h * LANES : (h + 1) * LANES
-                    ]
-
-    @pl.when(step == pl.num_programs(0) - 1)
-    def _():
-        row = lax.broadcasted_iota(jnp.int32, (HALF, 256), 0)
-        col = lax.broadcasted_iota(jnp.int32, (HALF, 256), 1)
-        for hemi in (0, 1):
-            pick = jnp.where(col == (row if hemi == 0 else HALF - 1 - row), 1.0, 0.0).astype(bf16)
-            values = jnp.concatenate(
-                [
-                    jnp.concatenate(
-                        [
-                            waves[hemi, h, l * L_PITCH : l * L_PITCH + 2 * ML, :].astype(bf16)
-                            for h in (0, 1)
-                        ],
-                        axis=1,
-                    )
-                    for l in range(LL)
-                ],
-                axis=0,
-            )
-            four_ref[hemi * HALF : (hemi + 1) * HALF, :] = dot_nt(pick, values).astype(bf16)
+        four_ref[hemi * HALF : (hemi + 1) * HALF, :] = dot_nt(pick, values).astype(bf16)
+    store(steps - 2).wait()
+    store(steps - 1).wait()
 
 
 def legendre_transform(lat_index, spectral):
     geo, norm = geometry()
-    whole = lambda shape: pl.BlockSpec(shape, lambda i, *_: (0,) * len(shape))
     return pl.pallas_call(
         legendre_kernel,
-        grid_spec=pltpu.PrefetchScalarGridSpec(
-            num_scalar_prefetch=1,
-            grid=(ML // M_STEP,),
-            in_specs=[whole((8, 256)), whole((M, LANES)), whole((ROWS, N))],
-            out_specs=[
-                pl.BlockSpec((M_STEP, N, 256), lambda i, *_: (i, 0, 0)),
-                VMEM_SPEC,
-            ],
-            scratch_shapes=[
-                pltpu.VMEM((2, N * M_PITCH, LANES), f32),
-                pltpu.VMEM((2, 2, LL * L_PITCH, LANES), f32),
-                pltpu.VMEM((2, 2 * LL * M_PITCH, LANES), f32),
-            ],
-        ),
+        in_specs=[pl.BlockSpec(memory_space=pltpu.SMEM), VMEM_SPEC, VMEM_SPEC, VMEM_SPEC],
+        out_specs=[pl.BlockSpec(memory_space=pl.ANY), VMEM_SPEC],
+        scratch_shapes=[
+            pltpu.VMEM((2, N * M_PITCH, LANES), f32),
+            pltpu.VMEM((2, 2, LL * L_PITCH, LANES), f32),
+            pltpu.VMEM((2, 2 * LL * M_PITCH, LANES), f32),
+            pltpu.VMEM((2, M_STEP, N, 256), bf16),
+            pltpu.SemaphoreType.DMA((2,)),
+        ],
         out_shape=[
             pltpu.HBM((ML, N, 256), bf16),
             pltpu.VMEM((NLAT, ROWS), bf16),
         ],
-        compiler_params=params(18),
+        compiler_params=params(24),
         name="legendre",
     )(lat_index, in_hbm(jnp.asarray(geo)), in_hbm(jnp.asarray(norm)), in_hbm(spectral.reshape(ROWS, N)))
 
@@ -355,6 +364,7 @@
 GROUPS = CELLS // GROUP
 TILE = 240
 SUM_TILE = 2 * TILE
+QUARTER = CAP // 4
 ROW_TILES = -(-(CAP + 7 * GROUPS) // SUM_TILE)
 MAX_ROWS = ROW_TILES * SUM_TILE
 
@@ -384,17 +394,37 @@
     return row, jnp.where(used > 0.5, rank, -1.0), first
 
 
-def sum_rows(step, total, row_of_slot, masked, sum_ref):
-    @pl.when(step * SUM_TILE < total)
+def write_sums(total, row_of_slot, masked, tile_buf, out_hbm, sems):
+    tiles = (total + (SUM_TILE - 1)) // SUM_TILE
+
+    def store(t):
+        slot = lax.rem(t, 2)
+        r = pl.ds(pl.multiple_of(t * SUM_TILE, 8), SUM_TILE)
+        return pltpu.make_async_copy(tile_buf.at[slot], out_hbm.at[r, :], sems.at[slot])
+
+    def one_tile(t, _):
+        @pl.when(t >= 2)
+        def _():
+            store(t - 2).wait()
+
+        row = lax.broadcasted_iota(jnp.int32, (SUM_TILE, CAP), 0) + t * SUM_TILE
+        hit = jnp.where(row == row_of_slot[...], 1.0, 0.0).astype(bf16)
+        tile_buf[lax.rem(t, 2)] = dot_nn(hit, masked[...])
+        store(t).start()
+        return 0
+
+    lax.fori_loop(0, tiles, one_tile, 0)
+
+    @pl.when(tiles >= 2)
     def _():
-        row = lax.broadcasted_iota(jnp.int32, (SUM_TILE, CAP), 0) + step * SUM_TILE
-        hit = jnp.where(row == row_of_slot, 1.0, 0.0).astype(bf16)
-        sum_ref[...] = dot_nn(hit, masked[...])
-
-
-def active_channels(pairs_ref, value, masked):
+        store(tiles - 2).wait()
+
+    store(tiles - 1).wait()
+
+
+def active_channels(part, pairs_ref, value, masked):
     channel = lax.broadcasted_iota(jnp.int32, (LANES, LANES), 1)
-    for i in range(CAP // LANES):
+    for i in range(part * QUARTER // LANES, (part + 1) * QUARTER // LANES):
         r = slice(i * LANES, (i + 1) * LANES)
         used = jnp.transpose(jnp.broadcast_to(2 * pairs_ref[:, r], (LANES, LANES)))
         for c in range(CHAN // LANES):
@@ -408,39 +438,41 @@
     count_ref,
     columns_ref,
     pairs_ref,
-    obs_ref,
+    obs_hbm,
     after_ref,
-    sum_ref,
+    sum_hbm,
     row_ref,
     rank_ref,
     first_ref,
+    obs,
     masked,
-    total_ref,
+    tile_buf,
+    sems,
+    obs_sems,
 ):
     del after_ref
-    step = pl.program_id(0)
-
-    @pl.when(step == 0)
-    def _():
-        row, rank, first = assign_rows(count_ref[0], columns_ref[...])
-        row_ref[...] = row
-        rank_ref[...] = rank
-        first_ref[...] = first.astype(jnp.int32)
-        total_ref[0] = jnp.max(first).astype(jnp.int32)
-        active_channels(pairs_ref, lambda r, lanes: obs_ref[r, lanes].astype(f32), masked)
-
-    sum_rows(step, total_ref[0], row_ref[...], masked, sum_ref)
-
-
-def seen_kernel(first_ref, pairs_ref, row_ref, after_ref, sum_ref, masked):
+
+    def fetch(part):
+        r = pl.ds(part * QUARTER, QUARTER)
+        return pltpu.make_async_copy(obs_hbm.at[r, :], obs.at[r, :], obs_sems.at[part])
+
+    for part in range(4):
+        fetch(part).start()
+    row, rank, first = assign_rows(count_ref[0], columns_ref[...])
+    row_ref[...] = row
+    rank_ref[...] = rank
+    first_ref[...] = first.astype(jnp.int32)
+    for part in range(4):
+        fetch(part).wait()
+        active_channels(part, pairs_ref, lambda r, lanes: obs[r, lanes].astype(f32), masked)
+    write_sums(jnp.max(first).astype(jnp.int32), row_ref, masked, tile_buf, sum_hbm, sems)
+
+
+def seen_kernel(first_ref, pairs_ref, row_ref, after_ref, sum_hbm, masked, tile_buf, sems):
     del after_ref
-    step = pl.program_id(0)
-
-    @pl.when(step == 0)
-    def _():
-        active_channels(pairs_ref, lambda r, lanes: 1.0, masked)
-
-    sum_rows(step, first_ref[GROUPS, 0], row_ref[...], masked, sum_ref)
+    for part in range(4):
+        active_channels(part, pairs_ref, lambda r, lanes: 1.0, masked)
+    write_sums(first_ref[GROUPS, 0], row_ref, masked, tile_buf, sum_hbm, sems)
 
 
 ROW_COST = pl.CostEstimate(
@@ -448,27 +480,28 @@
 )
 
 
+SUM_SCRATCH = [
+    pltpu.VMEM((CAP, CHAN), bf16),
+    pltpu.VMEM((2, SUM_TILE, CHAN), f32),
+    pltpu.SemaphoreType.DMA((2,)),
+]
+
+
 def row_sums(counts, columns, pairs, obs, after):
-    whole = lambda shape: pl.BlockSpec(shape, lambda i, *_: (0,) * len(shape))
+    anywhere = pl.BlockSpec(memory_space=pl.ANY)
     return pl.pallas_call(
         sums_kernel,
-        grid_spec=pltpu.PrefetchScalarGridSpec(
-            num_scalar_prefetch=1,
-            grid=(ROW_TILES,),
-            in_specs=[
-                whole((1, CAP)),
-                whole((1, CAP)),
-                whole((CAP, CHAN)),
-                pl.BlockSpec(memory_space=pl.ANY),
-            ],
-            out_specs=[
-                pl.BlockSpec((SUM_TILE, CHAN), lambda i, *_: (i, 0)),
-                whole((1, CAP)),
-                whole((16, GROUP)),
-                whole((16, LANES)),
-            ],
-            scratch_shapes=[pltpu.VMEM((CAP, CHAN), bf16), pltpu.SMEM((1,), jnp.int32)],
-        ),
+        in_specs=[
+            pl.BlockSpec(memory_space=pltpu.SMEM),
+            VMEM_SPEC,
+            VMEM_SPEC,
+            anywhere,
+            anywhere,
+        ],
+        out_specs=[anywhere, VMEM_SPEC, VMEM_SPEC, VMEM_SPEC],
+        scratch_shapes=[pltpu.VMEM((CAP, CHAN), bf16)]
+        + SUM_SCRATCH
+        + [pltpu.SemaphoreType.DMA((4,))],
         out_shape=[
             pltpu.HBM((MAX_ROWS, CHAN), f32),
             pltpu.HBM((1, CAP), jnp.int32),
@@ -482,18 +515,12 @@
 
 
 def row_seen(first, pairs, row, after):
-    whole = lambda shape: pl.BlockSpec(shape, lambda i: (0,) * len(shape))
+    anywhere = pl.BlockSpec(memory_space=pl.ANY)
     return pl.pallas_call(
         seen_kernel,
-        grid=(ROW_TILES,),
-        in_specs=[
-            pl.BlockSpec(memory_space=pltpu.SMEM),
-            whole((1, CAP)),
-            whole((1, CAP)),
-            pl.BlockSpec(memory_space=pl.ANY),
-        ],
-        out_specs=pl.BlockSpec((SUM_TILE, CHAN), lambda i: (i, 0)),
-        scratch_shapes=[pltpu.VMEM((CAP, CHAN), bf16)],
+        in_specs=[pl.BlockSpec(memory_space=pltpu.SMEM), VMEM_SPEC, VMEM_SPEC, anywhere],
+        out_specs=anywhere,
+        scratch_shapes=SUM_SCRATCH,
         out_shape=pltpu.HBM((MAX_ROWS, CHAN), f32),
         compiler_params=params(24),
         cost_estimate=ROW_COST,
@@ -542,6 +569,7 @@
     grad_hbm,
     send_ref,
     state,
+    picks,
     packed,
     packed_grad,
     w_twice,
@@ -578,6 +606,10 @@
         fetch.start()
     for fetch in fetches(0, 0):
         fetch.start()
+
+    row = lax.broadcasted_iota(jnp.int32, (GROUP, GROUP), 0).astype(f32)
+    for g in range(GROUPS):
+        picks[g] = jnp.where(row == rank_ref[g : g + 1, :], 1.0, 0.0).astype(bf16)
 
     def to_state(jc, _):
         part_copy(0, back_hbm, back_buf, jc).wait()
@@ -601,9 +633,7 @@
 
     def group_rows(g):
         first = pl.ds(pl.multiple_of(first_ref[g, 0], 8), GROUP)
-        row = lax.broadcasted_iota(jnp.int32, (GROUP, GROUP), 0).astype(f32)
-        pick = jnp.where(row == rank_ref[g : g + 1, :], 1.0, 0.0).astype(bf16)
-        return first, slice(g * GROUP, (g + 1) * GROUP), pick
+        return first, slice(g * GROUP, (g + 1) * GROUP), picks[g]
 
     for g in range(GROUPS):
         rows, cells, pick = group_rows(g)
@@ -686,6 +716,7 @@
         ],
         scratch_shapes=[
             pltpu.VMEM((CELLS, 2 * LEV), bf16),
+            pltpu.VMEM((GROUPS, GROUP, GROUP), bf16),
             pltpu.VMEM((MAX_ROWS + GROUP, 2 * LEV), f32),
             pltpu.VMEM((MAX_ROWS + GROUP, LEV), f32),
             pltpu.VMEM((2 * LEV, w_in.shape[1]), bf16),

time: 96.2 us -> 95.4 us (level)
  Pallas kernels: 46 us -> 30.5 us
  blocking collectives: 30.7 us -> 39.8 us
  waiting for transfers between devices: 4.05 us -> 8.92 us
    all_to_all x2, blocking collectives: 30.7 us -> 39.8 us  [exchange(): lax.all_to_all(rows, axis, split_axis=0, concat_axis=0, tiled=True)]
    pallas_call x1, Pallas kernels: 17 us -> 8.08 us  [network(): pl.pallas_call(network_kernel, in_specs=[pl.BlockSpec(memory_space=pltpu....]
    pallas_call x3, Pallas kernels: 24.1 us -> 17.7 us  [the longest x1 8.68 us: legendre_transform(): pl.pallas_call(legendre_kernel, in_specs=[pl.BlockSpec(memory_space=pltpu...]
    all_to_all x2, waiting for transfers between devices: 4.05 us -> 8.92 us  [exchange(): lax.all_to_all(rows, axis, split_axis=0, concat_axis=0, tiled=True)]
  transfers between devices with their start and end apart: 2 -> 2, of which waited for: 1 -> 2; matrix products, arithmetic and copies ran while one was open for 0% -> 0% of each run, Pallas kernels for 16% -> 10%
where the time goes in v4:
time: 95.4 us; the launch traced here: 94.7 us
  blocking collectives  39.8 us (42%)
  Pallas kernels  30.5 us (32%)
  starting transfers between devices  14.1 us (15%)
  waiting for transfers between devices  8.92 us (9%)
  between operations  1.36 us (1%)
    all_to_all x2, blocking collectives, exchange(): lax.all_to_all(rows, axis, split_axis=0, concat_axis=0, tiled=True)  39.8 us
    all_to_all x2, starting transfers between devices, exchange(): lax.all_to_all(rows, axis, split_axis=0, concat_axis=0, tiled=True)  14.1 us
    all_to_all x2, waiting for transfers between devices, exchange(): lax.all_to_all(rows, axis, split_axis=0, concat_axis=0, tiled=True)  8.92 us
    pallas_call x1, Pallas kernels, legendre_transform(): pl.pallas_call(legendre_kernel, in_specs=[pl.BlockSpec(memory_space=pltpu...  8.68 us
    pallas_call x1, Pallas kernels, network(): pl.pallas_call(network_kernel, in_specs=[pl.BlockSpec(memory_space=pltpu....  8.08 us
    pallas_call x1, Pallas kernels, row_sums(): pl.pallas_call(sums_kernel, in_specs=[pl.BlockSpec(memory_space=pltpu.SME...  5.47 us
    pallas_call x1, Pallas kernels, row_seen(): pl.pallas_call(seen_kernel, in_specs=[pl.BlockSpec(memory_space=pltpu.SME...  3.6 us
    pallas_call x1, Pallas kernels, legendre_adjoint(): pl.pallas_call(adjoint_kernel, grid=(ML // ADJOINT_STEP,), in_specs=[VMEM...  2.43 us
  transfers between devices with their start and end apart: 2, of which 2 were waited for; matrix products, arithmetic and copies ran while one was open for 0% of the time, Pallas kernels for 10%

profile of v4, /device:TPU:1, one launch (start us, length us, event | category | flops | bytes accessed | tf_op | source)
XLA Modules:
  0.0 94.7 jit_solution(10693965339299795454)
XLA Ops:
  0.6 8.7 %legendre.1 = (bf16[32,256,256]{2,1,0:T(8,128)(2,1)}, bf16[384,512]{1,0:T(8,128)(2,1)}) custom-call(s32[1]{0:T(128)} %bitcast.lat_ref, f32[8,256]{1,0:T(8,128)} %constant.13.clone.geo_ref, f32[256,128]{1,0:T(8,128)} %constant.14.clone.norm_ref, f32[512,256]{1,0:T(8,128)} %bitcast.24), custom_call_target="tpu_custom_call" | custom-call | tf_op jit(solution)/shard_map/legendre/pallas_call | solution.py:224
  9.3 5.8 %all-to-all-start = ((bf16[8,48,512]{2,1,0:T(8,128)(2,1)}), bf16[8,48,512]{2,1,0:T(8,128)(2,1)S(1)}, u32[]{:S(2)}, u32[]{:S(2)}) async-start(bf16[8,48,512]{2,1,0:T(8,128)(2,1)} %bitcast.3), calls=%async_computation | async-start | bytes 786432 | tf_op jit(solution)/shard_map/all_to_all | solution.py:749
  15.8 0.0 copy-start.1
  15.8 5.5 %row_sums.1 = (f32[2400,512]{1,0:T(8,128)}, s32[1,2048]{1,0:T(1,128)}, f32[16,256]{1,0:T(8,128)}, s32[16,128]{1,0:T(8,128)}) custom-call(s32[1]{0:T(128)S(6)} %copy.15.count_ref, s32[1,2048]{1,0:T(1,128)} %columns_ref.1, s32[1,2048]{1,0:T(1,128)} %pairs_ref.3, bf16[2048,512]{1,0:T(8,128)(2,1)} %bitcast.25, ...), custom_call_target="tpu_custom_call" | custom-call | flops 5033164800 | bytes 4915200 | tf_op jit(solution)/shard_map/row_sums/pallas_call | solution.py:492
  21.3 1.6 %all-to-all-done = bf16[8,48,512]{2,1,0:T(8,128)(2,1)S(1)} async-done(((bf16[8,48,512]{2,1,0:T(8,128)(2,1)}), bf16[8,48,512]{2,1,0:T(8,128)(2,1)S(1)}, u32[]{:S(2)}, u32[]{:S(2)}) %all-to-all-start) | async-done | bytes 393248 | tf_op jit(solution)/shard_map/all_to_all | solution.py:749
  22.8 0.0 copy-done.1
  22.8 1.5 %waves.1 = (bf16[768,384]{1,0:T(8,128)(2,1)}, f32[8,128]{1,0:T(8,128)}) custom-call(bf16[384,512]{1,0:T(8,128)(2,1)S(1)} %bitcast.19, bf16[768,512]{1,0:T(8,128)(2,1)S(1)} %copy-done.1, s32[16,128]{1,0:T(8,128)} %get-tuple-element.13.after_ref.first_ref), custom_call_target="tpu_custom_call" | custom-call | tf_op jit(solution)/shard_map/waves/pallas_call | solution.py:327
  24.4 8.3 %all-to-all-start.1 = ((bf16[16,48,384]{2,1,0:T(8,128)(2,1)}), bf16[16,48,384]{2,1,0:T(8,128)(2,1)S(1)}, u32[]{:S(2)}, u32[]{:S(2)}) async-start(bf16[16,48,384]{2,1,0:T(8,128)(2,1)} %bitcast.5), calls=%async_computation.1 | async-start | bytes 1179648 | tf_op jit(solution)/shard_map/all_to_all | solution.py:749
  32.7 0.0 copy-start.2
  32.7 0.0 copy-start.3
  32.7 3.6 %row_seen.1.seen_hbm = f32[2400,512]{1,0:T(8,128)} custom-call(s32[16,128]{1,0:T(8,128)} %get-tuple-element.13.after_ref.first_ref, s32[1,2048]{1,0:T(1,128)} %pairs_ref.3, s32[1,2048]{1,0:T(1,128)} %get-tuple-element.18.row_ref, f32[8,128]{1,0:T(8,128)} %get-tuple-element.19.after_ref), custom_call_target="tpu_custom_call" | custom-call | flops 5033164800 | bytes 4915200 | tf_op jit(solution)/shard_map/row_seen/pallas_call | solution.py:519
  36.3 7.4 %all-to-all-done.1 = bf16[16,48,384]{2,1,0:T(8,128)(2,1)S(1)} async-done(((bf16[16,48,384]{2,1,0:T(8,128)(2,1)}), bf16[16,48,384]{2,1,0:T(8,128)(2,1)S(1)}, u32[]{:S(2)}, u32[]{:S(2)}) %all-to-all-start.1) | async-done | bytes 589856 | tf_op jit(solution)/shard_map/all_to_all | solution.py:749
  43.7 0.0 copy-done.2
  43.7 0.0 copy-done.3
  43.7 0.0 copy-start
  43.7 8.1 %network.1 = (f32[2304,128]{1,0:T(8,128)}, bf16[768,384]{1,0:T(8,128)(2,1)S(1)}) custom-call(s32[16,128]{1,0:T(8,128)} %get-tuple-element.13.after_ref.first_ref, bf16[768,384]{1,0:T(8,128)(2,1)S(1)} %bitcast.16, bf16[2304,128]{1,0:T(8,128)(2,1)} %bitcast.22, f32[16,256]{1,0:T(8,128)} %get-tuple-element.16.rank_ref, f32[2400,512]{1,0:T(8,128)} %get-tuple-element.17.sum_hbm, ...), custom_call_target="tpu_custom_call" | custom-call | tf_op jit(solution)/shard_map/network/pallas_call | solution.py:698
  51.8 24.4 %all_to_all.44 = bf16[16,48,384]{2,1,0:T(8,128)(2,1)S(1)} all-to-all(bf16[16,48,384]{2,1,0:T(8,128)(2,1)S(1)} %bitcast.20), channel_id=1, replica_groups=mesh['lat'=8,'lev'=16] {'lev'}, dimensions={0} | all-to-all | bytes 1179648 | tf_op jit(solution)/shard_map/all_to_all | solution.py:749
  76.1 0.7 waves_adjoint.1
  76.8 15.5 %all_to_all.45 = bf16[8,48,512]{2,1,0:T(8,128)(2,1)S(1)} all-to-all(bf16[8,48,512]{2,1,0:T(8,128)(2,1)S(1)} %bitcast.17), channel_id=1, replica_groups=mesh['lat'=8,'lev'=16] {'lat'}, dimensions={0} | all-to-all | bytes 786432 | tf_op jit(solution)/shard_map/all_to_all | solution.py:749
  92.2 0.0 copy-done
  92.3 2.4 %legendre_adjoint.1 = f32[512,256]{1,0:T(8,128)} custom-call(bf16[32,256,256]{2,1,0:T(8,128)(2,1)S(1)} %copy-done, bf16[384,512]{1,0:T(8,128)(2,1)S(1)} %bitcast.18), custom_call_target="tpu_custom_call" | custom-call | tf_op jit(solution)/shard_map/legendre_adjoint/pallas_call | solution.py:293
Async XLA Ops:
  9.3 13.5 %all-to-all-start = ((bf16[8,48,512]{2,1,0:T(8,128)(2,1)}), bf16[8,48,512]{2,1,0:T(8,128)(2,1)S(1)}, u32[]{:S(2)}, u32[]{:S(2)}) async-start(bf16[8,48,512]{2,1,0:T(8,128)(2,1)} %bitcast.3), calls=%async_computation | async-start | bytes 786432 | tf_op jit(solution)/shard_map/all_to_all | solution.py:749
  15.8 7.1 %copy-start.1 = (bf16[768,512]{1,0:T(8,128)(2,1)S(1)}, bf16[768,512]{1,0:T(8,128)(2,1)}, u32[]{:S(2)}) copy-start(bf16[768,512]{1,0:T(8,128)(2,1)} %constant.20.table_ref) | copy-start | bytes 2359300
  24.4 19.3 %all-to-all-start.1 = ((bf16[16,48,384]{2,1,0:T(8,128)(2,1)}), bf16[16,48,384]{2,1,0:T(8,128)(2,1)S(1)}, u32[]{:S(2)}, u32[]{:S(2)}) async-start(bf16[16,48,384]{2,1,0:T(8,128)(2,1)} %bitcast.5), calls=%async_computation.1 | async-start | bytes 1179648 | tf_op jit(solution)/shard_map/all_to_all | solution.py:749
  32.7 11.0 %copy-start.2 = (bf16[1024,1024]{1,0:T(8,128)(2,1)S(1)}, bf16[1024,1024]{1,0:T(8,128)(2,1)}, u32[]{:S(2)}) copy-start(bf16[1024,1024]{1,0:T(8,128)(2,1)} %w_mid.1) | copy-start | bytes 6291460
  32.7 11.0 %copy-start.3 = (f32[512]{0:T(512)S(1)}, f32[512]{0:T(512)}, u32[]{:S(2)}) copy-start(f32[512]{0:T(512)} %param.19) | copy-start | bytes 6148
  43.7 48.6 %copy-start = (bf16[32,256,256]{2,1,0:T(8,128)(2,1)S(1)}, bf16[32,256,256]{2,1,0:T(8,128)(2,1)}, u32[]{:S(2)}) copy-start(bf16[32,256,256]{2,1,0:T(8,128)(2,1)} %get-tuple-element.12.after_ref.p_ref) | copy-start | bytes 12582916

commit v5 on v4

--- a/solution.py
+++ b/solution.py
@@ -67,19 +67,6 @@
     return jnp.dot(a, b, preferred_element_type=f32)
 
 
-def geometry():
-    lat = (0.5 - (np.arange(256, dtype=np.float64) + 0.5) / NLAT) * np.pi
-    valid = np.arange(256) < HALF
-    sin_lat = np.where(valid, np.sin(lat), 0.0)
-    log_cos = np.where(valid, np.log(np.cos(np.where(valid, lat, 0.0))), 0.0)
-    rows = np.zeros((8, 256), np.float32)
-    rows[0], rows[1], rows[2] = sin_lat, log_cos, valid
-    k = np.arange(1, M, dtype=np.float64)
-    steps = 0.5 * np.log((2.0 * k + 1.0) / (2.0 * k))
-    log_norm = np.concatenate([[0.0], np.cumsum(steps)]) + HALF_LOG
-    return rows, np.repeat(log_norm[:, None], LANES, axis=1).astype(np.float32)
-
-
 def wave_table():
     m = np.arange(M)
     phase = (np.arange(NLON)[:, None] * m[None, :] % NLON) * (2.0 * np.pi / NLON)
@@ -94,30 +81,31 @@
 
 
 def legendre_kernel(
-    lat_ref, geo_ref, norm_ref, spec_ref, p_hbm, four_ref, table, waves, halves, p_buf, sems
+    spec_hbm, p_hbm, four_ref, spec_ref, table, waves, halves, p_buf, sems, spec_sem
 ):
     groups = range(ML // 8)
 
-    for h in (0, 1):
-        for k in range(2 * LL):
-            halves[h, k * M_PITCH : k * M_PITCH + ML, :] = spec_ref[
-                k * ML : (k + 1) * ML, h * LANES : (h + 1) * LANES
-            ]
-    m0 = lat_ref[0] * ML
+    fetch = pltpu.make_async_copy(spec_hbm, spec_ref, spec_sem)
+    fetch.start()
+    m0 = lax.axis_index("lat").astype(jnp.int32) * ML
     sub = lax.broadcasted_iota(jnp.int32, (8, LANES), 0)
     mf = [(sub + (m0 + 8 * g)).astype(f32) for g in groups]
     m2 = [v * v for v in mf]
     zero = jnp.zeros((8, LANES), f32)
-    x = [jnp.broadcast_to(geo_ref[0:1, h * LANES : (h + 1) * LANES], (8, LANES)) for h in (0, 1)]
-    log_cos = [
-        jnp.broadcast_to(geo_ref[1:2, h * LANES : (h + 1) * LANES], (8, LANES)) for h in (0, 1)
+    lanes = [lax.broadcasted_iota(jnp.int32, (8, LANES), 1) + h * LANES for h in (0, 1)]
+    valid = [jnp.where(lanes[h] < HALF, 1.0, 0.0) for h in (0, 1)]
+    colat = [
+        (jnp.minimum(lanes[h], HALF - 1).astype(f32) + 0.5) * (math.pi / NLAT) for h in (0, 1)
     ]
-    valid = [
-        jnp.broadcast_to(geo_ref[2:3, h * LANES : (h + 1) * LANES], (8, LANES)) for h in (0, 1)
+    x = [jnp.cos(colat[h]) * valid[h] for h in (0, 1)]
+    log_cos = [jnp.log(jnp.sin(colat[h])) for h in (0, 1)]
+    k_ids = lax.broadcasted_iota(jnp.int32, (8, M), 1).astype(f32) + 1.0
+    half_logs = 0.5 * jnp.log((2.0 * k_ids + 1.0) / (2.0 * k_ids))
+    norm = [
+        jnp.sum(jnp.where(k_ids <= mf[g][:, 0:1], half_logs, 0.0), axis=1, keepdims=True)
+        for g in groups
     ]
-    logs = [
-        [norm_ref[pl.ds(m0 + 8 * g, 8), :] + mf[g] * log_cos[h] for h in (0, 1)] for g in groups
-    ]
+    logs = [[HALF_LOG + norm[g] + mf[g] * log_cos[h] for h in (0, 1)] for g in groups]
 
     def block(i, carry):
         prev, earlier, logs, eps_prev, nf = carry
@@ -159,6 +147,12 @@
     empty = [[zero, zero] for _ in groups]
     lax.fori_loop(0, N // 8, block, (empty, empty, logs, [zero for _ in groups], zero))
 
+    fetch.wait()
+    for h in (0, 1):
+        for k in range(2 * LL):
+            halves[h, k * M_PITCH : k * M_PITCH + ML, :] = spec_ref[
+                k * ML : (k + 1) * ML, h * LANES : (h + 1) * LANES
+            ]
     lane = lax.broadcasted_iota(jnp.int32, (1, N), 1)
     alternate = jnp.where(lane % 2 == 0, 1.0, -1.0)
     def store(step):
@@ -219,18 +213,19 @@
     store(steps - 1).wait()
 
 
-def legendre_transform(lat_index, spectral):
-    geo, norm = geometry()
+def legendre_transform(spectral):
     return pl.pallas_call(
         legendre_kernel,
-        in_specs=[pl.BlockSpec(memory_space=pltpu.SMEM), VMEM_SPEC, VMEM_SPEC, VMEM_SPEC],
+        in_specs=[pl.BlockSpec(memory_space=pl.ANY)],
         out_specs=[pl.BlockSpec(memory_space=pl.ANY), VMEM_SPEC],
         scratch_shapes=[
+            pltpu.VMEM((ROWS, N), f32),
             pltpu.VMEM((2, N * M_PITCH, LANES), f32),
             pltpu.VMEM((2, 2, LL * L_PITCH, LANES), f32),
             pltpu.VMEM((2, 2 * LL * M_PITCH, LANES), f32),
             pltpu.VMEM((2, M_STEP, N, 256), bf16),
             pltpu.SemaphoreType.DMA((2,)),
+            pltpu.SemaphoreType.DMA,
         ],
         out_shape=[
             pltpu.HBM((ML, N, 256), bf16),
@@ -238,7 +233,7 @@
         ],
         compiler_params=params(24),
         name="legendre",
-    )(lat_index, in_hbm(jnp.asarray(geo)), in_hbm(jnp.asarray(norm)), in_hbm(spectral.reshape(ROWS, N)))
+    )(in_hbm(spectral.reshape(ROWS, N)))
 
 
 def adjoint_kernel(p_ref, rows_ref, out_ref, folded, held):
@@ -556,10 +551,10 @@
 
 
 def network_kernel(
-    first_ref,
+    first_hbm,
     inc_ref,
     back_hbm,
-    rank_ref,
+    rank_hbm,
     sum_hbm,
     seen_hbm,
     chan_ref,
@@ -568,6 +563,8 @@
     w_out_hbm,
     grad_hbm,
     send_ref,
+    first_ref,
+    rank_ref,
     state,
     picks,
     packed,
@@ -581,9 +578,6 @@
     sems,
     part_sems,
 ):
-    total = first_ref[GROUPS, 0]
-    tiles = (total + (TILE - 1)) // TILE
-
     def fetches(t, slot):
         r = pl.ds(pl.multiple_of(t * TILE, 8), TILE)
         return (
@@ -595,6 +589,12 @@
         r = pl.ds(pl.multiple_of(jc * PART, PART), PART)
         return pltpu.make_async_copy(src.at[r, :], dst.at[r, :], part_sems.at[k, jc])
 
+    ranks = [
+        pltpu.make_async_copy(rank_hbm, rank_ref, part_sems.at[3, 0]),
+        pltpu.make_async_copy(first_hbm, first_ref, part_sems.at[3, 1]),
+    ]
+    for fetch in ranks:
+        fetch.start()
     for jc in range(CLAT // J_STEP):
         part_copy(0, back_hbm, back_buf, jc).start()
     weights = [
@@ -606,10 +606,6 @@
         fetch.start()
     for fetch in fetches(0, 0):
         fetch.start()
-
-    row = lax.broadcasted_iota(jnp.int32, (GROUP, GROUP), 0).astype(f32)
-    for g in range(GROUPS):
-        picks[g] = jnp.where(row == rank_ref[g : g + 1, :], 1.0, 0.0).astype(bf16)
 
     def to_state(jc, _):
         part_copy(0, back_hbm, back_buf, jc).wait()
@@ -630,6 +626,14 @@
         return 0
 
     lax.fori_loop(0, CLAT // J_STEP, to_state, 0)
+    for fetch in ranks:
+        fetch.wait()
+    total = first_ref[GROUPS, 0]
+    tiles = (total + (TILE - 1)) // TILE
+    row = lax.broadcasted_iota(jnp.int32, (GROUP, GROUP), 0).astype(f32)
+    for g in range(GROUPS):
+        picks[g] = jnp.where(row == rank_ref[g : g + 1, :], 1.0, 0.0).astype(bf16)
+
 
     def group_rows(g):
         first = pl.ds(pl.multiple_of(first_ref[g, 0], 8), GROUP)
@@ -698,10 +702,10 @@
     grad, send = pl.pallas_call(
         network_kernel,
         in_specs=[
-            pl.BlockSpec(memory_space=pltpu.SMEM),
+            anywhere,
             VMEM_SPEC,
             anywhere,
-            VMEM_SPEC,
+            anywhere,
             anywhere,
             anywhere,
             VMEM_SPEC,
@@ -715,6 +719,8 @@
             pltpu.VMEM((NLON, JL), bf16),
         ],
         scratch_shapes=[
+            pltpu.SMEM((16, LANES), jnp.int32),
+            pltpu.VMEM((16, GROUP), f32),
             pltpu.VMEM((CELLS, 2 * LEV), bf16),
             pltpu.VMEM((GROUPS, GROUP, GROUP), bf16),
             pltpu.VMEM((MAX_ROWS + GROUP, 2 * LEV), f32),
@@ -726,7 +732,7 @@
             pltpu.VMEM((2, TILE, CHAN), f32),
             pltpu.VMEM((2, TILE, CHAN), f32),
             pltpu.SemaphoreType.DMA((2, 2)),
-            pltpu.SemaphoreType.DMA((3, 3)),
+            pltpu.SemaphoreType.DMA((4, 3)),
         ],
         compiler_params=params(30),
         name="network",
@@ -762,8 +768,7 @@
     weight_out,
 ):
     table = on_chip(wave_table())
-    lat_index = lax.axis_index("lat").astype(jnp.int32).reshape(1)
-    legendre, fourier = legendre_transform(lat_index, spectral)
+    legendre, fourier = legendre_transform(spectral)
     sums, row, rank, first = row_sums(counts, columns, used_pairs, radiances[0], legendre)
     waves, token = waves_to_grid(exchange(fourier, "lat"), table, first)
     seen = row_seen(first, used_pairs, row, token)

time: 95.4 us -> 93.8 us (0.983)
  Pallas kernels: 30.5 us -> 35.6 us
  waiting for transfers between devices: 8.92 us -> 5.96 us
  blocking collectives: 39.8 us -> 37 us
    all_to_all x2, waiting for transfers between devices: 8.92 us -> 5.96 us  [exchange(): lax.all_to_all(rows, axis, split_axis=0, concat_axis=0, tiled=True)]
    all_to_all x2, blocking collectives: 39.8 us -> 37 us  [exchange(): lax.all_to_all(rows, axis, split_axis=0, concat_axis=0, tiled=True)]
    pallas_call x2, Pallas kernels: 16.8 us -> 19.5 us  [the longest x1 11.8 us: network(): pl.pallas_call(network_kernel, in_specs=[anywhere, VMEM_SPEC, anywhere, a...]
    pallas_call x1, Pallas kernels: 5.47 us -> 6.71 us  [row_sums(): pl.pallas_call(sums_kernel, in_specs=[pl.BlockSpec(memory_space=pltpu.SME...]
    pallas_call x1, Pallas kernels: 3.6 us -> 4.74 us  [row_seen(): pl.pallas_call(seen_kernel, in_specs=[pl.BlockSpec(memory_space=pltpu.SME...]
  transfers between devices with their start and end apart: 2 -> 2, of which waited for: 2 -> 2; matrix products, arithmetic and copies ran while one was open for 0% -> 0% of each run, Pallas kernels for 10% -> 12%
where the time goes in v5:
time: 93.8 us; the launch traced here: 93.5 us
  blocking collectives  37 us (39%)
  Pallas kernels  35.6 us (38%)
  starting transfers between devices  13.6 us (14%)
  waiting for transfers between devices  5.96 us (6%)
  between operations  1.36 us (1%)
    all_to_all x2, blocking collectives, exchange(): lax.all_to_all(rows, axis, split_axis=0, concat_axis=0, tiled=True)  37 us
    all_to_all x2, starting transfers between devices, exchange(): lax.all_to_all(rows, axis, split_axis=0, concat_axis=0, tiled=True)  13.6 us
    pallas_call x1, Pallas kernels, network(): pl.pallas_call(network_kernel, in_specs=[anywhere, VMEM_SPEC, anywhere, a...  11.8 us
    pallas_call x1, Pallas kernels, legendre_transform(): pl.pallas_call(legendre_kernel, in_specs=[pl.BlockSpec(memory_space=pl.AN...  7.76 us
    pallas_call x1, Pallas kernels, row_sums(): pl.pallas_call(sums_kernel, in_specs=[pl.BlockSpec(memory_space=pltpu.SME...  6.71 us
    all_to_all x2, waiting for transfers between devices, exchange(): lax.all_to_all(rows, axis, split_axis=0, concat_axis=0, tiled=True)  5.96 us
    pallas_call x1, Pallas kernels, row_seen(): pl.pallas_call(seen_kernel, in_specs=[pl.BlockSpec(memory_space=pltpu.SME...  4.74 us
    pallas_call x1, Pallas kernels, legendre_adjoint(): pl.pallas_call(adjoint_kernel, grid=(ML // ADJOINT_STEP,), in_specs=[VMEM...  2.44 us
  transfers between devices with their start and end apart: 2, of which 2 were waited for; matrix products, arithmetic and copies ran while one was open for 0% of the time, Pallas kernels for 12%

profile of v5, /device:TPU:1, one launch (start us, length us, event | category | flops | bytes accessed | tf_op | source)
XLA Modules:
  0.0 93.5 jit_solution(15836466053990676268)
XLA Ops:
  0.6 7.8 %legendre.1 = (bf16[32,256,256]{2,1,0:T(8,128)(2,1)}, bf16[384,512]{1,0:T(8,128)(2,1)}) custom-call(f32[512,256]{1,0:T(8,128)} %bitcast.23), custom_call_target="tpu_custom_call" | custom-call | tf_op jit(solution)/shard_map/legendre/pallas_call | solution.py:217
  8.4 5.8 %all-to-all-start = ((bf16[8,48,512]{2,1,0:T(8,128)(2,1)}), bf16[8,48,512]{2,1,0:T(8,128)(2,1)S(1)}, u32[]{:S(2)}, u32[]{:S(2)}) async-start(bf16[8,48,512]{2,1,0:T(8,128)(2,1)} %bitcast.2), calls=%async_computation | async-start | bytes 786432 | tf_op jit(solution)/shard_map/all_to_all | solution.py:755
  14.8 0.0 copy-start.1
  14.9 6.7 %row_sums.1 = (f32[2400,512]{1,0:T(8,128)}, s32[1,2048]{1,0:T(1,128)}, f32[16,256]{1,0:T(8,128)}, s32[16,128]{1,0:T(8,128)}) custom-call(s32[1]{0:T(128)S(6)} %copy.13.count_ref, s32[1,2048]{1,0:T(1,128)} %columns_ref.1, s32[1,2048]{1,0:T(1,128)} %pairs_ref.3, bf16[2048,512]{1,0:T(8,128)(2,1)} %bitcast.24, ...), custom_call_target="tpu_custom_call" | custom-call | flops 5033164800 | bytes 4915200 | tf_op jit(solution)/shard_map/row_sums/pallas_call | solution.py:487
  21.6 0.3 all-to-all-done
  21.9 0.0 copy-done.1
  21.9 1.5 %waves.1 = (bf16[768,384]{1,0:T(8,128)(2,1)}, f32[8,128]{1,0:T(8,128)}) custom-call(bf16[384,512]{1,0:T(8,128)(2,1)S(1)} %bitcast.18, bf16[768,512]{1,0:T(8,128)(2,1)S(1)} %copy-done.1, s32[16,128]{1,0:T(8,128)} %get-tuple-element.13.after_ref.first_ref.first_hbm), custom_call_target="tpu_custom_call" | custom-call | tf_op jit(solution)/shard_map/waves/pallas_call | solution.py:322
  23.4 7.8 %all-to-all-start.1 = ((bf16[16,48,384]{2,1,0:T(8,128)(2,1)}), bf16[16,48,384]{2,1,0:T(8,128)(2,1)S(1)}, u32[]{:S(2)}, u32[]{:S(2)}) async-start(bf16[16,48,384]{2,1,0:T(8,128)(2,1)} %bitcast.4), calls=%async_computation.1 | async-start | bytes 1179648 | tf_op jit(solution)/shard_map/all_to_all | solution.py:755
  31.2 0.0 copy-start.2
  31.2 0.0 copy-start.3
  31.3 4.7 %row_seen.1.seen_hbm = f32[2400,512]{1,0:T(8,128)} custom-call(s32[16,128]{1,0:T(8,128)} %get-tuple-element.13.after_ref.first_ref.first_hbm, s32[1,2048]{1,0:T(1,128)} %pairs_ref.3, s32[1,2048]{1,0:T(1,128)} %get-tuple-element.18.row_ref, f32[8,128]{1,0:T(8,128)} %get-tuple-element.19.after_ref), custom_call_target="tpu_custom_call" | custom-call | flops 5033164800 | bytes 4915200 | tf_op jit(solution)/shard_map/row_seen/pallas_call | solution.py:514
  36.0 5.6 %all-to-all-done.1 = bf16[16,48,384]{2,1,0:T(8,128)(2,1)S(1)} async-done(((bf16[16,48,384]{2,1,0:T(8,128)(2,1)}), bf16[16,48,384]{2,1,0:T(8,128)(2,1)S(1)}, u32[]{:S(2)}, u32[]{:S(2)}) %all-to-all-start.1) | async-done | bytes 589856 | tf_op jit(solution)/shard_map/all_to_all | solution.py:755
  41.6 0.0 copy-done.2
  41.6 0.0 copy-done.3
  41.6 0.0 copy-start
  41.6 11.8 %network.1 = (f32[2304,128]{1,0:T(8,128)}, bf16[768,384]{1,0:T(8,128)(2,1)S(1)}) custom-call(s32[16,128]{1,0:T(8,128)} %get-tuple-element.13.after_ref.first_ref.first_hbm, bf16[768,384]{1,0:T(8,128)(2,1)S(1)} %bitcast.15, bf16[2304,128]{1,0:T(8,128)(2,1)} %bitcast.21, f32[16,256]{1,0:T(8,128)} %get-tuple-element.16.rank_hbm, ...), custom_call_target="tpu_custom_call" | custom-call | tf_op jit(solution)/shard_map/network/pallas_call | solution.py:702
  53.4 17.9 %all_to_all.44 = bf16[16,48,384]{2,1,0:T(8,128)(2,1)S(1)} all-to-all(bf16[16,48,384]{2,1,0:T(8,128)(2,1)S(1)} %bitcast.19), channel_id=1, replica_groups=mesh['lat'=8,'lev'=16] {'lev'}, dimensions={0} | all-to-all | bytes 1179648 | tf_op jit(solution)/shard_map/all_to_all | solution.py:755
  71.3 0.7 waves_adjoint.1
  71.9 19.1 %all_to_all.45 = bf16[8,48,512]{2,1,0:T(8,128)(2,1)S(1)} all-to-all(bf16[8,48,512]{2,1,0:T(8,128)(2,1)S(1)} %bitcast.16), channel_id=1, replica_groups=mesh['lat'=8,'lev'=16] {'lat'}, dimensions={0} | all-to-all | bytes 786432 | tf_op jit(solution)/shard_map/all_to_all | solution.py:755
  91.1 0.0 copy-done
  91.1 2.4 %legendre_adjoint.1 = f32[512,256]{1,0:T(8,128)} custom-call(bf16[32,256,256]{2,1,0:T(8,128)(2,1)S(1)} %copy-done, bf16[384,512]{1,0:T(8,128)(2,1)S(1)} %bitcast.17), custom_call_target="tpu_custom_call" | custom-call | tf_op jit(solution)/shard_map/legendre_adjoint/pallas_call | solution.py:288
Async XLA Ops:
  8.4 13.5 %all-to-all-start = ((bf16[8,48,512]{2,1,0:T(8,128)(2,1)}), bf16[8,48,512]{2,1,0:T(8,128)(2,1)S(1)}, u32[]{:S(2)}, u32[]{:S(2)}) async-start(bf16[8,48,512]{2,1,0:T(8,128)(2,1)} %bitcast.2), calls=%async_computation | async-start | bytes 786432 | tf_op jit(solution)/shard_map/all_to_all | solution.py:755
  14.8 7.1 %copy-start.1 = (bf16[768,512]{1,0:T(8,128)(2,1)S(1)}, bf16[768,512]{1,0:T(8,128)(2,1)}, u32[]{:S(2)}) copy-start(bf16[768,512]{1,0:T(8,128)(2,1)} %constant.8.table_ref) | copy-start | bytes 2359300
  23.4 18.2 %all-to-all-start.1 = ((bf16[16,48,384]{2,1,0:T(8,128)(2,1)}), bf16[16,48,384]{2,1,0:T(8,128)(2,1)S(1)}, u32[]{:S(2)}, u32[]{:S(2)}) async-start(bf16[16,48,384]{2,1,0:T(8,128)(2,1)} %bitcast.4), calls=%async_computation.1 | async-start | bytes 1179648 | tf_op jit(solution)/shard_map/all_to_all | solution.py:755
  31.2 10.4 %copy-start.2 = (bf16[1024,1024]{1,0:T(8,128)(2,1)S(1)}, bf16[1024,1024]{1,0:T(8,128)(2,1)}, u32[]{:S(2)}) copy-start(bf16[1024,1024]{1,0:T(8,128)(2,1)} %w_mid.1) | copy-start | bytes 6291460
  31.2 10.4 %copy-start.3 = (f32[512]{0:T(512)S(1)}, f32[512]{0:T(512)}, u32[]{:S(2)}) copy-start(f32[512]{0:T(512)} %param.17) | copy-start | bytes 6148
  41.6 49.4 %copy-start = (bf16[32,256,256]{2,1,0:T(8,128)(2,1)S(1)}, bf16[32,256,256]{2,1,0:T(8,128)(2,1)}, u32[]{:S(2)}) copy-start(bf16[32,256,256]{2,1,0:T(8,128)(2,1)} %get-tuple-element.12.after_ref.p_ref) | copy-start | bytes 12582916

commit v6 on v5

--- a/solution.py
+++ b/solution.py
@@ -607,8 +607,7 @@
     for fetch in fetches(0, 0):
         fetch.start()
 
-    def to_state(jc, _):
-        part_copy(0, back_hbm, back_buf, jc).wait()
+    def turn(jc, _):
         lanes = pl.ds(pl.multiple_of(jc * LANES, LANES), LANES)
         for part in range(CLON // X_ROWS):
             x0 = part * X_ROWS
@@ -619,13 +618,10 @@
             v = swap_blocks(v)
             for j in range(J_STEP):
                 r = pl.ds(pl.multiple_of((jc * J_STEP + j) * CLON + x0, 16), X_ROWS)
-                grid_state = back_buf[r, :].astype(f32) + v[j]
-                high = grid_state.astype(bf16)
-                state[r, :LEV] = high
-                state[r, LEV:] = (grid_state - high.astype(f32)).astype(bf16)
+                grads[r, :] = v[j]
         return 0
 
-    lax.fori_loop(0, CLAT // J_STEP, to_state, 0)
+    lax.fori_loop(0, CLAT // J_STEP, turn, 0)
     for fetch in ranks:
         fetch.wait()
     total = first_ref[GROUPS, 0]
@@ -633,7 +629,18 @@
     row = lax.broadcasted_iota(jnp.int32, (GROUP, GROUP), 0).astype(f32)
     for g in range(GROUPS):
         picks[g] = jnp.where(row == rank_ref[g : g + 1, :], 1.0, 0.0).astype(bf16)
-
+    for jc in range(CLAT // J_STEP):
+        part_copy(0, back_hbm, back_buf, jc).wait()
+
+    def to_state(i, _):
+        r = pl.ds(pl.multiple_of(i * GROUP, GROUP), GROUP)
+        grid_state = back_buf[r, :].astype(f32) + grads[r, :]
+        high = grid_state.astype(bf16)
+        state[r, :LEV] = high
+        state[r, LEV:] = (grid_state - high.astype(f32)).astype(bf16)
+        return 0
+
+    lax.fori_loop(0, GROUPS, to_state, 0)
 
     def group_rows(g):
         first = pl.ds(pl.multiple_of(first_ref[g, 0], 8), GROUP)

time: 93.8 us -> 92.5 us (0.986)
  blocking collectives: 37 us -> 35.6 us
    all_to_all x2, blocking collectives: 37 us -> 35.6 us  [exchange(): lax.all_to_all(rows, axis, split_axis=0, concat_axis=0, tiled=True)]
where the time goes in v6:
time: 92.5 us; the launch traced here: 92.6 us
  blocking collectives  35.6 us (38%)
  Pallas kernels  34.7 us (38%)
  starting transfers between devices  14.4 us (16%)
  waiting for transfers between devices  6.45 us (7%)
  between operations  1.36 us (1%)
    all_to_all x2, blocking collectives, exchange(): lax.all_to_all(rows, axis, split_axis=0, concat_axis=0, tiled=True)  35.6 us
    all_to_all x2, starting transfers between devices, exchange(): lax.all_to_all(rows, axis, split_axis=0, concat_axis=0, tiled=True)  14.4 us
    pallas_call x1, Pallas kernels, network(): pl.pallas_call(network_kernel, in_specs=[anywhere, VMEM_SPEC, anywhere, a...  10.9 us
    pallas_call x1, Pallas kernels, legendre_transform(): pl.pallas_call(legendre_kernel, in_specs=[pl.BlockSpec(memory_space=pl.AN...  7.76 us
    pallas_call x1, Pallas kernels, row_sums(): pl.pallas_call(sums_kernel, in_specs=[pl.BlockSpec(memory_space=pltpu.SME...  6.71 us
    all_to_all x2, waiting for transfers between devices, exchange(): lax.all_to_all(rows, axis, split_axis=0, concat_axis=0, tiled=True)  6.45 us
    pallas_call x1, Pallas kernels, row_seen(): pl.pallas_call(seen_kernel, in_specs=[pl.BlockSpec(memory_space=pltpu.SME...  4.74 us
    pallas_call x1, Pallas kernels, legendre_adjoint(): pl.pallas_call(adjoint_kernel, grid=(ML // ADJOINT_STEP,), in_specs=[VMEM...  2.43 us
  transfers between devices with their start and end apart: 2, of which 2 were waited for; matrix products, arithmetic and copies ran while one was open for 0% of the time, Pallas kernels for 12%

profile of v6, /device:TPU:1, one launch (start us, length us, event | category | flops | bytes accessed | tf_op | source)
XLA Modules:
  0.0 92.6 jit_solution(1423022412999415051)
XLA Ops:
  0.6 7.8 %legendre.1 = (bf16[32,256,256]{2,1,0:T(8,128)(2,1)}, bf16[384,512]{1,0:T(8,128)(2,1)}) custom-call(f32[512,256]{1,0:T(8,128)} %bitcast.23), custom_call_target="tpu_custom_call" | custom-call | tf_op jit(solution)/shard_map/legendre/pallas_call | solution.py:217
  8.4 5.8 %all-to-all-start = ((bf16[8,48,512]{2,1,0:T(8,128)(2,1)}), bf16[8,48,512]{2,1,0:T(8,128)(2,1)S(1)}, u32[]{:S(2)}, u32[]{:S(2)}) async-start(bf16[8,48,512]{2,1,0:T(8,128)(2,1)} %bitcast.2), calls=%async_computation | async-start | bytes 786432 | tf_op jit(solution)/shard_map/all_to_all | solution.py:762
  14.8 0.0 copy-start.1
  14.9 6.7 %row_sums.1 = (f32[2400,512]{1,0:T(8,128)}, s32[1,2048]{1,0:T(1,128)}, f32[16,256]{1,0:T(8,128)}, s32[16,128]{1,0:T(8,128)}) custom-call(s32[1]{0:T(128)S(6)} %copy.13.count_ref, s32[1,2048]{1,0:T(1,128)} %columns_ref.1, s32[1,2048]{1,0:T(1,128)} %pairs_ref.3, bf16[2048,512]{1,0:T(8,128)(2,1)} %bitcast.24, ...), custom_call_target="tpu_custom_call" | custom-call | flops 5033164800 | bytes 4915200 | tf_op jit(solution)/shard_map/row_sums/pallas_call | solution.py:487
  21.6 0.3 all-to-all-done
  21.9 0.0 copy-done.1
  21.9 1.5 %waves.1 = (bf16[768,384]{1,0:T(8,128)(2,1)}, f32[8,128]{1,0:T(8,128)}) custom-call(bf16[384,512]{1,0:T(8,128)(2,1)S(1)} %bitcast.18, bf16[768,512]{1,0:T(8,128)(2,1)S(1)} %copy-done.1, s32[16,128]{1,0:T(8,128)} %get-tuple-element.13.after_ref.first_ref.first_hbm), custom_call_target="tpu_custom_call" | custom-call | tf_op jit(solution)/shard_map/waves/pallas_call | solution.py:322
  23.4 8.6 %all-to-all-start.1 = ((bf16[16,48,384]{2,1,0:T(8,128)(2,1)}), bf16[16,48,384]{2,1,0:T(8,128)(2,1)S(1)}, u32[]{:S(2)}, u32[]{:S(2)}) async-start(bf16[16,48,384]{2,1,0:T(8,128)(2,1)} %bitcast.4), calls=%async_computation.1 | async-start | bytes 1179648 | tf_op jit(solution)/shard_map/all_to_all | solution.py:762
  32.1 0.0 copy-start.2
  32.1 0.0 copy-start.3
  32.1 4.7 %row_seen.1.seen_hbm = f32[2400,512]{1,0:T(8,128)} custom-call(s32[16,128]{1,0:T(8,128)} %get-tuple-element.13.after_ref.first_ref.first_hbm, s32[1,2048]{1,0:T(1,128)} %pairs_ref.3, s32[1,2048]{1,0:T(1,128)} %get-tuple-element.18.row_ref, f32[8,128]{1,0:T(8,128)} %get-tuple-element.19.after_ref), custom_call_target="tpu_custom_call" | custom-call | flops 5033164800 | bytes 4915200 | tf_op jit(solution)/shard_map/row_seen/pallas_call | solution.py:514
  36.8 6.1 %all-to-all-done.1 = bf16[16,48,384]{2,1,0:T(8,128)(2,1)S(1)} async-done(((bf16[16,48,384]{2,1,0:T(8,128)(2,1)}), bf16[16,48,384]{2,1,0:T(8,128)(2,1)S(1)}, u32[]{:S(2)}, u32[]{:S(2)}) %all-to-all-start.1) | async-done | bytes 589856 | tf_op jit(solution)/shard_map/all_to_all | solution.py:762
  43.0 0.0 copy-done.2
  43.0 0.0 copy-done.3
  43.0 0.0 copy-start
  43.0 10.9 %network.1 = (f32[2304,128]{1,0:T(8,128)}, bf16[768,384]{1,0:T(8,128)(2,1)S(1)}) custom-call(s32[16,128]{1,0:T(8,128)} %get-tuple-element.13.after_ref.first_ref.first_hbm, bf16[768,384]{1,0:T(8,128)(2,1)S(1)} %bitcast.15, bf16[2304,128]{1,0:T(8,128)(2,1)} %bitcast.21, f32[16,256]{1,0:T(8,128)} %get-tuple-element.16.rank_hbm, ...), custom_call_target="tpu_custom_call" | custom-call | tf_op jit(solution)/shard_map/network/pallas_call | solution.py:709
  53.8 20.2 %all_to_all.44 = bf16[16,48,384]{2,1,0:T(8,128)(2,1)S(1)} all-to-all(bf16[16,48,384]{2,1,0:T(8,128)(2,1)S(1)} %bitcast.19), channel_id=1, replica_groups=mesh['lat'=8,'lev'=16] {'lev'}, dimensions={0} | all-to-all | bytes 1179648 | tf_op jit(solution)/shard_map/all_to_all | solution.py:762
  74.1 0.7 waves_adjoint.1
  74.7 15.4 %all_to_all.45 = bf16[8,48,512]{2,1,0:T(8,128)(2,1)S(1)} all-to-all(bf16[8,48,512]{2,1,0:T(8,128)(2,1)S(1)} %bitcast.16), channel_id=1, replica_groups=mesh['lat'=8,'lev'=16] {'lat'}, dimensions={0} | all-to-all | bytes 786432 | tf_op jit(solution)/shard_map/all_to_all | solution.py:762
  90.1 0.0 copy-done
  90.1 2.4 %legendre_adjoint.1 = f32[512,256]{1,0:T(8,128)} custom-call(bf16[32,256,256]{2,1,0:T(8,128)(2,1)S(1)} %copy-done, bf16[384,512]{1,0:T(8,128)(2,1)S(1)} %bitcast.17), custom_call_target="tpu_custom_call" | custom-call | tf_op jit(solution)/shard_map/legendre_adjoint/pallas_call | solution.py:288
Async XLA Ops:
  8.4 13.5 %all-to-all-start = ((bf16[8,48,512]{2,1,0:T(8,128)(2,1)}), bf16[8,48,512]{2,1,0:T(8,128)(2,1)S(1)}, u32[]{:S(2)}, u32[]{:S(2)}) async-start(bf16[8,48,512]{2,1,0:T(8,128)(2,1)} %bitcast.2), calls=%async_computation | async-start | bytes 786432 | tf_op jit(solution)/shard_map/all_to_all | solution.py:762
  14.8 7.1 %copy-start.1 = (bf16[768,512]{1,0:T(8,128)(2,1)S(1)}, bf16[768,512]{1,0:T(8,128)(2,1)}, u32[]{:S(2)}) copy-start(bf16[768,512]{1,0:T(8,128)(2,1)} %constant.8.table_ref) | copy-start | bytes 2359300
  23.4 19.5 %all-to-all-start.1 = ((bf16[16,48,384]{2,1,0:T(8,128)(2,1)}), bf16[16,48,384]{2,1,0:T(8,128)(2,1)S(1)}, u32[]{:S(2)}, u32[]{:S(2)}) async-start(bf16[16,48,384]{2,1,0:T(8,128)(2,1)} %bitcast.4), calls=%async_computation.1 | async-start | bytes 1179648 | tf_op jit(solution)/shard_map/all_to_all | solution.py:762
  32.1 10.9 %copy-start.2 = (bf16[1024,1024]{1,0:T(8,128)(2,1)S(1)}, bf16[1024,1024]{1,0:T(8,128)(2,1)}, u32[]{:S(2)}) copy-start(bf16[1024,1024]{1,0:T(8,128)(2,1)} %w_mid.1) | copy-start | bytes 6291460
  32.1 10.9 %copy-start.3 = (f32[512]{0:T(512)S(1)}, f32[512]{0:T(512)}, u32[]{:S(2)}) copy-start(f32[512]{0:T(512)} %param.17) | copy-start | bytes 6148
  43.0 47.2 %copy-start = (bf16[32,256,256]{2,1,0:T(8,128)(2,1)S(1)}, bf16[32,256,256]{2,1,0:T(8,128)(2,1)}, u32[]{:S(2)}) copy-start(bf16[32,256,256]{2,1,0:T(8,128)(2,1)} %get-tuple-element.12.after_ref.p_ref) | copy-start | bytes 12582916

commit v7 on v6

--- a/solution.py
+++ b/solution.py
@@ -436,6 +436,9 @@
     obs_hbm,
     after_ref,
     sum_hbm,
+    row_hbm,
+    rank_hbm,
+    first_hbm,
     row_ref,
     rank_ref,
     first_ref,
@@ -444,6 +447,7 @@
     tile_buf,
     sems,
     obs_sems,
+    small_sems,
 ):
     del after_ref
 
@@ -457,10 +461,19 @@
     row_ref[...] = row
     rank_ref[...] = rank
     first_ref[...] = first.astype(jnp.int32)
+    small = [
+        pltpu.make_async_copy(row_ref, row_hbm, small_sems.at[0]),
+        pltpu.make_async_copy(rank_ref, rank_hbm, small_sems.at[1]),
+        pltpu.make_async_copy(first_ref, first_hbm, small_sems.at[2]),
+    ]
+    for store in small:
+        store.start()
     for part in range(4):
         fetch(part).wait()
         active_channels(part, pairs_ref, lambda r, lanes: obs[r, lanes].astype(f32), masked)
     write_sums(jnp.max(first).astype(jnp.int32), row_ref, masked, tile_buf, sum_hbm, sems)
+    for store in small:
+        store.wait()
 
 
 def seen_kernel(first_ref, pairs_ref, row_ref, after_ref, sum_hbm, masked, tile_buf, sems):
@@ -493,10 +506,15 @@
             anywhere,
             anywhere,
         ],
-        out_specs=[anywhere, VMEM_SPEC, VMEM_SPEC, VMEM_SPEC],
-        scratch_shapes=[pltpu.VMEM((CAP, CHAN), bf16)]
+        out_specs=[anywhere] * 4,
+        scratch_shapes=[
+            pltpu.VMEM((1, CAP), jnp.int32),
+            pltpu.VMEM((16, GROUP), f32),
+            pltpu.VMEM((16, LANES), jnp.int32),
+            pltpu.VMEM((CAP, CHAN), bf16),
+        ]
         + SUM_SCRATCH
-        + [pltpu.SemaphoreType.DMA((4,))],
+        + [pltpu.SemaphoreType.DMA((4,)), pltpu.SemaphoreType.DMA((3,))],
         out_shape=[
             pltpu.HBM((MAX_ROWS, CHAN), f32),
             pltpu.HBM((1, CAP), jnp.int32),

time: 92.5 us -> 92.6 us (level)
  Pallas kernels: 34.7 us -> 29.5 us
  waiting for transfers between devices: 6.45 us -> 9.52 us
  blocking collectives: 35.6 us -> 37.7 us
    all_to_all x2, waiting for transfers between devices: 6.45 us -> 9.52 us  [exchange(): lax.all_to_all(rows, axis, split_axis=0, concat_axis=0, tiled=True)]
    pallas_call x1, Pallas kernels: 10.9 us -> 8.66 us  [network(): pl.pallas_call(network_kernel, in_specs=[anywhere, VMEM_SPEC, anywhere, a...]
    all_to_all x2, blocking collectives: 35.6 us -> 37.7 us  [exchange(): lax.all_to_all(rows, axis, split_axis=0, concat_axis=0, tiled=True)]
    pallas_call x1, Pallas kernels: 6.71 us -> 4.88 us  [row_sums(): pl.pallas_call(sums_kernel, in_specs=[pl.BlockSpec(memory_space=pltpu.SME...]
    pallas_call x1, Pallas kernels: 4.74 us -> 3.59 us  [row_seen(): pl.pallas_call(seen_kernel, in_specs=[pl.BlockSpec(memory_space=pltpu.SME...]
  transfers between devices with their start and end apart: 2 -> 2, of which waited for: 2 -> 2; matrix products, arithmetic and copies ran while one was open for 0% -> 0% of each run, Pallas kernels for 12% -> 9%
where the time goes in v7:
time: 92.6 us; the launch traced here: 92 us
  blocking collectives  37.7 us (41%)
  Pallas kernels  29.5 us (32%)
  starting transfers between devices  13.8 us (15%)
  waiting for transfers between devices  9.52 us (10%)
  between operations  1.36 us (1%)
    all_to_all x2, blocking collectives, exchange(): lax.all_to_all(rows, axis, split_axis=0, concat_axis=0, tiled=True)  37.7 us
    all_to_all x2, starting transfers between devices, exchange(): lax.all_to_all(rows, axis, split_axis=0, concat_axis=0, tiled=True)  13.8 us
    all_to_all x2, waiting for transfers between devices, exchange(): lax.all_to_all(rows, axis, split_axis=0, concat_axis=0, tiled=True)  9.52 us
    pallas_call x1, Pallas kernels, network(): pl.pallas_call(network_kernel, in_specs=[anywhere, VMEM_SPEC, anywhere, a...  8.66 us
    pallas_call x1, Pallas kernels, legendre_transform(): pl.pallas_call(legendre_kernel, in_specs=[pl.BlockSpec(memory_space=pl.AN...  7.76 us
    pallas_call x1, Pallas kernels, row_sums(): pl.pallas_call(sums_kernel, in_specs=[pl.BlockSpec(memory_space=pltpu.SME...  4.88 us
    pallas_call x1, Pallas kernels, row_seen(): pl.pallas_call(seen_kernel, in_specs=[pl.BlockSpec(memory_space=pltpu.SME...  3.59 us
    pallas_call x1, Pallas kernels, legendre_adjoint(): pl.pallas_call(adjoint_kernel, grid=(ML // ADJOINT_STEP,), in_specs=[VMEM...  2.43 us
  transfers between devices with their start and end apart: 2, of which 2 were waited for; matrix products, arithmetic and copies ran while one was open for 0% of the time, Pallas kernels for 9%

profile of v7, /device:TPU:1, one launch (start us, length us, event | category | flops | bytes accessed | tf_op | source)
XLA Modules:
  0.0 92.0 jit_solution(13530939492838403217)
XLA Ops:
  0.6 7.8 %legendre.1 = (bf16[32,256,256]{2,1,0:T(8,128)(2,1)}, bf16[384,512]{1,0:T(8,128)(2,1)}) custom-call(f32[512,256]{1,0:T(8,128)} %bitcast.23), custom_call_target="tpu_custom_call" | custom-call | tf_op jit(solution)/shard_map/legendre/pallas_call | solution.py:217
  8.4 5.8 %all-to-all-start = ((bf16[8,48,512]{2,1,0:T(8,128)(2,1)}), bf16[8,48,512]{2,1,0:T(8,128)(2,1)S(1)}, u32[]{:S(2)}, u32[]{:S(2)}) async-start(bf16[8,48,512]{2,1,0:T(8,128)(2,1)} %bitcast.2), calls=%async_computation | async-start | bytes 786432 | tf_op jit(solution)/shard_map/all_to_all | solution.py:780
  14.8 0.0 copy-start.1
  14.9 4.9 %row_sums.1 = (f32[2400,512]{1,0:T(8,128)}, s32[1,2048]{1,0:T(1,128)}, f32[16,256]{1,0:T(8,128)}, s32[16,128]{1,0:T(8,128)}) custom-call(s32[1]{0:T(128)S(6)} %copy.13.count_ref, s32[1,2048]{1,0:T(1,128)} %columns_ref.1, s32[1,2048]{1,0:T(1,128)} %pairs_ref.3, bf16[2048,512]{1,0:T(8,128)(2,1)} %bitcast.24, ...), custom_call_target="tpu_custom_call" | custom-call | flops 5033164800 | bytes 4915200 | tf_op jit(solution)/shard_map/row_sums/pallas_call | solution.py:500
  19.8 2.1 %all-to-all-done = bf16[8,48,512]{2,1,0:T(8,128)(2,1)S(1)} async-done(((bf16[8,48,512]{2,1,0:T(8,128)(2,1)}), bf16[8,48,512]{2,1,0:T(8,128)(2,1)S(1)}, u32[]{:S(2)}, u32[]{:S(2)}) %all-to-all-start) | async-done | bytes 393248 | tf_op jit(solution)/shard_map/all_to_all | solution.py:780
  21.9 0.0 copy-done.1
  21.9 1.5 %waves.1 = (bf16[768,384]{1,0:T(8,128)(2,1)}, f32[8,128]{1,0:T(8,128)}) custom-call(bf16[384,512]{1,0:T(8,128)(2,1)S(1)} %bitcast.18, bf16[768,512]{1,0:T(8,128)(2,1)S(1)} %copy-done.1, s32[16,128]{1,0:T(8,128)} %get-tuple-element.13.after_ref.first_ref.first_hbm), custom_call_target="tpu_custom_call" | custom-call | tf_op jit(solution)/shard_map/waves/pallas_call | solution.py:322
  23.4 8.0 %all-to-all-start.1 = ((bf16[16,48,384]{2,1,0:T(8,128)(2,1)}), bf16[16,48,384]{2,1,0:T(8,128)(2,1)S(1)}, u32[]{:S(2)}, u32[]{:S(2)}) async-start(bf16[16,48,384]{2,1,0:T(8,128)(2,1)} %bitcast.4), calls=%async_computation.1 | async-start | bytes 1179648 | tf_op jit(solution)/shard_map/all_to_all | solution.py:780
  31.5 0.0 copy-start.2
  31.5 0.0 copy-start.3
  31.5 3.6 %row_seen.1.seen_hbm = f32[2400,512]{1,0:T(8,128)} custom-call(s32[16,128]{1,0:T(8,128)} %get-tuple-element.13.after_ref.first_ref.first_hbm, s32[1,2048]{1,0:T(1,128)} %pairs_ref.3, s32[1,2048]{1,0:T(1,128)} %get-tuple-element.18.row_ref, f32[8,128]{1,0:T(8,128)} %get-tuple-element.19.after_ref), custom_call_target="tpu_custom_call" | custom-call | flops 5033164800 | bytes 4915200 | tf_op jit(solution)/shard_map/row_seen/pallas_call | solution.py:532
  35.1 7.4 %all-to-all-done.1 = bf16[16,48,384]{2,1,0:T(8,128)(2,1)S(1)} async-done(((bf16[16,48,384]{2,1,0:T(8,128)(2,1)}), bf16[16,48,384]{2,1,0:T(8,128)(2,1)S(1)}, u32[]{:S(2)}, u32[]{:S(2)}) %all-to-all-start.1) | async-done | bytes 589856 | tf_op jit(solution)/shard_map/all_to_all | solution.py:780
  42.5 0.0 copy-done.2
  42.5 0.0 copy-done.3
  42.5 0.0 copy-start
  42.5 8.7 %network.1 = (f32[2304,128]{1,0:T(8,128)}, bf16[768,384]{1,0:T(8,128)(2,1)S(1)}) custom-call(s32[16,128]{1,0:T(8,128)} %get-tuple-element.13.after_ref.first_ref.first_hbm, bf16[768,384]{1,0:T(8,128)(2,1)S(1)} %bitcast.15, bf16[2304,128]{1,0:T(8,128)(2,1)} %bitcast.21, f32[16,256]{1,0:T(8,128)} %get-tuple-element.16.rank_hbm, ...), custom_call_target="tpu_custom_call" | custom-call | tf_op jit(solution)/shard_map/network/pallas_call | solution.py:727
  51.2 19.8 %all_to_all.44 = bf16[16,48,384]{2,1,0:T(8,128)(2,1)S(1)} all-to-all(bf16[16,48,384]{2,1,0:T(8,128)(2,1)S(1)} %bitcast.19), channel_id=1, replica_groups=mesh['lat'=8,'lev'=16] {'lev'}, dimensions={0} | all-to-all | bytes 1179648 | tf_op jit(solution)/shard_map/all_to_all | solution.py:780
  71.0 0.7 waves_adjoint.1
  71.6 17.9 %all_to_all.45 = bf16[8,48,512]{2,1,0:T(8,128)(2,1)S(1)} all-to-all(bf16[8,48,512]{2,1,0:T(8,128)(2,1)S(1)} %bitcast.16), channel_id=1, replica_groups=mesh['lat'=8,'lev'=16] {'lat'}, dimensions={0} | all-to-all | bytes 786432 | tf_op jit(solution)/shard_map/all_to_all | solution.py:780
  89.6 0.0 copy-done
  89.6 2.4 %legendre_adjoint.1 = f32[512,256]{1,0:T(8,128)} custom-call(bf16[32,256,256]{2,1,0:T(8,128)(2,1)S(1)} %copy-done, bf16[384,512]{1,0:T(8,128)(2,1)S(1)} %bitcast.17), custom_call_target="tpu_custom_call" | custom-call | tf_op jit(solution)/shard_map/legendre_adjoint/pallas_call | solution.py:288
Async XLA Ops:
  8.4 13.5 %all-to-all-start = ((bf16[8,48,512]{2,1,0:T(8,128)(2,1)}), bf16[8,48,512]{2,1,0:T(8,128)(2,1)S(1)}, u32[]{:S(2)}, u32[]{:S(2)}) async-start(bf16[8,48,512]{2,1,0:T(8,128)(2,1)} %bitcast.2), calls=%async_computation | async-start | bytes 786432 | tf_op jit(solution)/shard_map/all_to_all | solution.py:780
  14.8 7.1 %copy-start.1 = (bf16[768,512]{1,0:T(8,128)(2,1)S(1)}, bf16[768,512]{1,0:T(8,128)(2,1)}, u32[]{:S(2)}) copy-start(bf16[768,512]{1,0:T(8,128)(2,1)} %constant.8.table_ref) | copy-start | bytes 2359300
  23.4 19.0 %all-to-all-start.1 = ((bf16[16,48,384]{2,1,0:T(8,128)(2,1)}), bf16[16,48,384]{2,1,0:T(8,128)(2,1)S(1)}, u32[]{:S(2)}, u32[]{:S(2)}) async-start(bf16[16,48,384]{2,1,0:T(8,128)(2,1)} %bitcast.4), calls=%async_computation.1 | async-start | bytes 1179648 | tf_op jit(solution)/shard_map/all_to_all | solution.py:780
  31.5 11.0 %copy-start.2 = (bf16[1024,1024]{1,0:T(8,128)(2,1)S(1)}, bf16[1024,1024]{1,0:T(8,128)(2,1)}, u32[]{:S(2)}) copy-start(bf16[1024,1024]{1,0:T(8,128)(2,1)} %w_mid.1) | copy-start | bytes 6291460
  31.5 11.0 %copy-start.3 = (f32[512]{0:T(512)S(1)}, f32[512]{0:T(512)}, u32[]{:S(2)}) copy-start(f32[512]{0:T(512)} %param.17) | copy-start | bytes 6148
  42.5 47.1 %copy-start = (bf16[32,256,256]{2,1,0:T(8,128)(2,1)S(1)}, bf16[32,256,256]{2,1,0:T(8,128)(2,1)}, u32[]{:S(2)}) copy-start(bf16[32,256,256]{2,1,0:T(8,128)(2,1)} %get-tuple-element.12.after_ref.p_ref) | copy-start | bytes 12582916
